TPU v7x, 256 devices: a whole 4x4x8 slice. The times are simulated.
256 devices in a mesh: pass: 32 (over x, y, core), kv: 8 (over z).
Axes of the slice: x: 4, y: 4, z: 8, core: 2. Of those that a mesh axis runs over, the one named last changes fastest.
Arguments:
- queries: bfloat16 [32, 64, 8192], P('pass', None, 'kv'), may hold values from -40 to 40
- suffix_keys: bfloat16 [32, 64, 1024], P('pass', None, 'kv'), may hold values from -5 to 5
- suffix_values: bfloat16 [32, 64, 1024], P('pass', None, 'kv'), may hold values from -40 to 40
- passage_keys: bfloat16 [128, 1024, 1024], P('pass', None, 'kv'), may hold values from -5 to 5
- passage_values: bfloat16 [128, 1024, 1024], P('pass', None, 'kv'), may hold values from -40 to 40
- fresh_keys: bfloat16 [32, 8, 128, 1024], P('pass', None, None, 'kv'), may hold values from -5 to 5
- fresh_values: bfloat16 [32, 8, 128, 1024], P('pass', None, None, 'kv'), may hold values from -40 to 40
- citations: int32 [32, 8], P('pass'), may hold values from 0 to 127, all different within a row; in each aligned block of 32 rows (0 to 31, 32 to 63, ...) at most 4 rows name the same one
- selected: int32 [32, 8, 128], P('pass'), may hold values from 0 to 1023, as said below
Outputs:
- attention: bfloat16 [32, 64, 8192], P('pass', 'kv')
Inputs may be any that keep to these rules, and one draw needn't show every extreme that they name: `citations`: each request cites 8 distinct passages; every passage is cited; no passage is cited by more than 4 requests, a bound that some block reaches. `selected`: each list holds 128 distinct positions of its passage.
All inputs are finite; a program needn't handle non-finite values.
Results may differ from a plain program's by a relative error of at most 0.0053.
Values may be sent and summed in bfloat16 or wider, within the bound.
No kernel may reach another device: no remote copies, remote signals or barrier semaphores. Data moves between devices by JAX's collectives and lax.ppermute only.
A program may use at most 128 MiB of HBM per device.

v0:
```python
import math

import jax
import jax.numpy as jnp
from jax import lax
from jax.sharding import PartitionSpec as P

HD = 128
PMOST = 4


very_low = -1e30


def body(
    queries,
    suffix_keys,
    suffix_values,
    passage_keys,
    passage_values,
    fresh_keys,
    fresh_values,
    citations,
    selected,
):
    my_place = lax.axis_index("pass")
    local_requests, suffix_len, row_width = queries.shape
    local_passages, length, kv_width = passage_keys.shape
    kv_heads = kv_width // HD
    group_size = row_width // kv_width
    head_count = kv_heads * group_size
    cite_count = citations.shape[1]
    pick_count = selected.shape[2]
    score_scale = 1.0 / math.sqrt(HD)
    all_cites, all_picks = (
        lax.all_gather(citations, "pass", axis=0, tiled=True),
        lax.all_gather(selected, "pass", axis=0, tiled=True),
    )
    all_queries = lax.all_gather(queries, "pass", axis=0, tiled=True)
    total_requests = all_cites.shape[0]
    own_query = queries.reshape(local_requests, suffix_len, kv_heads, group_size, HD)
    fresh_count = cite_count * pick_count
    fresh_key_rows = fresh_keys.reshape(local_requests, fresh_count, kv_heads, HD)
    fresh_value_rows = fresh_values.reshape(local_requests, fresh_count, kv_heads, HD)
    suffix_key_rows = suffix_keys.reshape(local_requests, suffix_len, kv_heads, HD)
    suffix_value_rows = suffix_values.reshape(local_requests, suffix_len, kv_heads, HD)
    fresh_scores = (
        jnp.einsum(
            "rskgd,rtkd->rskgt", own_query, fresh_key_rows, preferred_element_type=jnp.float32
        )
        * score_scale
    )
    suffix_scores = (
        jnp.einsum(
            "rskgd,rtkd->rskgt", own_query, suffix_key_rows, preferred_element_type=jnp.float32
        )
        * score_scale
    )
    causal = jnp.arange(suffix_len)[None, :] <= jnp.arange(suffix_len)[:, None]
    suffix_scores = jnp.where(causal[None, :, None, None, :], suffix_scores, very_low)
    host_max = jnp.maximum(jnp.max(fresh_scores, axis=-1), jnp.max(suffix_scores, axis=-1))
    fresh_weights = jnp.exp(fresh_scores - host_max[..., None])
    suffix_weights = jnp.exp(suffix_scores - host_max[..., None])
    host_sum = (jnp.sum(fresh_weights, axis=-1) + jnp.sum(suffix_weights, axis=-1)).reshape(
        local_requests, suffix_len, head_count
    )
    host_acc = jnp.einsum(
        "rskgt,rtkd->rskgd",
        fresh_weights.astype(jnp.bfloat16),
        fresh_value_rows,
        preferred_element_type=jnp.float32,
    )
    host_acc = host_acc + jnp.einsum(
        "rskgt,rtkd->rskgd",
        suffix_weights.astype(jnp.bfloat16),
        suffix_value_rows,
        preferred_element_type=jnp.float32,
    )
    host_acc = host_acc.reshape(local_requests, suffix_len, head_count, HD)
    host_max = host_max.reshape(local_requests, suffix_len, head_count)
    local_ids = my_place * local_passages + jnp.arange(local_passages, dtype=jnp.int32)
    hit_table = all_cites[None, :, :] == local_ids[:, None, None]
    cited_here = jnp.any(hit_table, axis=2)
    cite_slot = jnp.sum(
        jnp.where(hit_table, jnp.arange(cite_count, dtype=jnp.int32)[None, None, :], 0), axis=2
    )
    cite_rank = jnp.cumsum(cited_here.astype(jnp.int32), axis=1) - 1
    slot_ids = jnp.arange(PMOST, dtype=jnp.int32)
    slot_hit = cited_here[:, None, :] & (cite_rank[:, None, :] == slot_ids[None, :, None])
    request_ids = jnp.arange(total_requests, dtype=jnp.int32)
    slot_request = jnp.sum(jnp.where(slot_hit, request_ids[None, None, :], 0), axis=2).reshape(-1)
    slot_cite = jnp.sum(jnp.where(slot_hit, cite_slot[:, None, :], 0), axis=2).reshape(-1)
    slot_live = jnp.any(slot_hit, axis=2).reshape(-1)
    positions = jnp.arange(length, dtype=jnp.int32)

    def attend_slot(slot_index, loop_state):
        row_max, row_sum, row_acc = loop_state
        source = slot_index // PMOST
        request = slot_request[slot_index]
        active = slot_live[slot_index]
        query_block = lax.dynamic_index_in_dim(all_queries, request, 0, keepdims=False).reshape(
            suffix_len, kv_heads, group_size, HD
        )
        key_block = lax.dynamic_index_in_dim(passage_keys, source, 0, keepdims=False).reshape(
            length, kv_heads, HD
        )
        value_block = lax.dynamic_index_in_dim(passage_values, source, 0, keepdims=False).reshape(
            length, kv_heads, HD
        )
        pick_rows = lax.dynamic_index_in_dim(all_picks, request, 0, keepdims=False)
        pick_list = lax.dynamic_index_in_dim(pick_rows, slot_cite[slot_index], 0, keepdims=False)
        dropped = jnp.any(pick_list[:, None] == positions[None, :], axis=0)
        scores = (
            jnp.einsum("skgd,lkd->skgl", query_block, key_block, preferred_element_type=jnp.float32)
            * score_scale
        )
        scores = jnp.where(dropped, very_low, scores)
        slot_max = jnp.max(scores, axis=-1)
        weights = jnp.exp(scores - slot_max[..., None])
        slot_sum = jnp.where(active, jnp.sum(weights, axis=-1), 0.0).reshape(suffix_len, head_count)
        slot_acc = jnp.einsum(
            "skgl,lkd->skgd",
            weights.astype(jnp.bfloat16),
            value_block,
            preferred_element_type=jnp.float32,
        )
        slot_acc = jnp.where(active, slot_acc, 0.0).reshape(suffix_len, head_count, HD)
        slot_max = jnp.where(active, slot_max, very_low).reshape(suffix_len, head_count)
        old_max = lax.dynamic_index_in_dim(row_max, request, 0, keepdims=False)
        old_sum = lax.dynamic_index_in_dim(row_sum, request, 0, keepdims=False)
        old_acc = lax.dynamic_index_in_dim(row_acc, request, 0, keepdims=False).reshape(
            suffix_len, head_count, HD
        )
        new_max = jnp.maximum(old_max, slot_max)
        old_factor = jnp.exp(old_max - new_max)
        new_factor = jnp.exp(slot_max - new_max)
        new_sum = old_sum * old_factor + slot_sum * new_factor
        new_acc = (old_acc * old_factor[..., None] + slot_acc * new_factor[..., None]).reshape(
            suffix_len, row_width
        )
        row_max = lax.dynamic_update_index_in_dim(row_max, new_max, request, 0)
        row_sum = lax.dynamic_update_index_in_dim(row_sum, new_sum, request, 0)
        row_acc = lax.dynamic_update_index_in_dim(row_acc, new_acc, request, 0)
        return (row_max, row_sum, row_acc)

    def slot_step(slot_index, loop_state):
        return attend_slot(slot_index, loop_state)

    start_state = (
        jnp.full((total_requests, suffix_len, head_count), very_low, jnp.float32),
        jnp.zeros((total_requests, suffix_len, head_count), jnp.float32),
        jnp.zeros((total_requests, suffix_len, row_width), jnp.float32),
    )
    row_max, row_sum, row_acc = lax.fori_loop(0, local_passages * PMOST, slot_step, start_state)
    partial_value = (
        row_acc.reshape(total_requests, suffix_len, head_count, HD)
        / jnp.maximum(row_sum, 1.0)[..., None]
    ).astype(jnp.bfloat16)
    ceiling_all = lax.pmax(row_max.astype(jnp.bfloat16), "pass").astype(row_max.dtype)
    weight_share = row_sum * jnp.exp(row_max - ceiling_all)
    weighted = lax.optimization_barrier(partial_value).astype(jnp.float32) * weight_share[..., None]
    far_sum, far_weight = (
        lax.psum_scatter(
            weighted.reshape(total_requests, suffix_len, row_width),
            "pass",
            scatter_dimension=0,
            tiled=True,
        ),
        lax.psum_scatter(weight_share, "pass", scatter_dimension=0, tiled=True),
    )
    own_ceiling = lax.dynamic_slice_in_dim(
        ceiling_all, my_place * local_requests, local_requests, 0
    )
    ceiling = jnp.maximum(host_max, own_ceiling)
    near_scale = jnp.exp(host_max - ceiling)
    far_scale = jnp.exp(own_ceiling - ceiling)
    numerator = (
        host_acc * near_scale[..., None]
        + far_sum.reshape(local_requests, suffix_len, head_count, HD) * far_scale[..., None]
    )
    denominator = host_sum * near_scale + far_weight * far_scale
    attended = (
        (numerator / denominator[..., None])
        .reshape(local_requests, suffix_len, row_width)
        .astype(jnp.bfloat16)
    )
    return lax.all_to_all(attended, "kv", split_axis=1, concat_axis=2, tiled=True)


def solution(mesh):
    placed = (
        P("pass", None, "kv"),
        P("pass", None, "kv"),
        P("pass", None, "kv"),
        P("pass", None, "kv"),
        P("pass", None, "kv"),
        P("pass", None, None, "kv"),
        P("pass", None, None, "kv"),
        P("pass", None),
        P("pass", None, None),
    )
    return jax.shard_map(
        body, mesh=mesh, in_specs=placed, out_specs=P("pass", "kv", None), check_vma=False
    )
```

profile of v0, /device:TPU:24, one launch (start us, length us, event | category | flops | bytes accessed | tf_op | source)
XLA Modules:
  0.0 771.7 jit_solution(18331333335364585933)
XLA Ops:
  7.3 20.5 %all-gather = s32[32,1,8]{2,1,0:T(1,128)S(1)} all-gather(s32[1,1,8]{2,1,0:T(1,128)} %bitcast.232), channel_id=1, replica_groups=mesh['pass'=32,'kv'=8] {'pass'}, dimensions={0}, use_global_device_ids=true | all-gather | bytes 1056 | tf_op jit(solution)/shard_map/all_gather | solution.py:36
  28.9 23.0 %all_gather.10 = s32[32,8,128]{2,1,0:T(8,128)S(1)} all-gather(s32[1,8,128]{2,1,0:T(8,128)} %param.19), channel_id=1, replica_groups=mesh['pass'=32,'kv'=8] {'pass'}, dimensions={0}, use_global_device_ids=true | all-gather | bytes 135168 | tf_op jit(solution)/shard_map/all_gather | solution.py:37
  51.9 11.5 %all-gather.3.cloned.1.call-done = bf16[32,64,1024]{2,1,0:T(8,128)(2,1)} async-done(((bf16[1,64,1024]{2,1,0:T(8,128)(2,1)}), bf16[32,64,1024]{2,1,0:T(8,128)(2,1)}) %all-gather.3.cloned.1.call-update) | async-done | bytes 4194320 | tf_op jit(solution)/shard_map/all_gather | solution.py:39
  67.7 334.7 %while.21 = (s32[]{:T(128)}, f32[32,64,8]{1,2,0:T(8,128)S(1)}, f32[32,64,8]{1,2,0:T(8,128)S(1)}, f32[32,64,1024]{2,0,1:T(8,128)}, s32[16]{0:T(128)S(1)}, /*index...) while((s32[]{:T(128)}, f32[32,64,8]{1,2,0:T(8,128)S(1)}, ...), condition=%wide.region_12.13_spmd.clone, body=%wide.region_8.12_spmd.clone.sunk | while | flops 274731008 | bytes 10676701 | solution.py:154
  82.6 6.1 dynamic_update_slice.43
  124.4 6.1 dynamic_update_slice.43
  145.3 6.1 dynamic_update_slice.43
  187.1 6.1 dynamic_update_slice.43
  208.1 6.1 dynamic_update_slice.43
  229.0 6.1 dynamic_update_slice.43
  249.9 6.1 dynamic_update_slice.43
  270.9 6.1 dynamic_update_slice.43
  291.8 6.1 dynamic_update_slice.43
  312.7 6.1 dynamic_update_slice.43
  333.6 6.1 dynamic_update_slice.43
  354.5 6.1 dynamic_update_slice.43
  375.4 6.1 dynamic_update_slice.43
  396.4 6.1 dynamic_update_slice.43
  402.5 112.0 %pmax.7 = bf16[32,64,8]{1,2,0:T(8,128)(2,1)S(1)} all-reduce(bf16[32,64,8]{1,2,0:T(8,128)(2,1)S(1)} %convert_element_type.44), channel_id=1, replica_groups=mesh['pass'=32,'kv'=8] {'pass'}, use_global_device_ids=true, to_apply=%region_13.14 | all-reduce | flops 16384 | bytes 65536 | tf_op jit(solution)/shard_map/pmax | solution.py:159
  515.8 8.7 %copy.100 = f32[256,8,8,128]{3,2,1,0:T(8,128)} copy(f32[256,8,8,128]{3,1,2,0:T(8,128)} %bitcast.216) | data formatting | bytes 16777216
  535.5 9.3 %reshape.426 = f32[32,64,1024]{2,1,0:T(8,128)} reshape(f32[32,64,8,128]{3,2,1,0:T(8,128)} %convert_multiply_fusion) | data formatting | bytes 16777216 | tf_op jit(solution)/shard_map/reshape | solution.py:164
  548.8 91.4 %all-reduce.3.cloned.1.call-done = f32[32,64,8]{1,2,0:T(8,128)} async-done(((f32[32,64,8]{1,2,0:T(8,128)}), f32[32,64,8]{1,2,0:T(8,128)}) %all-reduce.3.cloned.1.call-update) | async-done | bytes 65552
  641.7 102.8 %reduce-scatter.2.cloned.1.call-done = f32[1,64,1024]{2,1,0:T(8,128)} async-done(((f32[32,64,1024]{2,1,0:T(8,128)}), f32[1,64,1024]{2,1,0:T(8,128)}) %reduce-scatter.2.cloned.1.call-update) | async-done | bytes 262160 | tf_op jit(solution)/shard_map/reduce_scatter | solution.py:163
  748.4 15.9 %all_to_all.18 = bf16[8,2,4096]{2,1,0:T(2,128)(2,1)S(1)} all-to-all(bf16[8,2,4096]{2,1,0:T(2,128)(2,1)S(1)} %reshape.441), channel_id=1, replica_groups=mesh['pass'=32,'kv'=8] {'kv'}, dimensions={0} | all-to-all | bytes 262144 | tf_op jit(solution)/shard_map/all_to_all | solution.py:187
  (356 shorter events, 218.4 us)
Async XLA Ops:
  6.5 540.1 %copy-start = (bf16[1,8,128,128]{3,2,1,0:T(8,128)(2,1)S(1)}, bf16[1,8,128,128]{3,2,1,0:T(8,128)(2,1)}, u32[]{:S(2)}) copy-start(bf16[1,8,128,128]{3,2,1,0:T(8,128)(2,1)} %param.16) | copy-start | bytes 786436
  6.5 56.9 %all-gather.3.cloned.1.call-start = ((), (), s32[]{:S(2)}) async-start(), calls=%async_computation.2 | async-start | bytes 4325376 | tf_op jit(solution)/shard_map/all_gather | solution.py:39
  514.5 0.7 copy-start.1
  514.8 125.4 %all-reduce.3.cloned.1.call-start = ((), (), s32[]{:S(2)}) async-start(), calls=%async_computation.4 | async-start | bytes 262144
  515.6 228.9 %reduce-scatter.2.cloned.1.call-start = ((), (), s32[]{:S(2)}) async-start(), calls=%async_computation.3 | async-start | bytes 8650752 | tf_op jit(solution)/shard_map/reduce_scatter | solution.py:163
  544.8 0.9 copy-start.2
  544.8 0.9 copy-start.6
  544.8 1.6 copy-start.4
  544.8 2.4 copy-start.3
  546.6 1.1 copy-start.5
Sparse Core Ops, SparseCore 0:
  9.9 53.4 all-gather.2
  518.9 121.2 all-reduce.2
  644.7 99.6 reduce-scatter.1
where the time goes:
time: 778 us; the launch traced here: 772 us
  waiting for transfers between devices  207 us (27%)
  local copies, waits for them, and re-layouts  178 us (23%)
  blocking collectives  171 us (22%)
  other arithmetic  82 us (11%)
  loops' own time  59.8 us (8%)
  matrix products  59.6 us (8%)
  between operations  13.4 us (2%)
    pmax x1, blocking collectives, body(): lax.pmax(row_max.astype(jnp.bfloat16), 'pass').astype(row_max.dtype)  112 us
    reduce_scatter x1, waiting for transfers between devices, body(): lax.psum_scatter(weighted.reshape(total_requests, suffix_len, row_width),...  103 us
    dynamic_update_slice x16, local copies, waits for them, and re-layouts, attend_slot(): row_acc = lax.dynamic_update_index_in_dim(row_acc, new_acc, request, 0)  97.2 us
    unnamed x4, waiting for transfers between devices  92.5 us
    another operation x1, loops' own time, body(): lax.fori_loop(0, local_passages * PMOST, slot_step, start_state)  59.8 us
    add x16, other arithmetic, attend_slot(): old_acc * old_factor[..., None] + slot_acc * new_factor[..., None]  34.6 us
    dot_general x16, matrix products, attend_slot(): jnp.einsum('skgl,lkd->skgd', weights.astype(jnp.bfloat16), value_block, p...  34.5 us
    dot_general x16, matrix products, attend_slot(): jnp.einsum('skgd,lkd->skgl', query_block, key_block, preferred_element_ty...  23.6 us
  transfers between devices with their start and end apart: 3, of which 3 were waited for; matrix products, arithmetic and copies ran while one was open for 4% of the time, Pallas kernels for 0%

commit v1 on v0

v1 whole, which is shorter than its diff:
```python
import functools
import math

import jax
import jax.numpy as jnp
from jax import lax
from jax.experimental import pallas as pl
from jax.experimental.pallas import tpu as pltpu
from jax.sharding import Mesh
from jax.sharding import PartitionSpec as P

HD = 128
LANES = 128
PARTS = 3
RING = 4
HOPS = (0, 1, 3, 2)
very_low = -1e30
log2_scale = math.log2(math.e) / math.sqrt(HD)
VMEM_BYTES = 48 * 1024 * 1024


def contract_last(left, right):
    return lax.dot_general(
        left, right, (((1,), (1,)), ((), ())), preferred_element_type=jnp.float32
    )


def stack_heads(rows, heads):
    return jnp.concatenate([rows[:, g * HD : (g + 1) * HD] for g in range(heads)], axis=0)


def attend_kernel(
    table_ref, packed_ref, key_ref, value_ref, out_ref, mask_s, query_s, max_s, acc_s, *, suffix_len, heads, cites
):
    rows = suffix_len * heads
    chunk = rows // 2
    requests = packed_ref.shape[0]
    mask_s[...] = packed_ref[:, suffix_len : suffix_len + cites, :].astype(jnp.float32)

    def one_request(j, carry):
        query_s[...] = stack_heads(packed_ref[j, 0:suffix_len, :], heads)
        max_s[...] = jnp.full_like(max_s, very_low)
        acc_s[...] = jnp.zeros_like(acc_s)

        def one_cite(c, inner):
            place = table_ref[j, c]

            @pl.when(place >= 0)
            def _():
                bias = mask_s[j, pl.ds(c, 1), :]
                for start in range(0, rows, chunk):
                    part = pl.ds(start, chunk)
                    scores = contract_last(query_s[part, :], key_ref[place]) * log2_scale + bias
                    old_max = max_s[part, :]
                    new_max = jnp.maximum(old_max, jnp.max(scores, axis=1, keepdims=True))
                    weights = jnp.exp2(scores - new_max[:, 0:1]).astype(jnp.bfloat16)
                    factor = jnp.exp2(old_max - new_max)
                    added = jnp.dot(weights, value_ref[place], preferred_element_type=jnp.float32)
                    acc_s[part, :] = acc_s[part, :] * jnp.concatenate([factor, factor], axis=1) + added
                    max_s[part, :] = new_max

            return inner

        lax.fori_loop(0, cites, one_cite, 0)
        lane = lax.broadcasted_iota(jnp.int32, (suffix_len, LANES), 1)
        stats = jnp.zeros((suffix_len, LANES), jnp.float32)
        for g in range(heads):
            part = slice(g * suffix_len, (g + 1) * suffix_len)
            total = acc_s[part, HD : 2 * HD]
            live = total > 0.0
            safe = jnp.where(live, total, 1.0)
            out_ref[j, :, g * HD : (g + 1) * HD] = (acc_s[part, 0:HD] / safe).astype(jnp.bfloat16)
            level = jnp.where(live, max_s[part, :] + jnp.log2(safe), very_low)
            stats = put_level(stats, level, lane, g, heads)
        out_ref[j, :, heads * HD :] = stats.astype(jnp.bfloat16)
        return carry

    lax.fori_loop(0, requests, one_request, 0)


def put_level(stats, level, lane, g, heads):
    for i in range(PARTS):
        piece = level.astype(jnp.bfloat16).astype(jnp.float32)
        stats = jnp.where(lane == i * heads + g, piece, stats)
        level = level - piece
    return stats


def get_level(tile, heads):
    level = tile.astype(jnp.float32)
    total = level
    for i in range(1, PARTS):
        total = total + pltpu.roll(level, LANES - i * heads, 1)
    return total


def host_kernel(query_ref, fresh_key_ref, fresh_value_ref, suffix_key_ref, suffix_value_ref, out_ref, level_ref):
    suffix_len, width = query_ref.shape
    heads = width // HD
    query = stack_heads(query_ref[...], heads)
    fresh = contract_last(query, fresh_key_ref[...]) * log2_scale
    near = contract_last(query, suffix_key_ref[...]) * log2_scale
    place = lax.broadcasted_iota(jnp.int32, near.shape, 0) % suffix_len
    near = jnp.where(lax.broadcasted_iota(jnp.int32, near.shape, 1) <= place, near, very_low)
    top = jnp.maximum(jnp.max(fresh, axis=1, keepdims=True), jnp.max(near, axis=1, keepdims=True))
    fresh = jnp.exp2(fresh - top)
    near = jnp.exp2(near - top)
    total = jnp.sum(fresh, axis=1, keepdims=True) + jnp.sum(near, axis=1, keepdims=True)
    acc = jnp.dot(fresh.astype(jnp.bfloat16), fresh_value_ref[...], preferred_element_type=jnp.float32)
    acc = acc + jnp.dot(near.astype(jnp.bfloat16), suffix_value_ref[...], preferred_element_type=jnp.float32)
    acc = acc / total
    level = jnp.broadcast_to(top + jnp.log2(total), acc.shape)
    lane = lax.broadcasted_iota(jnp.int32, (suffix_len, LANES), 1)
    levels = jnp.zeros((suffix_len, LANES), jnp.float32)
    for g in range(heads):
        part = slice(g * suffix_len, (g + 1) * suffix_len)
        out_ref[:, g * HD : (g + 1) * HD] = acc[part]
        levels = jnp.where(lane == g, level[part], levels)
    level_ref[...] = levels


def weigh(levels):
    top = functools.reduce(jnp.maximum, levels)
    shares = [jnp.exp2(level - top) for level in levels]
    total = functools.reduce(jnp.add, shares)
    return [share / total for share in shares], top + jnp.log2(total)


def merge_kernel(*refs):
    sources, out_ref = refs[:-1], refs[-1]
    requests, suffix_len, wide = out_ref.shape
    heads = (wide - LANES) // HD
    lane = lax.broadcasted_iota(jnp.int32, (suffix_len, LANES), 1)
    for j in range(requests):
        shares, level = weigh([get_level(s[j, :, heads * HD :], heads) for s in sources])
        for g in range(heads):
            part = slice(g * HD, (g + 1) * HD)
            terms = [s[j, :, part].astype(jnp.float32) * w[:, g : g + 1] for s, w in zip(sources, shares)]
            out_ref[j, :, part] = functools.reduce(jnp.add, terms).astype(jnp.bfloat16)
        stats = jnp.zeros((suffix_len, LANES), jnp.float32)
        for i in range(PARTS):
            piece = level.astype(jnp.bfloat16).astype(jnp.float32)
            moved = piece if i == 0 else pltpu.roll(piece, i * heads, 1)
            stats = jnp.where((lane >= i * heads) & (lane < (i + 1) * heads), moved, stats)
            level = level - piece
        out_ref[j, :, heads * HD :] = stats.astype(jnp.bfloat16)


def final_kernel(*refs):
    sources, host_ref, level_ref, out_ref = refs[:-3], refs[-3], refs[-2], refs[-1]
    suffix_len, width = out_ref.shape
    heads = width // HD
    levels = [get_level(s[:, width:], heads) for s in sources] + [level_ref[...]]
    shares, _ = weigh(levels)
    for g in range(heads):
        part = slice(g * HD, (g + 1) * HD)
        terms = [s[:, part].astype(jnp.float32) * w[:, g : g + 1] for s, w in zip(sources, shares)]
        terms.append(host_ref[:, part] * shares[-1][:, g : g + 1])
        out_ref[:, part] = functools.reduce(jnp.add, terms).astype(jnp.bfloat16)


def in_vmem(kernel, out_shape, operands, scratch=(), smem=0, name=None):
    spaces = [pltpu.SMEM] * smem + [pltpu.VMEM] * (len(operands) - smem)
    many = isinstance(out_shape, tuple)
    return pl.pallas_call(
        kernel,
        out_shape=out_shape,
        in_specs=[pl.BlockSpec(memory_space=s) for s in spaces],
        out_specs=tuple(pl.BlockSpec(memory_space=pltpu.VMEM) for _ in out_shape)
        if many
        else pl.BlockSpec(memory_space=pltpu.VMEM),
        scratch_shapes=list(scratch),
        compiler_params=pltpu.CompilerParams(vmem_limit_bytes=VMEM_BYTES),
        name=name,
    )(*operands)


def shift(value, axis, hop):
    return lax.ppermute(value, axis, [(i, (i + hop) % RING) for i in range(RING)])


def body(
    queries,
    suffix_keys,
    suffix_values,
    passage_keys,
    passage_values,
    fresh_keys,
    fresh_values,
    citations,
    selected,
):
    _, suffix_len, width = queries.shape
    local_passages, length, _ = passage_keys.shape
    heads = width // HD
    cites = citations.shape[1]
    chip = lax.axis_index("x") * RING + lax.axis_index("y")
    core = lax.axis_index("c")

    positions = jnp.arange(length, dtype=jnp.int32)
    dropped = jnp.any(selected[0][:, :, None] == positions[None, None, :], axis=1)
    masks = jnp.where(dropped, very_low, 0.0).astype(jnp.bfloat16)
    ids = jnp.pad(citations.astype(jnp.bfloat16), ((0, 7), (0, width - cites)))
    packed = jnp.concatenate([queries[0], masks, ids], axis=0)

    swap = [(0, 1), (1, 0)]
    keys = jnp.concatenate([passage_keys, lax.ppermute(passage_keys, "c", swap)], axis=0)
    values = jnp.concatenate([passage_values, lax.ppermute(passage_values, "c", swap)], axis=0)
    values = jnp.concatenate([values, jnp.ones_like(values)], axis=2)

    row = jnp.stack([packed] + [shift(packed, "x", hop) for hop in HOPS[1:]])
    classes = [row] + [shift(row, "y", hop) for hop in HOPS[1:]]

    host_out, host_level = in_vmem(
        host_kernel,
        (
            jax.ShapeDtypeStruct((suffix_len, width), jnp.float32),
            jax.ShapeDtypeStruct((suffix_len, LANES), jnp.float32),
        ),
        (
            queries[0],
            fresh_keys.reshape(-1, HD),
            fresh_values.reshape(-1, HD),
            suffix_keys[0],
            suffix_values[0],
        ),
        name="host_part",
    )

    rows = suffix_len * heads
    results = []
    for block in classes:
        named = block[:, suffix_len + cites, 0:cites].astype(jnp.int32)
        local = named - chip * (2 * local_passages)
        here = (local >= 0) & (local < 2 * local_passages)
        table = jnp.where(here, (local + core * local_passages) % (2 * local_passages), -1)
        results.append(
            in_vmem(
                functools.partial(attend_kernel, suffix_len=suffix_len, heads=heads, cites=cites),
                jax.ShapeDtypeStruct((RING, suffix_len, width + LANES), jnp.bfloat16),
                (table, block, keys, values),
                scratch=(
                    pltpu.VMEM((RING, cites, length), jnp.float32),
                    pltpu.VMEM((rows, HD), jnp.bfloat16),
                    pltpu.VMEM((rows, LANES), jnp.float32),
                    pltpu.VMEM((rows, 2 * HD), jnp.float32),
                ),
                smem=1,
                name="attend_class",
            )
        )
    back = [results[0]] + [shift(r, "y", RING - hop) for r, hop in zip(results[1:], HOPS[1:])]
    merged = in_vmem(
        merge_kernel,
        jax.ShapeDtypeStruct((RING, suffix_len, width + LANES), jnp.bfloat16),
        tuple(back),
        name="merge_row",
    )
    home = [merged[0]] + [shift(merged[j], "x", RING - HOPS[j]) for j in range(1, RING)]
    attended = in_vmem(
        final_kernel,
        jax.ShapeDtypeStruct((suffix_len, width), jnp.bfloat16),
        tuple(home) + (host_out, host_level),
        name="merge_home",
    )
    groups = lax.psum(1, "kv")
    pieces = attended.reshape(groups, suffix_len // groups, width)
    pieces = lax.all_to_all(pieces, "kv", split_axis=0, concat_axis=0, tiled=True)
    return jnp.transpose(pieces, (1, 0, 2)).reshape(1, suffix_len // groups, groups * width)


def solution(mesh):
    fine = Mesh(mesh.devices.reshape(RING, RING, 2, -1), ("x", "y", "c", "kv"))
    part = ("x", "y", "c")
    placed = (
        P(part, None, "kv"),
        P(part, None, "kv"),
        P(part, None, "kv"),
        P(part, None, "kv"),
        P(part, None, "kv"),
        P(part, None, None, "kv"),
        P(part, None, None, "kv"),
        P(part, None),
        P(part, None, None),
    )
    return jax.shard_map(body, mesh=fine, in_specs=placed, out_specs=P(part, "kv", None), check_vma=False)
```

time: 778 us -> 122 us (0.16)
  local copies, waits for them, and re-layouts: 178 us -> 2.16 us
  waiting for transfers between devices: 207 us -> 48.2 us
  blocking collectives: 171 us -> 17.3 us
  other arithmetic: 82 us -> 6.86 us
  loops' own time: 59.8 us -> 0 us
  matrix products: 59.6 us -> 0 us
  Pallas kernels: 0 us -> 27.9 us
  starting transfers between devices: 0.26 us -> 18.7 us
  between operations: 13.4 us -> 0.28 us
    pmax x1 -> x0, blocking collectives: 112 us -> none  [body(): lax.pmax(row_max.astype(jnp.bfloat16), 'pass').astype(row_max.dtype)]
    reduce_scatter x1 -> x0, waiting for transfers between devices: 103 us -> none  [body(): lax.psum_scatter(weighted.reshape(total_requests, suffix_len, row_width),...]
    dynamic_update_slice x16 -> x0, local copies, waits for them, and re-layouts: 97.2 us -> none  [attend_slot(): row_acc = lax.dynamic_update_index_in_dim(row_acc, new_acc, request, 0)]
    unnamed x4 -> x0, waiting for transfers between devices: 92.5 us -> none
    another operation x1 -> x0, loops' own time: 59.8 us -> none  [body(): lax.fori_loop(0, local_passages * PMOST, slot_step, start_state)]
    dot_general x36 -> x0, matrix products: 59.6 us -> none  [the longest x16 34.5 us: attend_slot(): jnp.einsum('skgl,lkd->skgd', weights.astype(jnp.bfloat16), value_block, p...]
    ppermute x0 -> x14, waiting for transfers between devices: none -> 48.2 us  [the longest x12 48.2 us: shift(): lax.ppermute(value, axis, [(i, (i + hop) % RING) for i in range(RING)])]
    all_gather x2 -> x0, blocking collectives: 43.5 us -> none  [the longest x1 23 us: body(): lax.all_gather(selected, 'pass', axis=0, tiled=True)]
  transfers between devices with their start and end apart: 3 -> 14, of which waited for: 3 -> 9; matrix products, arithmetic and copies ran while one was open for 4% -> 4% of each run, Pallas kernels for 0% -> 15%
where the time goes in v1:
time: 122 us; the launch traced here: 121 us
  waiting for transfers between devices  48.2 us (40%)
  Pallas kernels  27.9 us (23%)
  starting transfers between devices  18.7 us (15%)
  blocking collectives  17.3 us (14%)
  other arithmetic  6.86 us (6%)
  local copies, waits for them, and re-layouts  2.16 us (2%)
    ppermute x12, waiting for transfers between devices, shift(): lax.ppermute(value, axis, [(i, (i + hop) % RING) for i in range(RING)])  48.2 us
    pallas_call x7, Pallas kernels, in_vmem(): pl.pallas_call(kernel, out_shape=out_shape, in_specs=[pl.BlockSpec(memory...  27.9 us
    ppermute x12, starting transfers between devices, shift(): lax.ppermute(value, axis, [(i, (i + hop) % RING) for i in range(RING)])  18.2 us
    all_to_all x1, blocking collectives, body(): lax.all_to_all(pieces, 'kv', split_axis=0, concat_axis=0, tiled=True)  17.3 us
    concatenate x1, other arithmetic, body(): jnp.concatenate([passage_values, lax.ppermute(passage_values, 'c', swap)]...  3.37 us
  transfers between devices with their start and end apart: 14, of which 9 were waited for; matrix products, arithmetic and copies ran while one was open for 4% of the time, Pallas kernels for 15%

profile of v1, /device:TPU:24, one launch (start us, length us, event | category | flops | bytes accessed | tf_op | source)
XLA Modules:
  0.0 121.4 jit_solution(13778891167852586780)
XLA Ops:
  0.0 1.7 %fusion.3 = pred[8,1024]{1,0:T(8,128)(4,1)S(1)} fusion(s32[8,128]{1,0:T(8,128)} %bitcast.50), kind=kLoop, calls=%fused_computation.5 | loop fusion | flops 2088960 | bytes 12288 | tf_op jit(solution)/shard_map/reduce_or | solution.py:201
  3.3 1.6 %collective-permute-start = (bf16[80,1024]{1,0:T(8,128)(2,1)S(1)}, bf16[80,1024]{1,0:T(8,128)(2,1)S(1)}, u32[]{:S(2)}, u32[]{:S(2)}) collective-permute-start(bf16[80,1024]{1,0:T(8,128)(2,1)S(1)} %get-tuple-element.14), channel_id=1, source_target_pairs={{0,64},{64,128},{128,192},{192,0},{1,65},{65,129},{129,193},{193,1... | collective-permute-start | bytes 491528 | tf_op jit(solution)/shard_map/ppermute | solution.py:179
  4.9 1.7 %collective-permute-start.1 = (bf16[80,1024]{1,0:T(8,128)(2,1)S(1)}, bf16[80,1024]{1,0:T(8,128)(2,1)S(1)}, u32[]{:S(2)}, u32[]{:S(2)}) collective-permute-start(bf16[80,1024]{1,0:T(8,128)(2,1)S(1)} %get-tuple-element.14), channel_id=1, source_target_pairs={{0,192},{64,0},{128,64},{192,128},{1,193},{65,1},{129,65},{193,129... | collective-permute-start | bytes 491528 | tf_op jit(solution)/shard_map/ppermute | solution.py:179
  6.6 1.8 %collective-permute-start.2 = (bf16[80,1024]{1,0:T(8,128)(2,1)S(1)}, bf16[80,1024]{1,0:T(8,128)(2,1)S(1)}, u32[]{:S(2)}, u32[]{:S(2)}) collective-permute-start(bf16[80,1024]{1,0:T(8,128)(2,1)S(1)} %get-tuple-element.14), channel_id=1, source_target_pairs={{0,128},{64,192},{128,0},{192,64},{1,129},{65,193},{129,1},{193,65... | collective-permute-start | bytes 491528 | tf_op jit(solution)/shard_map/ppermute | solution.py:179
  8.4 2.3 %collective-permute-done = bf16[80,1024]{1,0:T(8,128)(2,1)S(1)} collective-permute-done((bf16[80,1024]{1,0:T(8,128)(2,1)S(1)}, bf16[80,1024]{1,0:T(8,128)(2,1)S(1)}, u32[]{:S(2)}, u32[]{:S(2)}) %collective-permute-start) | collective-permute-done | bytes 163872 | tf_op jit(solution)/shard_map/ppermute | solution.py:179
  10.7 2.6 %collective-permute-done.1 = bf16[80,1024]{1,0:T(8,128)(2,1)S(1)} collective-permute-done((bf16[80,1024]{1,0:T(8,128)(2,1)S(1)}, bf16[80,1024]{1,0:T(8,128)(2,1)S(1)}, u32[]{:S(2)}, u32[]{:S(2)}) %collective-permute-start.1) | collective-permute-done | bytes 163872 | tf_op jit(solution)/shard_map/ppermute | solution.py:179
  13.3 1.7 %collective-permute-done.2 = bf16[80,1024]{1,0:T(8,128)(2,1)S(1)} collective-permute-done((bf16[80,1024]{1,0:T(8,128)(2,1)S(1)}, bf16[80,1024]{1,0:T(8,128)(2,1)S(1)}, u32[]{:S(2)}, u32[]{:S(2)}) %collective-permute-start.2) | collective-permute-done | bytes 163872 | tf_op jit(solution)/shard_map/ppermute | solution.py:179
  18.2 3.3 %collective-permute-start.5 = (bf16[4,80,1024]{2,1,0:T(8,128)(2,1)S(1)}, bf16[4,80,1024]{2,1,0:T(8,128)(2,1)S(1)}, u32[]{:S(2)}, u32[]{:S(2)}) collective-permute-start(bf16[4,80,1024]{2,1,0:T(8,128)(2,1)S(1)} %pad_maximum_fusion.packed_ref), channel_id=1, source_target_pairs={{0,16},{16,32},{32,48},{48,0},{1,17},{17,33},{33,49},{49,1},{2,18}... | collective-permute-start | bytes 1966088 | tf_op jit(solution)/shard_map/ppermute | solution.py:179
  21.5 12.9 %collective-permute-done.9.packed_ref = bf16[4,80,1024]{2,1,0:T(8,128)(2,1)S(1)} collective-permute-done((bf16[4,80,1024]{2,1,0:T(8,128)(2,1)S(1)}, bf16[4,80,1024]{2,1,0:T(8,128)(2,1)S(1)}, u32[]{:S(2)}, u32[]{:S(2)}) %collective-permute-start.9) | collective-permute-done | bytes 655392 | tf_op jit(solution)/shard_map/ppermute | solution.py:179
  34.4 11.9 %collective-permute-done.7.packed_ref = bf16[4,80,1024]{2,1,0:T(8,128)(2,1)S(1)} collective-permute-done((bf16[4,80,1024]{2,1,0:T(8,128)(2,1)S(1)}, bf16[4,80,1024]{2,1,0:T(8,128)(2,1)S(1)}, u32[]{:S(2)}, u32[]{:S(2)}) %collective-permute-start.7) | collective-permute-done | bytes 655392 | tf_op jit(solution)/shard_map/ppermute | solution.py:179
  46.5 3.4 %fusion.2.value_ref = bf16[8,1024,256]{2,1,0:T(8,128)(2,1)} fusion(bf16[4,1024,128]{2,1,0:T(8,128)(2,1)} %collective-permute-done.4, bf16[4,1024,128]{2,1,0:T(8,128)(2,1)} %param.13), kind=kLoop, calls=%fused_computation.3 | loop fusion | flops 14680064 | bytes 6291456 | tf_op jit(solution)/shard_map/concatenate | solution.py:208
  50.0 6.2 %attend_class.7 = bf16[4,64,1152]{2,1,0:T(8,128)(2,1)S(1)} custom-call(s32[4,8]{1,0:T(4,128)S(1)} %fusion.13.table_ref, bf16[4,80,1024]{2,1,0:T(8,128)(2,1)S(1)} %collective-permute-done.9.packed_ref, bf16[8,1024,128]{2,1,0:T(8,128)(2,1)S(1)} %constant_dynamic-update-slice_fusion.key_ref, bf16[8,1024,256]{2,1,0:T(8,128)(2,1)} %fusion.2.value_ref), custom_call_target="tpu_custom_call" | custom-call | tf_op jit(solution)/shard_map/attend_class/pallas_call | solution.py:165
  56.3 4.9 %attend_class.6 = bf16[4,64,1152]{2,1,0:T(8,128)(2,1)S(1)} custom-call(s32[4,8]{1,0:T(4,128)S(1)} %fusion.11.table_ref, bf16[4,80,1024]{2,1,0:T(8,128)(2,1)S(1)} %collective-permute-done.7.packed_ref, bf16[8,1024,128]{2,1,0:T(8,128)(2,1)S(1)} %constant_dynamic-update-slice_fusion.key_ref, bf16[8,1024,256]{2,1,0:T(8,128)(2,1)} %fusion.2.value_ref), custom_call_target="tpu_custom_call" | custom-call | tf_op jit(solution)/shard_map/attend_class/pallas_call | solution.py:165
  61.2 6.1 %collective-permute-start.8 = (bf16[4,64,1152]{2,1,0:T(8,128)(2,1)S(1)}, bf16[4,64,1152]{2,1,0:T(8,128)(2,1)S(1)}, u32[]{:S(2)}, u32[]{:S(2)}) collective-permute-start(bf16[4,64,1152]{2,1,0:T(8,128)(2,1)S(1)} %attend_class.6), channel_id=1, source_target_pairs={{0,16},{16,32},{32,48},{48,0},{1,17},{17,33},{33,49},{49,1},{2,18}... | collective-permute-start | bytes 1769480 | tf_op jit(solution)/shard_map/ppermute | solution.py:179
  67.4 7.5 %attend_class.5 = bf16[4,64,1152]{2,1,0:T(8,128)(2,1)S(1)} custom-call(s32[4,8]{1,0:T(4,128)S(1)} %fusion.9.table_ref, bf16[4,80,1024]{2,1,0:T(8,128)(2,1)S(1)} %collective-permute-done.5.packed_ref, bf16[8,1024,128]{2,1,0:T(8,128)(2,1)S(1)} %constant_dynamic-update-slice_fusion.key_ref, bf16[8,1024,256]{2,1,0:T(8,128)(2,1)} %fusion.2.value_ref), custom_call_target="tpu_custom_call" | custom-call | tf_op jit(solution)/shard_map/attend_class/pallas_call | solution.py:165
  75.1 5.0 %attend_class.4.refs_0_ = bf16[4,64,1152]{2,1,0:T(8,128)(2,1)S(1)} custom-call(s32[4,8]{1,0:T(4,128)S(1)} %fusion.7.table_ref, bf16[4,80,1024]{2,1,0:T(8,128)(2,1)S(1)} %pad_maximum_fusion.packed_ref, bf16[8,1024,128]{2,1,0:T(8,128)(2,1)S(1)} %constant_dynamic-update-slice_fusion.key_ref, bf16[8,1024,256]{2,1,0:T(8,128)(2,1)} %fusion.2.value_ref), custom_call_target="tpu_custom_call" | custom-call | tf_op jit(solution)/shard_map/attend_class/pallas_call | solution.py:165
  80.0 4.4 %collective-permute-done.8.refs_2_ = bf16[4,64,1152]{2,1,0:T(8,128)(2,1)S(1)} collective-permute-done((bf16[4,64,1152]{2,1,0:T(8,128)(2,1)S(1)}, bf16[4,64,1152]{2,1,0:T(8,128)(2,1)S(1)}, u32[]{:S(2)}, u32[]{:S(2)}) %collective-permute-start.8) | collective-permute-done | bytes 589856 | tf_op jit(solution)/shard_map/ppermute | solution.py:179
  84.4 6.4 %collective-permute-done.6.refs_1_ = bf16[4,64,1152]{2,1,0:T(8,128)(2,1)S(1)} collective-permute-done((bf16[4,64,1152]{2,1,0:T(8,128)(2,1)S(1)}, bf16[4,64,1152]{2,1,0:T(8,128)(2,1)S(1)}, u32[]{:S(2)}, u32[]{:S(2)}) %collective-permute-start.6) | collective-permute-done | bytes 589856 | tf_op jit(solution)/shard_map/ppermute | solution.py:179
  90.8 2.4 %merge_row.1 = bf16[4,64,1152]{2,1,0:T(8,128)(2,1)S(1)} custom-call(bf16[4,64,1152]{2,1,0:T(8,128)(2,1)S(1)} %attend_class.4.refs_0_, bf16[4,64,1152]{2,1,0:T(8,128)(2,1)S(1)} %collective-permute-done.6.refs_1_, bf16[4,64,1152]{2,1,0:T(8,128)(2,1)S(1)} %collective-permute-done.8.refs_2_, bf16[4,64,1152]{2,1,0:T(8,128)(2,1)S(1)} %collective-permute-done.10.refs_3_), custom_call_target="tpu_custom_call" | custom-call | tf_op jit(solution)/shard_map/merge_row/pallas_call | solution.py:165
  93.4 2.0 %collective-permute-start.12 = (bf16[64,1152]{1,0:T(8,128)(2,1)S(1)}, bf16[64,1152]{1,0:T(8,128)(2,1)S(1)}, u32[]{:S(2)}, u32[]{:S(2)}) collective-permute-start(bf16[64,1152]{1,0:T(8,128)(2,1)S(1)} %get-tuple-element.10), channel_id=1, source_target_pairs={{0,64},{64,128},{128,192},{192,0},{1,65},{65,129},{129,193},{193,1... | collective-permute-start | bytes 442376 | tf_op jit(solution)/shard_map/ppermute | solution.py:179
  95.4 1.4 %host_part.1 = (f32[64,1024]{1,0:T(8,128)S(1)}, f32[64,128]{1,0:T(8,128)S(1)}) custom-call(bf16[64,1024]{1,0:T(8,128)(2,1)S(1)} %bitcast.36, bf16[1024,128]{1,0:T(8,128)(2,1)S(1)} %bitcast.38, bf16[1024,128]{1,0:T(8,128)(2,1)S(1)} %bitcast.39, bf16[64,128]{1,0:T(8,128)(2,1)S(1)} %bitcast.40, bf16[64,128]{1,0:T(8,128)(2,1)S(1)} %bitcast.41), custom_call_target="tpu_custom_call" | custom-call | tf_op jit(solution)/shard_map/host_part/pallas_call | solution.py:165
  96.9 2.7 %collective-permute-done.11.refs_1_ = bf16[64,1152]{1,0:T(8,128)(2,1)S(1)} collective-permute-done((bf16[64,1152]{1,0:T(8,128)(2,1)S(1)}, bf16[64,1152]{1,0:T(8,128)(2,1)S(1)}, u32[]{:S(2)}, u32[]{:S(2)}) %collective-permute-start.11) | collective-permute-done | bytes 147488 | tf_op jit(solution)/shard_map/ppermute | solution.py:179
  99.5 3.4 %collective-permute-done.12.refs_2_ = bf16[64,1152]{1,0:T(8,128)(2,1)S(1)} collective-permute-done((bf16[64,1152]{1,0:T(8,128)(2,1)S(1)}, bf16[64,1152]{1,0:T(8,128)(2,1)S(1)}, u32[]{:S(2)}, u32[]{:S(2)}) %collective-permute-start.12) | collective-permute-done | bytes 147488 | tf_op jit(solution)/shard_map/ppermute | solution.py:179
  103.4 17.3 %all_to_all.5 = bf16[8,8,1024]{2,1,0:T(8,128)(2,1)S(1)} all-to-all(bf16[8,8,1024]{2,1,0:T(8,128)(2,1)S(1)} %bitcast.37), channel_id=1, replica_groups=mesh['x'=4,'y'=4,'c'=2,'kv'=8] {'kv'}, dimensions={0} | all-to-all | bytes 262144 | tf_op jit(solution)/shard_map/all_to_all | solution.py:268
  (44 shorter events, 6.7 us)
Async XLA Ops:
  3.3 7.4 %collective-permute-start = (bf16[80,1024]{1,0:T(8,128)(2,1)S(1)}, bf16[80,1024]{1,0:T(8,128)(2,1)S(1)}, u32[]{:S(2)}, u32[]{:S(2)}) collective-permute-start(bf16[80,1024]{1,0:T(8,128)(2,1)S(1)} %get-tuple-element.14), channel_id=1, source_target_pairs={{0,64},{64,128},{128,192},{192,0},{1,65},{65,129},{129,193},{193,1... | collective-permute-start | bytes 491528 | tf_op jit(solution)/shard_map/ppermute | solution.py:179
  4.9 8.5 %collective-permute-start.1 = (bf16[80,1024]{1,0:T(8,128)(2,1)S(1)}, bf16[80,1024]{1,0:T(8,128)(2,1)S(1)}, u32[]{:S(2)}, u32[]{:S(2)}) collective-permute-start(bf16[80,1024]{1,0:T(8,128)(2,1)S(1)} %get-tuple-element.14), channel_id=1, source_target_pairs={{0,192},{64,0},{128,64},{192,128},{1,193},{65,1},{129,65},{193,129... | collective-permute-start | bytes 491528 | tf_op jit(solution)/shard_map/ppermute | solution.py:179
  6.6 8.4 %collective-permute-start.2 = (bf16[80,1024]{1,0:T(8,128)(2,1)S(1)}, bf16[80,1024]{1,0:T(8,128)(2,1)S(1)}, u32[]{:S(2)}, u32[]{:S(2)}) collective-permute-start(bf16[80,1024]{1,0:T(8,128)(2,1)S(1)} %get-tuple-element.14), channel_id=1, source_target_pairs={{0,128},{64,192},{128,0},{192,64},{1,129},{65,193},{129,1},{193,65... | collective-permute-start | bytes 491528 | tf_op jit(solution)/shard_map/ppermute | solution.py:179
  15.1 19.3 %collective-permute-start.9 = (bf16[4,80,1024]{2,1,0:T(8,128)(2,1)S(1)}, bf16[4,80,1024]{2,1,0:T(8,128)(2,1)S(1)}, u32[]{:S(2)}, u32[]{:S(2)}) collective-permute-start(bf16[4,80,1024]{2,1,0:T(8,128)(2,1)S(1)} %pad_maximum_fusion.packed_ref), channel_id=1, source_target_pairs={{0,32},{16,48},{32,0},{48,16},{1,33},{17,49},{33,1},{49,17},{2,34}... | collective-permute-start | bytes 1966088 | tf_op jit(solution)/shard_map/ppermute | solution.py:179
  16.4 29.9 %collective-permute-start.7 = (bf16[4,80,1024]{2,1,0:T(8,128)(2,1)S(1)}, bf16[4,80,1024]{2,1,0:T(8,128)(2,1)S(1)}, u32[]{:S(2)}, u32[]{:S(2)}) collective-permute-start(bf16[4,80,1024]{2,1,0:T(8,128)(2,1)S(1)} %pad_maximum_fusion.packed_ref), channel_id=1, source_target_pairs={{0,48},{16,0},{32,16},{48,32},{1,49},{17,1},{33,17},{49,33},{2,50}... | collective-permute-start | bytes 1966088 | tf_op jit(solution)/shard_map/ppermute | solution.py:179
  16.4 33.4 %collective-permute-start.3 = (bf16[4,1024,128]{2,1,0:T(8,128)(2,1)}, bf16[4,1024,128]{2,1,0:T(8,128)(2,1)S(1)}, u32[]{:S(2)}, u32[]{:S(2)}) collective-permute-start(bf16[4,1024,128]{2,1,0:T(8,128)(2,1)} %param.12), channel_id=1, source_target_pairs={{0,8},{8,0},{1,9},{9,1},{2,10},{10,2},{3,11},{11,3},{4,12},{12,4},... | collective-permute-start | bytes 3145736 | tf_op jit(solution)/shard_map/ppermute | solution.py:207
  16.4 30.0 %collective-permute-start.4 = (bf16[4,1024,128]{2,1,0:T(8,128)(2,1)}, bf16[4,1024,128]{2,1,0:T(8,128)(2,1)}, u32[]{:S(2)}, u32[]{:S(2)}) collective-permute-start(bf16[4,1024,128]{2,1,0:T(8,128)(2,1)} %param.13), channel_id=1, source_target_pairs={{0,8},{8,0},{1,9},{9,1},{2,10},{10,2},{3,11},{11,3},{4,12},{12,4},... | collective-permute-start | bytes 3145736 | tf_op jit(solution)/shard_map/ppermute | solution.py:208
  18.2 28.2 %collective-permute-start.5 = (bf16[4,80,1024]{2,1,0:T(8,128)(2,1)S(1)}, bf16[4,80,1024]{2,1,0:T(8,128)(2,1)S(1)}, u32[]{:S(2)}, u32[]{:S(2)}) collective-permute-start(bf16[4,80,1024]{2,1,0:T(8,128)(2,1)S(1)} %pad_maximum_fusion.packed_ref), channel_id=1, source_target_pairs={{0,16},{16,32},{32,48},{48,0},{1,17},{17,33},{33,49},{49,1},{2,18}... | collective-permute-start | bytes 1966088 | tf_op jit(solution)/shard_map/ppermute | solution.py:179
  56.2 23.8 %collective-permute-start.10 = (bf16[4,64,1152]{2,1,0:T(8,128)(2,1)S(1)}, bf16[4,64,1152]{2,1,0:T(8,128)(2,1)S(1)}, u32[]{:S(2)}, u32[]{:S(2)}) collective-permute-start(bf16[4,64,1152]{2,1,0:T(8,128)(2,1)S(1)} %attend_class.7), channel_id=1, source_target_pairs={{0,32},{16,48},{32,0},{48,16},{1,33},{17,49},{33,1},{49,17},{2,34}... | collective-permute-start | bytes 1769480 | tf_op jit(solution)/shard_map/ppermute | solution.py:179
  61.2 23.2 %collective-permute-start.8 = (bf16[4,64,1152]{2,1,0:T(8,128)(2,1)S(1)}, bf16[4,64,1152]{2,1,0:T(8,128)(2,1)S(1)}, u32[]{:S(2)}, u32[]{:S(2)}) collective-permute-start(bf16[4,64,1152]{2,1,0:T(8,128)(2,1)S(1)} %attend_class.6), channel_id=1, source_target_pairs={{0,16},{16,32},{32,48},{48,0},{1,17},{17,33},{33,49},{49,1},{2,18}... | collective-permute-start | bytes 1769480 | tf_op jit(solution)/shard_map/ppermute | solution.py:179
  74.9 16.0 %collective-permute-start.6 = (bf16[4,64,1152]{2,1,0:T(8,128)(2,1)S(1)}, bf16[4,64,1152]{2,1,0:T(8,128)(2,1)S(1)}, u32[]{:S(2)}, u32[]{:S(2)}) collective-permute-start(bf16[4,64,1152]{2,1,0:T(8,128)(2,1)S(1)} %attend_class.5), channel_id=1, source_target_pairs={{0,48},{16,0},{32,16},{48,32},{1,49},{17,1},{33,17},{49,33},{2,50}... | collective-permute-start | bytes 1769480 | tf_op jit(solution)/shard_map/ppermute | solution.py:179
  75.0 20.4 %copy-start = (bf16[1,64,1024]{2,1,0:T(8,128)(2,1)S(1)}, bf16[1,64,1024]{2,1,0:T(8,128)(2,1)}, u32[]{:S(2)}) copy-start(bf16[1,64,1024]{2,1,0:T(8,128)(2,1)} %param.9) | copy-start | bytes 393220
  75.0 20.4 %copy-start.1 = (bf16[1,8,128,128]{3,2,1,0:T(8,128)(2,1)S(1)}, bf16[1,8,128,128]{3,2,1,0:T(8,128)(2,1)}, u32[]{:S(2)}) copy-start(bf16[1,8,128,128]{3,2,1,0:T(8,128)(2,1)} %param.14) | copy-start | bytes 786436
  75.0 20.4 %copy-start.2 = (bf16[1,8,128,128]{3,2,1,0:T(8,128)(2,1)S(1)}, bf16[1,8,128,128]{3,2,1,0:T(8,128)(2,1)}, u32[]{:S(2)}) copy-start(bf16[1,8,128,128]{3,2,1,0:T(8,128)(2,1)} %param.15) | copy-start | bytes 786436
  75.0 20.4 %copy-start.3 = (bf16[1,64,128]{2,1,0:T(8,128)(2,1)S(1)}, bf16[1,64,128]{2,1,0:T(8,128)(2,1)}, u32[]{:S(2)}) copy-start(bf16[1,64,128]{2,1,0:T(8,128)(2,1)} %param.10) | copy-start | bytes 49156
  75.1 20.4 %copy-start.4 = (bf16[1,64,128]{2,1,0:T(8,128)(2,1)S(1)}, bf16[1,64,128]{2,1,0:T(8,128)(2,1)}, u32[]{:S(2)}) copy-start(bf16[1,64,128]{2,1,0:T(8,128)(2,1)} %param.11) | copy-start | bytes 49156
  93.3 6.3 %collective-permute-start.11 = (bf16[64,1152]{1,0:T(8,128)(2,1)S(1)}, bf16[64,1152]{1,0:T(8,128)(2,1)S(1)}, u32[]{:S(2)}, u32[]{:S(2)}) collective-permute-start(bf16[64,1152]{1,0:T(8,128)(2,1)S(1)} %get-tuple-element.11), channel_id=1, source_target_pairs={{0,192},{64,0},{128,64},{192,128},{1,193},{65,1},{129,65},{193,129... | collective-permute-start | bytes 442376 | tf_op jit(solution)/shard_map/ppermute | solution.py:179
  93.4 9.5 %collective-permute-start.12 = (bf16[64,1152]{1,0:T(8,128)(2,1)S(1)}, bf16[64,1152]{1,0:T(8,128)(2,1)S(1)}, u32[]{:S(2)}, u32[]{:S(2)}) collective-permute-start(bf16[64,1152]{1,0:T(8,128)(2,1)S(1)} %get-tuple-element.10), channel_id=1, source_target_pairs={{0,64},{64,128},{128,192},{192,0},{1,65},{65,129},{129,193},{193,1... | collective-permute-start | bytes 442376 | tf_op jit(solution)/shard_map/ppermute | solution.py:179
  95.4 7.5 %collective-permute-start.13 = (bf16[64,1152]{1,0:T(8,128)(2,1)S(1)}, bf16[64,1152]{1,0:T(8,128)(2,1)S(1)}, u32[]{:S(2)}, u32[]{:S(2)}) collective-permute-start(bf16[64,1152]{1,0:T(8,128)(2,1)S(1)} %get-tuple-element.9), channel_id=1, source_target_pairs={{0,128},{64,192},{128,0},{192,64},{1,129},{65,193},{129,1},{193,65... | collective-permute-start | bytes 442376 | tf_op jit(solution)/shard_map/ppermute | solution.py:179

commit v2 on v1

v2 whole, which is shorter than its diff:
```python
import functools
import math

import jax
import jax.numpy as jnp
from jax import lax
from jax.experimental import pallas as pl
from jax.experimental.pallas import tpu as pltpu
from jax.sharding import Mesh
from jax.sharding import PartitionSpec as P

HD = 128
LANES = 128
PARTS = 3
RING = 4
HOPS = (0, 1, 3, 2)
very_low = -1e30
log2_scale = math.log2(math.e) / math.sqrt(HD)
VMEM_BYTES = 24 * 1024 * 1024


def contract_last(left, right):
    return lax.dot_general(
        left, right, (((1,), (1,)), ((), ())), preferred_element_type=jnp.float32
    )


def stack_heads(rows, heads):
    return jnp.concatenate([rows[:, g * HD : (g + 1) * HD] for g in range(heads)], axis=0)


def pack_kernel(cite_ref, query_ref, picks_ref, out_ref, sem):
    suffix_len, width = query_ref.shape
    cites, pick_count = picks_ref.shape
    blocks = width // LANES
    copy = pltpu.make_async_copy(query_ref, out_ref.at[pl.ds(0, suffix_len), :], sem)
    copy.start()
    picks = jnp.concatenate([picks_ref[c : c + 1, :] for c in range(cites)], axis=1)
    total = cites * pick_count
    within = lax.broadcasted_iota(jnp.int32, (LANES, total), 0)
    low = jnp.where(within == picks % LANES, 1.0, 0.0).astype(jnp.bfloat16)
    row = lax.broadcasted_iota(jnp.int32, (blocks * cites, total), 0)
    owner = lax.broadcasted_iota(jnp.int32, (blocks * cites, total), 1) // pick_count
    high = jnp.where(row == (picks // LANES) * cites + owner, 1.0, 0.0).astype(jnp.bfloat16)
    hits = contract_last(high, low)
    line = lax.broadcasted_iota(jnp.int32, (cites, LANES), 0)
    ids = jnp.zeros((cites, LANES), jnp.int32)
    for c in range(cites):
        ids = jnp.where(line == c, cite_ref[0, c], ids)
    ids = ids.astype(jnp.float32)
    for h in range(blocks):
        hit = hits[h * cites : (h + 1) * cites, :]
        out_ref[suffix_len:, h * LANES : (h + 1) * LANES] = jnp.where(hit > 0.5, -1.0 - ids, ids).astype(jnp.bfloat16)
    copy.wait()


def row_kernel(*refs):
    for j, source in enumerate(refs[:-1]):
        refs[-1][j, :, :] = source[...]


def attend_kernel(*refs, count, suffix_len, heads, cites):
    tables, blocks = refs[0:count], refs[count : 2 * count]
    own_key, own_value, other_key, other_value = refs[2 * count : 2 * count + 4]
    outs = refs[2 * count + 4 : 3 * count + 4]
    mask_s, query_s, max_s, acc_s = refs[3 * count + 4 :]
    rows = suffix_len * heads
    chunk = rows // 2
    requests = blocks[0].shape[0]
    local = own_key.shape[0]

    def add_slot(key_ref, value_ref, place, bias):
        for start in range(0, rows, chunk):
            part = pl.ds(start, chunk)
            scores = contract_last(query_s[part, :], key_ref[place]) * log2_scale + bias
            old_max = max_s[part, :]
            new_max = jnp.maximum(old_max, jnp.max(scores, axis=1, keepdims=True))
            weights = jnp.exp2(scores - new_max[:, 0:1]).astype(jnp.bfloat16)
            factor = jnp.exp2(old_max - new_max)
            value = value_ref[place]
            value = jnp.concatenate([value, jnp.ones_like(value)], axis=1)
            added = jnp.dot(weights, value, preferred_element_type=jnp.float32)
            acc_s[part, :] = acc_s[part, :] * jnp.concatenate([factor, factor], axis=1) + added
            max_s[part, :] = new_max

    for table_ref, packed_ref, out_ref in zip(tables, blocks, outs):

        def one_request(j, carry):
            found = table_ref[j, 0]
            for c in range(1, cites):
                found = jnp.maximum(found, table_ref[j, c])

            @pl.when(found >= 0)
            def _():
                query_s[...] = stack_heads(packed_ref[j, 0:suffix_len, :], heads)
                marks = packed_ref[j, suffix_len : suffix_len + cites, :].astype(jnp.float32)
                mask_s[...] = jnp.where(marks < 0.0, very_low, 0.0)
                max_s[...] = jnp.full_like(max_s, very_low)
                acc_s[...] = jnp.zeros_like(acc_s)

                def one_cite(c, inner):
                    place = table_ref[j, c]

                    @pl.when((place >= 0) & (place < local))
                    def _():
                        add_slot(own_key, own_value, place, mask_s[pl.ds(c, 1), :])

                    @pl.when(place >= local)
                    def _():
                        add_slot(other_key, other_value, place - local, mask_s[pl.ds(c, 1), :])

                    return inner

                lax.fori_loop(0, cites, one_cite, 0)
                lane = lax.broadcasted_iota(jnp.int32, (suffix_len, LANES), 1)
                stats = jnp.zeros((suffix_len, LANES), jnp.float32)
                for g in range(heads):
                    part = slice(g * suffix_len, (g + 1) * suffix_len)
                    total = acc_s[part, HD : 2 * HD]
                    out_ref[j, :, g * HD : (g + 1) * HD] = (acc_s[part, 0:HD] / total).astype(jnp.bfloat16)
                    stats = jnp.where(lane % heads == g, max_s[part, :] + jnp.log2(total), stats)
                out_ref[j, :, heads * HD :] = split_level(stats, lane, heads).astype(jnp.bfloat16)

            @pl.when(found < 0)
            def _():
                out_ref[j, :, 0 : heads * HD] = jnp.zeros((suffix_len, heads * HD), jnp.bfloat16)
                lane = lax.broadcasted_iota(jnp.int32, (suffix_len, LANES), 1)
                out_ref[j, :, heads * HD :] = jnp.where(lane < heads, very_low, 0.0).astype(jnp.bfloat16)

            return carry

        lax.fori_loop(0, requests, one_request, 0)


def split_level(level, lane, heads):
    stats = jnp.zeros_like(level)
    for i in range(PARTS):
        piece = level.astype(jnp.bfloat16).astype(jnp.float32)
        stats = jnp.where(lane // heads == i, piece, stats)
        level = level - piece
    return stats


def get_level(tile, heads):
    level = tile.astype(jnp.float32)
    total = level
    for i in range(1, PARTS):
        total = total + pltpu.roll(level, LANES - i * heads, 1)
    return total


def host_kernel(query_ref, fresh_key_ref, fresh_value_ref, suffix_key_ref, suffix_value_ref, out_ref, level_ref):
    suffix_len, width = query_ref.shape
    heads = width // HD
    query = stack_heads(query_ref[...], heads)
    fresh = contract_last(query, fresh_key_ref[...]) * log2_scale
    near = contract_last(query, suffix_key_ref[...]) * log2_scale
    place = lax.broadcasted_iota(jnp.int32, near.shape, 0) % suffix_len
    near = jnp.where(lax.broadcasted_iota(jnp.int32, near.shape, 1) <= place, near, very_low)
    top = jnp.maximum(jnp.max(fresh, axis=1, keepdims=True), jnp.max(near, axis=1, keepdims=True))
    fresh = jnp.exp2(fresh - top)
    near = jnp.exp2(near - top)
    total = jnp.sum(fresh, axis=1, keepdims=True) + jnp.sum(near, axis=1, keepdims=True)
    acc = jnp.dot(fresh.astype(jnp.bfloat16), fresh_value_ref[...], preferred_element_type=jnp.float32)
    acc = acc + jnp.dot(near.astype(jnp.bfloat16), suffix_value_ref[...], preferred_element_type=jnp.float32)
    acc = acc / total
    level = jnp.broadcast_to(top + jnp.log2(total), acc.shape)
    lane = lax.broadcasted_iota(jnp.int32, (suffix_len, LANES), 1)
    levels = jnp.zeros((suffix_len, LANES), jnp.float32)
    for g in range(heads):
        part = slice(g * suffix_len, (g + 1) * suffix_len)
        out_ref[:, g * HD : (g + 1) * HD] = acc[part]
        levels = jnp.where(lane == g, level[part], levels)
    level_ref[...] = levels


def weigh(levels):
    top = functools.reduce(jnp.maximum, levels)
    shares = [jnp.exp2(level - top) for level in levels]
    total = functools.reduce(jnp.add, shares)
    return [share / total for share in shares], top + jnp.log2(total)


def merge_kernel(*refs, packed, wide, wide_out):
    heads = refs[0].shape[-1] // HD - (1 if packed else 0)
    width = heads * HD
    outs = refs[packed + 2 * wide :]
    requests, suffix_len = outs[0].shape[:2]
    lane = lax.broadcasted_iota(jnp.int32, (suffix_len, LANES), 1)
    for j in range(requests):
        bodies = [refs[i] for i in range(packed)] + [refs[packed + 2 * i] for i in range(wide)]
        levels = [get_level(refs[i][j, :, width:], heads) for i in range(packed)]
        levels += [refs[packed + 2 * i + 1][j] for i in range(wide)]
        top = functools.reduce(jnp.maximum, levels)
        shares = [jnp.exp2(level - top) for level in levels]
        total = functools.reduce(jnp.add, shares)
        shares = [share / total for share in shares]
        for g in range(heads):
            part = slice(g * HD, (g + 1) * HD)
            terms = [b[j, :, part].astype(jnp.float32) * w[:, g : g + 1] for b, w in zip(bodies, shares)]
            outs[0][j, :, part] = functools.reduce(jnp.add, terms).astype(outs[0].dtype)
        level = top + jnp.log2(total)
        if wide_out:
            outs[1][j] = level
        elif outs[0].shape[-1] > width:
            spread = level
            for i in range(1, PARTS):
                spread = jnp.where(lane // heads == i, pltpu.roll(level, i * heads, 1), spread)
            outs[0][j, :, width:] = split_level(spread, lane, heads).astype(jnp.bfloat16)


def merge_call(packed, wide, out_shape, name):
    wide_out = isinstance(out_shape, tuple)
    return in_vmem(
        functools.partial(merge_kernel, packed=len(packed), wide=len(wide), wide_out=wide_out),
        out_shape,
        (*packed, *(part for pair in wide for part in pair)),
        name=name,
    )


def in_vmem(kernel, out_shape, operands, scratch=(), smem=0, spaces=None, cost=None, name=None):
    spaces = spaces or [pltpu.SMEM] * smem + [pltpu.VMEM] * (len(operands) - smem)
    many = isinstance(out_shape, tuple)
    return pl.pallas_call(
        kernel,
        out_shape=out_shape,
        in_specs=[pl.BlockSpec(memory_space=s) for s in spaces],
        out_specs=tuple(pl.BlockSpec(memory_space=pltpu.VMEM) for _ in out_shape)
        if many
        else pl.BlockSpec(memory_space=pltpu.VMEM),
        scratch_shapes=list(scratch),
        compiler_params=pltpu.CompilerParams(vmem_limit_bytes=VMEM_BYTES),
        cost_estimate=cost,
        name=name,
    )(*operands)


def shift(value, first, hop):
    pairs = []
    for x in range(RING):
        for y in range(RING):
            for c in range(2):
                along_x = (c == 0) == first
                to_x = (x + hop) % RING if along_x else x
                to_y = y if along_x else (y + hop) % RING
                pairs.append(((x * RING + y) * 2 + c, (to_x * RING + to_y) * 2 + c))
    return lax.ppermute(value, ("x", "y", "c"), pairs)


def attend_call(tables, blocks, caches):
    requests, packed_len, width = blocks[0].shape
    cites = tables[0].shape[1]
    suffix_len, heads = packed_len - cites, width // HD
    rows = suffix_len * heads
    count = len(blocks)
    out = jax.ShapeDtypeStruct((requests, suffix_len, width + LANES), jnp.bfloat16)
    return in_vmem(
        functools.partial(attend_kernel, count=count, suffix_len=suffix_len, heads=heads, cites=cites),
        (out,) * count,
        (*tables, *blocks, *caches),
        scratch=(
            pltpu.VMEM((cites, caches[0].shape[1]), jnp.float32),
            pltpu.VMEM((rows, HD), jnp.bfloat16),
            pltpu.VMEM((rows, LANES), jnp.float32),
            pltpu.VMEM((rows, 2 * HD), jnp.float32),
        ),
        smem=count,
        cost=pl.CostEstimate(
            flops=count * requests * cites * rows * HD * 1024, transcendentals=0, bytes_accessed=count * 16 * 1024 * 1024
        ),
        name="attend_class",
    )


def body(
    queries,
    suffix_keys,
    suffix_values,
    passage_keys,
    passage_values,
    fresh_keys,
    fresh_values,
    citations,
    selected,
):
    _, suffix_len, width = queries.shape
    local_passages, length, _ = passage_keys.shape
    heads = width // HD
    cites = citations.shape[1]
    chip = lax.axis_index("x") * RING + lax.axis_index("y")
    core = lax.axis_index("c")

    packed = in_vmem(
        pack_kernel,
        jax.ShapeDtypeStruct((suffix_len + cites, width), jnp.bfloat16),
        (citations, queries[0], selected[0]),
        scratch=(pltpu.SemaphoreType.DMA,),
        spaces=(pltpu.SMEM, pl.ANY, pltpu.VMEM),
        name="pack",
    )
    packed, passage_keys, passage_values = lax.optimization_barrier((packed, passage_keys, passage_values))
    swap = [(0, 1), (1, 0)]
    other_keys = lax.ppermute(passage_keys, "c", swap)
    other_values = lax.ppermute(passage_values, "c", swap)

    host_out, host_level = in_vmem(
        host_kernel,
        (
            jax.ShapeDtypeStruct((suffix_len, width), jnp.float32),
            jax.ShapeDtypeStruct((suffix_len, LANES), jnp.float32),
        ),
        (
            queries[0],
            fresh_keys.reshape(-1, HD),
            fresh_values.reshape(-1, HD),
            suffix_keys[0],
            suffix_values[0],
        ),
        name="host_part",
    )

    row = in_vmem(
        row_kernel,
        jax.ShapeDtypeStruct((RING, *packed.shape), packed.dtype),
        (packed, *(shift(packed, True, hop) for hop in HOPS[1:])),
        name="row",
    )
    row, host_out, host_level = lax.optimization_barrier((row, host_out, host_level))
    classes = [row] + [shift(row, False, hop) for hop in HOPS[1:]]

    def places(block):
        marks = block[:, suffix_len:, 0].astype(jnp.int32)
        named = jnp.where(marks < 0, -1 - marks, marks)
        local = named - chip * (2 * local_passages)
        here = (local >= 0) & (local < 2 * local_passages)
        return jnp.where(here, (local + core * local_passages) % (2 * local_passages), -1)

    def attend(blocks):
        return attend_call([places(b) for b in blocks], blocks, (passage_keys, passage_values, other_keys, other_values))

    own = attend(classes[0:1])
    near_blocks, own = lax.optimization_barrier((classes[1:3], own))
    near = attend(near_blocks)
    far_block, near = lax.optimization_barrier((classes[3:4], near))
    far = attend(far_block)
    results = list(own) + list(near) + list(far)
    back = [shift(r, False, RING - hop) for r, hop in zip(results[1:], HOPS[1:])]
    partial = merge_call(
        (results[0], *back[:2]),
        (),
        (
            jax.ShapeDtypeStruct((RING, suffix_len, width), jnp.float32),
            jax.ShapeDtypeStruct((RING, suffix_len, LANES), jnp.float32),
        ),
        "merge_near",
    )
    merged = merge_call(
        back[2:], (partial,), jax.ShapeDtypeStruct((RING, suffix_len, width + LANES), jnp.bfloat16), "merge_row"
    )
    home = [merged[j : j + 1] for j in range(RING)]
    home = home[:1] + [shift(h, True, RING - hop) for h, hop in zip(home[1:], HOPS[1:])]
    attended = merge_call(
        home,
        ((host_out[None], host_level[None]),),
        jax.ShapeDtypeStruct((1, suffix_len, width), jnp.bfloat16),
        "merge_home",
    )[0]
    groups = lax.psum(1, "kv")
    pieces = attended.reshape(groups, suffix_len // groups, width)
    pieces = lax.all_to_all(pieces, "kv", split_axis=0, concat_axis=0, tiled=True)
    return jnp.transpose(pieces, (1, 0, 2)).reshape(1, suffix_len // groups, groups * width)


def solution(mesh):
    fine = Mesh(mesh.devices.reshape(RING, RING, 2, -1), ("x", "y", "c", "kv"))
    part = ("x", "y", "c")
    placed = (
        P(part, None, "kv"),
        P(part, None, "kv"),
        P(part, None, "kv"),
        P(part, None, "kv"),
        P(part, None, "kv"),
        P(part, None, None, "kv"),
        P(part, None, None, "kv"),
        P(part, None),
        P(part, None, None),
    )
    return jax.shard_map(body, mesh=fine, in_specs=placed, out_specs=P(part, "kv", None), check_vma=False)
```

time: 122 us -> 93.7 us (0.77)
  waiting for transfers between devices: 48.2 us -> 24.5 us
  other arithmetic: 6.86 us -> 0.64 us
  local copies, waits for them, and re-layouts: 2.16 us -> 6.08 us
  starting transfers between devices: 18.7 us -> 16 us
  Pallas kernels: 27.9 us -> 29.2 us
    ppermute x14, waiting for transfers between devices: 48.2 us -> 24.5 us  [the longest x12 24.5 us: shift(): return lax.ppermute(value, ('x', 'y', 'c'), pairs)]
    unnamed x12 -> x23, local copies, waits for them, and re-layouts: 1.98 us -> 6.03 us
    concatenate x1 -> x0, other arithmetic: 3.37 us -> none  [body(): jnp.concatenate([passage_values, lax.ppermute(passage_values, 'c', swap)]...]
    ppermute x14, starting transfers between devices: 18.7 us -> 16 us  [the longest x12 15.4 us: shift(): return lax.ppermute(value, ('x', 'y', 'c'), pairs)]
    reduce_or x1 -> x0, other arithmetic: 1.68 us -> none  [body(): jnp.any(selected[0][:, :, None] == positions[None, None, :], axis=1)]
    pallas_call x7 -> x9, Pallas kernels: 27.9 us -> 29.2 us  [in_vmem(): pl.pallas_call(kernel, out_shape=out_shape, in_specs=[pl.BlockSpec(memory...]
  transfers between devices with their start and end apart: 14 -> 14, of which waited for: 9 -> 7; matrix products, arithmetic and copies ran while one was open for 4% -> 1% of each run, Pallas kernels for 15% -> 28%
where the time goes in v2:
time: 93.7 us; the launch traced here: 94 us
  Pallas kernels  29.2 us (31%)
  waiting for transfers between devices  24.5 us (26%)
  blocking collectives  17.3 us (18%)
  starting transfers between devices  16 us (17%)
  local copies, waits for them, and re-layouts  6.08 us (6%)
    pallas_call x9, Pallas kernels, in_vmem(): pl.pallas_call(kernel, out_shape=out_shape, in_specs=[pl.BlockSpec(memory...  29.2 us
    ppermute x12, waiting for transfers between devices, shift(): return lax.ppermute(value, ('x', 'y', 'c'), pairs)  24.5 us
    all_to_all x1, blocking collectives, body(): lax.all_to_all(pieces, 'kv', split_axis=0, concat_axis=0, tiled=True)  17.3 us
    ppermute x12, starting transfers between devices, shift(): return lax.ppermute(value, ('x', 'y', 'c'), pairs)  15.4 us
    unnamed x23, local copies, waits for them, and re-layouts  6.03 us
  transfers between devices with their start and end apart: 14, of which 7 were waited for; matrix products, arithmetic and copies ran while one was open for 1% of the time, Pallas kernels for 28%

profile of v2, /device:TPU:24, one launch (start us, length us, event | category | flops | bytes accessed | tf_op | source)
XLA Modules:
  0.0 94.0 jit_solution(18280266321483235650)
XLA Ops:
  0.7 0.9 copy-done
  2.3 1.0 %pack.1.refs_0_ = bf16[72,1024]{1,0:T(8,128)(2,1)S(1)} custom-call(s32[1,8]{1,0:T(1,128)S(1)} %copy-done.7, bf16[64,1024]{1,0:T(8,128)(2,1)S(1)} %bitcast.12, s32[8,128]{1,0:T(8,128)S(1)} %bitcast.21), custom_call_target="tpu_custom_call" | custom-call | tf_op jit(solution)/shard_map/pack/pallas_call | solution.py:225
  3.8 3.0 %collective-permute-start.2 = (bf16[72,1024]{1,0:T(8,128)(2,1)S(1)}, bf16[72,1024]{1,0:T(8,128)(2,1)S(1)}, u32[]{:S(2)}, u32[]{:S(2)}) collective-permute-start(bf16[72,1024]{1,0:T(8,128)(2,1)S(1)} %pack.1.refs_0_), channel_id=1, source_target_pairs={{0,128},{8,40},{16,144},{24,56},{32,160},{40,8},{48,176},{56,24},{... | collective-permute-start | bytes 442376 | tf_op jit(solution)/shard_map/ppermute | solution.py:248
  6.9 1.1 %collective-permute-start.1 = (bf16[72,1024]{1,0:T(8,128)(2,1)S(1)}, bf16[72,1024]{1,0:T(8,128)(2,1)S(1)}, u32[]{:S(2)}, u32[]{:S(2)}) collective-permute-start(bf16[72,1024]{1,0:T(8,128)(2,1)S(1)} %pack.1.refs_0_), channel_id=1, source_target_pairs={{0,192},{8,56},{16,208},{24,8},{32,224},{40,24},{48,240},{56,40},{... | collective-permute-start | bytes 442376 | tf_op jit(solution)/shard_map/ppermute | solution.py:248
  8.9 0.9 %copy-done.2 = bf16[1,8,128,128]{3,2,1,0:T(8,128)(2,1)S(1)} copy-done((bf16[1,8,128,128]{3,2,1,0:T(8,128)(2,1)S(1)}, bf16[1,8,128,128]{3,2,1,0:T(8,128)(2,1)}, u32[]{:S(2)}) %copy-start.2) | copy-done | bytes 262168
  9.8 0.9 %copy-done.3 = bf16[1,8,128,128]{3,2,1,0:T(8,128)(2,1)S(1)} copy-done((bf16[1,8,128,128]{3,2,1,0:T(8,128)(2,1)S(1)}, bf16[1,8,128,128]{3,2,1,0:T(8,128)(2,1)}, u32[]{:S(2)}) %copy-start.3) | copy-done | bytes 262168
  10.8 1.4 %host_part.1 = (f32[64,1024]{1,0:T(8,128)S(1)}, f32[64,128]{1,0:T(8,128)S(1)}) custom-call(bf16[64,1024]{1,0:T(8,128)(2,1)S(1)} %bitcast.13, bf16[1024,128]{1,0:T(8,128)(2,1)S(1)} %bitcast.15, bf16[1024,128]{1,0:T(8,128)(2,1)S(1)} %bitcast.16, bf16[64,128]{1,0:T(8,128)(2,1)S(1)} %bitcast.19, bf16[64,128]{1,0:T(8,128)(2,1)S(1)} %bitcast.20), custom_call_target="tpu_custom_call" | custom-call | tf_op jit(solution)/shard_map/host_part/pallas_call | solution.py:225
  12.3 2.1 %collective-permute-done.refs_1_ = bf16[72,1024]{1,0:T(8,128)(2,1)S(1)} collective-permute-done((bf16[72,1024]{1,0:T(8,128)(2,1)S(1)}, bf16[72,1024]{1,0:T(8,128)(2,1)S(1)}, u32[]{:S(2)}, u32[]{:S(2)}) %collective-permute-start) | collective-permute-done | bytes 147488 | tf_op jit(solution)/shard_map/ppermute | solution.py:248
  15.2 2.5 %collective-permute-start.4 = (bf16[4,72,1024]{2,1,0:T(8,128)(2,1)S(1)}, bf16[4,72,1024]{2,1,0:T(8,128)(2,1)S(1)}, u32[]{:S(2)}, u32[]{:S(2)}) collective-permute-start(bf16[4,72,1024]{2,1,0:T(8,128)(2,1)S(1)} %row.1.refs_1_), channel_id=1, source_target_pairs={{0,16},{8,72},{16,32},{24,88},{32,48},{40,104},{48,0},{56,120},{64... | collective-permute-start | bytes 1769480 | tf_op jit(solution)/shard_map/ppermute | solution.py:248
  17.9 1.2 %copy-done.9 = bf16[4,1024,128]{2,1,0:T(8,128)(2,1)S(1)} copy-done((bf16[4,1024,128]{2,1,0:T(8,128)(2,1)S(1)}, bf16[4,1024,128]{2,1,0:T(8,128)(2,1)}, u32[]{:S(2)}) %copy-start.9) | copy-done | bytes 1048600
  19.2 5.0 %attend_class.3.refs_0_ = bf16[4,64,1152]{2,1,0:T(8,128)(2,1)S(1)} custom-call(s32[4,8]{1,0:T(4,128)S(1)} %fusion.1.refs_0_, bf16[4,72,1024]{2,1,0:T(8,128)(2,1)S(1)} %row.1.refs_1_, bf16[4,1024,128]{2,1,0:T(8,128)(2,1)S(1)} %copy-done.8, bf16[4,1024,128]{2,1,0:T(8,128)(2,1)S(1)} %copy-done.9, bf16[4,1024,128]{2,1,0:T(8,128)(2,1)} %collective-permute-done.6.refs_4_.refs_6_, ...), custom_call_target="tpu_custom_call" | custom-call | flops 2147483648 | bytes 16777216 | tf_op jit(solution)/shard_map/attend_class/pallas_call | solution.py:225
  24.1 7.7 %collective-permute-done.5.refs_3_ = bf16[4,72,1024]{2,1,0:T(8,128)(2,1)S(1)} collective-permute-done((bf16[4,72,1024]{2,1,0:T(8,128)(2,1)S(1)}, bf16[4,72,1024]{2,1,0:T(8,128)(2,1)S(1)}, u32[]{:S(2)}, u32[]{:S(2)}) %collective-permute-start.5) | collective-permute-done | bytes 589856 | tf_op jit(solution)/shard_map/ppermute | solution.py:248
  32.2 11.4 %attend_class.4 = (bf16[4,64,1152]{2,1,0:T(8,128)(2,1)S(1)}, bf16[4,64,1152]{2,1,0:T(8,128)(2,1)S(1)}) custom-call(s32[4,8]{1,0:T(4,128)S(1)} %get-tuple-element.45.refs_0_, s32[4,8]{1,0:T(4,128)S(1)} %get-tuple-element.46.refs_1_, bf16[4,72,1024]{2,1,0:T(8,128)(2,1)S(1)} %collective-permute-done.4.refs_2_, ...), custom_call_target="tpu_custom_call" | custom-call | flops 4294967296 | bytes 33554432 | tf_op jit(solution)/shard_map/attend_class/pallas_call | solution.py:225
  43.9 3.2 %collective-permute-start.10 = (bf16[4,64,1152]{2,1,0:T(8,128)(2,1)S(1)}, bf16[4,64,1152]{2,1,0:T(8,128)(2,1)S(1)}, u32[]{:S(2)}, u32[]{:S(2)}) collective-permute-start(bf16[4,64,1152]{2,1,0:T(8,128)(2,1)S(1)} %get-tuple-element.36), channel_id=1, source_target_pairs={{0,16},{8,72},{16,32},{24,88},{32,48},{40,104},{48,0},{56,120},{64... | collective-permute-start | bytes 1769480 | tf_op jit(solution)/shard_map/ppermute | solution.py:248
  47.2 6.5 %attend_class.5 = bf16[4,64,1152]{2,1,0:T(8,128)(2,1)S(1)} custom-call(s32[4,8]{1,0:T(4,128)S(1)} %fusion.7.refs_0_, bf16[4,72,1024]{2,1,0:T(8,128)(2,1)S(1)} %collective-permute-done.3.refs_1_, bf16[4,1024,128]{2,1,0:T(8,128)(2,1)S(1)} %copy-done.8, bf16[4,1024,128]{2,1,0:T(8,128)(2,1)S(1)} %copy-done.10, ...), custom_call_target="tpu_custom_call" | custom-call | flops 2147483648 | bytes 16777216 | tf_op jit(solution)/shard_map/attend_class/pallas_call | solution.py:225
  54.0 1.0 %collective-permute-done.9.refs_1_ = bf16[4,64,1152]{2,1,0:T(8,128)(2,1)S(1)} collective-permute-done((bf16[4,64,1152]{2,1,0:T(8,128)(2,1)S(1)}, bf16[4,64,1152]{2,1,0:T(8,128)(2,1)S(1)}, u32[]{:S(2)}, u32[]{:S(2)}) %collective-permute-start.9) | collective-permute-done | bytes 589856 | tf_op jit(solution)/shard_map/ppermute | solution.py:248
  55.0 5.9 %collective-permute-done.10.refs_2_ = bf16[4,64,1152]{2,1,0:T(8,128)(2,1)S(1)} collective-permute-done((bf16[4,64,1152]{2,1,0:T(8,128)(2,1)S(1)}, bf16[4,64,1152]{2,1,0:T(8,128)(2,1)S(1)}, u32[]{:S(2)}, u32[]{:S(2)}) %collective-permute-start.10) | collective-permute-done | bytes 589856 | tf_op jit(solution)/shard_map/ppermute | solution.py:248
  60.9 1.9 %merge_near.1 = (f32[4,64,1024]{2,1,0:T(8,128)S(1)}, f32[4,64,128]{2,1,0:T(8,128)S(1)}) custom-call(bf16[4,64,1152]{2,1,0:T(8,128)(2,1)S(1)} %attend_class.3.refs_0_, bf16[4,64,1152]{2,1,0:T(8,128)(2,1)S(1)} %collective-permute-done.9.refs_1_, bf16[4,64,1152]{2,1,0:T(8,128)(2,1)S(1)} %collective-permute-done.10.refs_2_), custom_call_target="tpu_custom_call" | custom-call | tf_op jit(solution)/shard_map/merge_near/pallas_call | solution.py:225
  62.8 3.1 %collective-permute-done.8.refs_0_ = bf16[4,64,1152]{2,1,0:T(8,128)(2,1)S(1)} collective-permute-done((bf16[4,64,1152]{2,1,0:T(8,128)(2,1)S(1)}, bf16[4,64,1152]{2,1,0:T(8,128)(2,1)S(1)}, u32[]{:S(2)}, u32[]{:S(2)}) %collective-permute-start.8) | collective-permute-done | bytes 589856 | tf_op jit(solution)/shard_map/ppermute | solution.py:248
  65.8 1.4 %merge_row.1 = bf16[4,64,1152]{2,1,0:T(8,128)(2,1)S(1)} custom-call(bf16[4,64,1152]{2,1,0:T(8,128)(2,1)S(1)} %collective-permute-done.8.refs_0_, f32[4,64,1024]{2,1,0:T(8,128)S(1)} %get-tuple-element.37.refs_1_, f32[4,64,128]{2,1,0:T(8,128)S(1)} %get-tuple-element.38.refs_2_), custom_call_target="tpu_custom_call" | custom-call | tf_op jit(solution)/shard_map/merge_row/pallas_call | solution.py:225
  67.5 3.2 %collective-permute-start.11 = (bf16[1,64,1152]{2,1,0:T(8,128)(2,1)S(1)}, bf16[1,64,1152]{2,1,0:T(8,128)(2,1)S(1)}, u32[]{:S(2)}, u32[]{:S(2)}) collective-permute-start(bf16[1,64,1152]{2,1,0:T(8,128)(2,1)S(1)} %get-tuple-element.43), channel_id=1, source_target_pairs={{0,192},{8,56},{16,208},{24,8},{32,224},{40,24},{48,240},{56,40},{... | collective-permute-start | bytes 442376 | tf_op jit(solution)/shard_map/ppermute | solution.py:248
  70.7 3.4 %collective-permute-done.13.refs_3_ = bf16[1,64,1152]{2,1,0:T(8,128)(2,1)S(1)} collective-permute-done((bf16[1,64,1152]{2,1,0:T(8,128)(2,1)S(1)}, bf16[1,64,1152]{2,1,0:T(8,128)(2,1)S(1)}, u32[]{:S(2)}, u32[]{:S(2)}) %collective-permute-start.13) | collective-permute-done | bytes 147488 | tf_op jit(solution)/shard_map/ppermute | solution.py:248
  74.1 1.3 %collective-permute-done.12.refs_2_ = bf16[1,64,1152]{2,1,0:T(8,128)(2,1)S(1)} collective-permute-done((bf16[1,64,1152]{2,1,0:T(8,128)(2,1)S(1)}, bf16[1,64,1152]{2,1,0:T(8,128)(2,1)S(1)}, u32[]{:S(2)}, u32[]{:S(2)}) %collective-permute-start.12) | collective-permute-done | bytes 147488 | tf_op jit(solution)/shard_map/ppermute | solution.py:248
  76.0 17.3 %all_to_all.5 = bf16[8,8,1024]{2,1,0:T(8,128)(2,1)S(1)} all-to-all(bf16[8,8,1024]{2,1,0:T(8,128)(2,1)S(1)} %bitcast.14), channel_id=1, replica_groups=mesh['x'=4,'y'=4,'c'=2,'kv'=8] {'kv'}, dimensions={0} | all-to-all | bytes 262144 | tf_op jit(solution)/shard_map/all_to_all | solution.py:371
  (45 shorter events, 6.2 us)
Async XLA Ops:
  0.7 0.9 copy-start
  1.6 0.7 copy-start.6
  2.2 6.6 %copy-start.1 = (bf16[1,64,1024]{2,1,0:T(8,128)(2,1)S(1)}, bf16[1,64,1024]{2,1,0:T(8,128)(2,1)}, u32[]{:S(2)}) copy-start(bf16[1,64,1024]{2,1,0:T(8,128)(2,1)} %param.9) | copy-start | bytes 393220
  2.3 6.6 %copy-start.4 = (bf16[1,64,128]{2,1,0:T(8,128)(2,1)S(1)}, bf16[1,64,128]{2,1,0:T(8,128)(2,1)}, u32[]{:S(2)}) copy-start(bf16[1,64,128]{2,1,0:T(8,128)(2,1)} %param.10) | copy-start | bytes 49156
  2.3 6.6 %copy-start.5 = (bf16[1,64,128]{2,1,0:T(8,128)(2,1)S(1)}, bf16[1,64,128]{2,1,0:T(8,128)(2,1)}, u32[]{:S(2)}) copy-start(bf16[1,64,128]{2,1,0:T(8,128)(2,1)} %param.11) | copy-start | bytes 49156
  3.2 14.7 %collective-permute-start.6 = (bf16[4,1024,128]{2,1,0:T(8,128)(2,1)}, bf16[4,1024,128]{2,1,0:T(8,128)(2,1)}, u32[]{:S(2)}, u32[]{:S(2)}) collective-permute-start(bf16[4,1024,128]{2,1,0:T(8,128)(2,1)} %refs_2_.1), channel_id=1, source_target_pairs={{0,8},{8,0},{1,9},{9,1},{2,10},{10,2},{3,11},{11,3},{4,12},{12,4},... | collective-permute-start | bytes 3145736 | tf_op jit(solution)/shard_map/ppermute | solution.py:304
  3.3 14.6 %collective-permute-start.7 = (bf16[4,1024,128]{2,1,0:T(8,128)(2,1)}, bf16[4,1024,128]{2,1,0:T(8,128)(2,1)}, u32[]{:S(2)}, u32[]{:S(2)}) collective-permute-start(bf16[4,1024,128]{2,1,0:T(8,128)(2,1)} %refs_3_.1), channel_id=1, source_target_pairs={{0,8},{8,0},{1,9},{9,1},{2,10},{10,2},{3,11},{11,3},{4,12},{12,4},... | collective-permute-start | bytes 3145736 | tf_op jit(solution)/shard_map/ppermute | solution.py:305
  3.8 8.4 %collective-permute-start.2 = (bf16[72,1024]{1,0:T(8,128)(2,1)S(1)}, bf16[72,1024]{1,0:T(8,128)(2,1)S(1)}, u32[]{:S(2)}, u32[]{:S(2)}) collective-permute-start(bf16[72,1024]{1,0:T(8,128)(2,1)S(1)} %pack.1.refs_0_), channel_id=1, source_target_pairs={{0,128},{8,40},{16,144},{24,56},{32,160},{40,8},{48,176},{56,24},{... | collective-permute-start | bytes 442376 | tf_op jit(solution)/shard_map/ppermute | solution.py:248
  6.9 5.4 %collective-permute-start.1 = (bf16[72,1024]{1,0:T(8,128)(2,1)S(1)}, bf16[72,1024]{1,0:T(8,128)(2,1)S(1)}, u32[]{:S(2)}, u32[]{:S(2)}) collective-permute-start(bf16[72,1024]{1,0:T(8,128)(2,1)S(1)} %pack.1.refs_0_), channel_id=1, source_target_pairs={{0,192},{8,56},{16,208},{24,8},{32,224},{40,24},{48,240},{56,40},{... | collective-permute-start | bytes 442376 | tf_op jit(solution)/shard_map/ppermute | solution.py:248
  8.0 6.4 %collective-permute-start = (bf16[72,1024]{1,0:T(8,128)(2,1)S(1)}, bf16[72,1024]{1,0:T(8,128)(2,1)S(1)}, u32[]{:S(2)}, u32[]{:S(2)}) collective-permute-start(bf16[72,1024]{1,0:T(8,128)(2,1)S(1)} %pack.1.refs_0_), channel_id=1, source_target_pairs={{0,64},{8,24},{16,80},{24,40},{32,96},{40,56},{48,112},{56,8},{64,... | collective-permute-start | bytes 442376 | tf_op jit(solution)/shard_map/ppermute | solution.py:248
  8.9 1.0 %copy-start.2 = (bf16[1,8,128,128]{3,2,1,0:T(8,128)(2,1)S(1)}, bf16[1,8,128,128]{3,2,1,0:T(8,128)(2,1)}, u32[]{:S(2)}) copy-start(bf16[1,8,128,128]{3,2,1,0:T(8,128)(2,1)} %param.14) | copy-start | bytes 786436
  9.8 0.9 %copy-start.3 = (bf16[1,8,128,128]{3,2,1,0:T(8,128)(2,1)S(1)}, bf16[1,8,128,128]{3,2,1,0:T(8,128)(2,1)}, u32[]{:S(2)}) copy-start(bf16[1,8,128,128]{3,2,1,0:T(8,128)(2,1)} %param.15) | copy-start | bytes 786436
  10.8 7.1 %copy-start.8 = (bf16[4,1024,128]{2,1,0:T(8,128)(2,1)S(1)}, bf16[4,1024,128]{2,1,0:T(8,128)(2,1)}, u32[]{:S(2)}) copy-start(bf16[4,1024,128]{2,1,0:T(8,128)(2,1)} %refs_2_.1) | copy-start | bytes 3145732
  14.4 17.5 %collective-permute-start.5 = (bf16[4,72,1024]{2,1,0:T(8,128)(2,1)S(1)}, bf16[4,72,1024]{2,1,0:T(8,128)(2,1)S(1)}, u32[]{:S(2)}, u32[]{:S(2)}) collective-permute-start(bf16[4,72,1024]{2,1,0:T(8,128)(2,1)S(1)} %row.1.refs_1_), channel_id=1, source_target_pairs={{0,48},{8,200},{16,0},{24,216},{32,16},{40,232},{48,32},{56,248},{... | collective-permute-start | bytes 1769480 | tf_op jit(solution)/shard_map/ppermute | solution.py:248
  15.2 16.7 %collective-permute-start.4 = (bf16[4,72,1024]{2,1,0:T(8,128)(2,1)S(1)}, bf16[4,72,1024]{2,1,0:T(8,128)(2,1)S(1)}, u32[]{:S(2)}, u32[]{:S(2)}) collective-permute-start(bf16[4,72,1024]{2,1,0:T(8,128)(2,1)S(1)} %row.1.refs_1_), channel_id=1, source_target_pairs={{0,16},{8,72},{16,32},{24,88},{32,48},{40,104},{48,0},{56,120},{64... | collective-permute-start | bytes 1769480 | tf_op jit(solution)/shard_map/ppermute | solution.py:248
  17.7 26.0 %collective-permute-start.3 = (bf16[4,72,1024]{2,1,0:T(8,128)(2,1)S(1)}, bf16[4,72,1024]{2,1,0:T(8,128)(2,1)S(1)}, u32[]{:S(2)}, u32[]{:S(2)}) collective-permute-start(bf16[4,72,1024]{2,1,0:T(8,128)(2,1)S(1)} %row.1.refs_1_), channel_id=1, source_target_pairs={{0,32},{8,136},{16,48},{24,152},{32,0},{40,168},{48,16},{56,184},{... | collective-permute-start | bytes 1769480 | tf_op jit(solution)/shard_map/ppermute | solution.py:248
  17.9 1.2 %copy-start.9 = (bf16[4,1024,128]{2,1,0:T(8,128)(2,1)S(1)}, bf16[4,1024,128]{2,1,0:T(8,128)(2,1)}, u32[]{:S(2)}) copy-start(bf16[4,1024,128]{2,1,0:T(8,128)(2,1)} %refs_3_.1) | copy-start | bytes 3145732
  19.2 13.1 %copy-start.10 = (bf16[4,1024,128]{2,1,0:T(8,128)(2,1)S(1)}, bf16[4,1024,128]{2,1,0:T(8,128)(2,1)}, u32[]{:S(2)}) copy-start(bf16[4,1024,128]{2,1,0:T(8,128)(2,1)} %refs_3_.1) | copy-start | bytes 3145732
  43.8 11.2 %collective-permute-start.9 = (bf16[4,64,1152]{2,1,0:T(8,128)(2,1)S(1)}, bf16[4,64,1152]{2,1,0:T(8,128)(2,1)S(1)}, u32[]{:S(2)}, u32[]{:S(2)}) collective-permute-start(bf16[4,64,1152]{2,1,0:T(8,128)(2,1)S(1)} %get-tuple-element.35), channel_id=1, source_target_pairs={{0,48},{8,200},{16,0},{24,216},{32,16},{40,232},{48,32},{56,248},{... | collective-permute-start | bytes 1769480 | tf_op jit(solution)/shard_map/ppermute | solution.py:248
  43.9 17.0 %collective-permute-start.10 = (bf16[4,64,1152]{2,1,0:T(8,128)(2,1)S(1)}, bf16[4,64,1152]{2,1,0:T(8,128)(2,1)S(1)}, u32[]{:S(2)}, u32[]{:S(2)}) collective-permute-start(bf16[4,64,1152]{2,1,0:T(8,128)(2,1)S(1)} %get-tuple-element.36), channel_id=1, source_target_pairs={{0,16},{8,72},{16,32},{24,88},{32,48},{40,104},{48,0},{56,120},{64... | collective-permute-start | bytes 1769480 | tf_op jit(solution)/shard_map/ppermute | solution.py:248
  53.7 12.2 %collective-permute-start.8 = (bf16[4,64,1152]{2,1,0:T(8,128)(2,1)S(1)}, bf16[4,64,1152]{2,1,0:T(8,128)(2,1)S(1)}, u32[]{:S(2)}, u32[]{:S(2)}) collective-permute-start(bf16[4,64,1152]{2,1,0:T(8,128)(2,1)S(1)} %attend_class.5), channel_id=1, source_target_pairs={{0,32},{8,136},{16,48},{24,152},{32,0},{40,168},{48,16},{56,184},{... | collective-permute-start | bytes 1769480 | tf_op jit(solution)/shard_map/ppermute | solution.py:248
  67.3 6.8 %collective-permute-start.13 = (bf16[1,64,1152]{2,1,0:T(8,128)(2,1)S(1)}, bf16[1,64,1152]{2,1,0:T(8,128)(2,1)S(1)}, u32[]{:S(2)}, u32[]{:S(2)}) collective-permute-start(bf16[1,64,1152]{2,1,0:T(8,128)(2,1)S(1)} %get-tuple-element.41), channel_id=1, source_target_pairs={{0,128},{8,40},{16,144},{24,56},{32,160},{40,8},{48,176},{56,24},{... | collective-permute-start | bytes 442376 | tf_op jit(solution)/shard_map/ppermute | solution.py:248
  67.4 8.0 %collective-permute-start.12 = (bf16[1,64,1152]{2,1,0:T(8,128)(2,1)S(1)}, bf16[1,64,1152]{2,1,0:T(8,128)(2,1)S(1)}, u32[]{:S(2)}, u32[]{:S(2)}) collective-permute-start(bf16[1,64,1152]{2,1,0:T(8,128)(2,1)S(1)} %get-tuple-element.42), channel_id=1, source_target_pairs={{0,64},{8,24},{16,80},{24,40},{32,96},{40,56},{48,112},{56,8},{64,... | collective-permute-start | bytes 442376 | tf_op jit(solution)/shard_map/ppermute | solution.py:248
  67.5 7.9 %collective-permute-start.11 = (bf16[1,64,1152]{2,1,0:T(8,128)(2,1)S(1)}, bf16[1,64,1152]{2,1,0:T(8,128)(2,1)S(1)}, u32[]{:S(2)}, u32[]{:S(2)}) collective-permute-start(bf16[1,64,1152]{2,1,0:T(8,128)(2,1)S(1)} %get-tuple-element.43), channel_id=1, source_target_pairs={{0,192},{8,56},{16,208},{24,8},{32,224},{40,24},{48,240},{56,40},{... | collective-permute-start | bytes 442376 | tf_op jit(solution)/shard_map/ppermute | solution.py:248
  (1 other events, 0.7 us)

commit v3 on v2

--- a/solution.py
+++ b/solution.py
@@ -16,6 +16,7 @@
 HOPS = (0, 1, 3, 2)
 very_low = -1e30
 log2_scale = math.log2(math.e) / math.sqrt(HD)
+CHUNKS = 2
 VMEM_BYTES = 24 * 1024 * 1024
 
 
@@ -29,13 +30,19 @@
     return jnp.concatenate([rows[:, g * HD : (g + 1) * HD] for g in range(heads)], axis=0)
 
 
-def pack_kernel(cite_ref, query_ref, picks_ref, out_ref, sem):
+def pack_kernel(cite_ref, query_ref, picks_ref, out_ref, cite_s, picks_s, sems):
     suffix_len, width = query_ref.shape
     cites, pick_count = picks_ref.shape
     blocks = width // LANES
-    copy = pltpu.make_async_copy(query_ref, out_ref.at[pl.ds(0, suffix_len), :], sem)
-    copy.start()
-    picks = jnp.concatenate([picks_ref[c : c + 1, :] for c in range(cites)], axis=1)
+    copies = (
+        pltpu.make_async_copy(picks_ref, picks_s, sems.at[0]),
+        pltpu.make_async_copy(cite_ref, cite_s, sems.at[1]),
+        pltpu.make_async_copy(query_ref, out_ref.at[pl.ds(0, suffix_len), :], sems.at[2]),
+    )
+    for copy in copies:
+        copy.start()
+    copies[0].wait()
+    picks = jnp.concatenate([picks_s[c : c + 1, :] for c in range(cites)], axis=1)
     total = cites * pick_count
     within = lax.broadcasted_iota(jnp.int32, (LANES, total), 0)
     low = jnp.where(within == picks % LANES, 1.0, 0.0).astype(jnp.bfloat16)
@@ -43,15 +50,16 @@
     owner = lax.broadcasted_iota(jnp.int32, (blocks * cites, total), 1) // pick_count
     high = jnp.where(row == (picks // LANES) * cites + owner, 1.0, 0.0).astype(jnp.bfloat16)
     hits = contract_last(high, low)
+    copies[1].wait()
     line = lax.broadcasted_iota(jnp.int32, (cites, LANES), 0)
     ids = jnp.zeros((cites, LANES), jnp.int32)
     for c in range(cites):
-        ids = jnp.where(line == c, cite_ref[0, c], ids)
+        ids = jnp.where(line == c, cite_s[0, c], ids)
     ids = ids.astype(jnp.float32)
     for h in range(blocks):
         hit = hits[h * cites : (h + 1) * cites, :]
         out_ref[suffix_len:, h * LANES : (h + 1) * LANES] = jnp.where(hit > 0.5, -1.0 - ids, ids).astype(jnp.bfloat16)
-    copy.wait()
+    copies[2].wait()
 
 
 def row_kernel(*refs):
@@ -63,21 +71,58 @@
     tables, blocks = refs[0:count], refs[count : 2 * count]
     own_key, own_value, other_key, other_value = refs[2 * count : 2 * count + 4]
     outs = refs[2 * count + 4 : 3 * count + 4]
-    mask_s, query_s, max_s, acc_s = refs[3 * count + 4 :]
+    mask_s, query_s, max_s, acc_s, key_s, value_s, order_s, sems = refs[3 * count + 4 :]
     rows = suffix_len * heads
-    chunk = rows // 2
+    chunk = rows // CHUNKS
     requests = blocks[0].shape[0]
     local = own_key.shape[0]
 
-    def add_slot(key_ref, value_ref, place, bias):
-        for start in range(0, rows, chunk):
-            part = pl.ds(start, chunk)
-            scores = contract_last(query_s[part, :], key_ref[place]) * log2_scale + bias
+    limit = count * requests * cites
+    total = jnp.int32(0)
+    for table_ref in tables:
+        for i in range(requests * cites):
+            place = table_ref[i // cites, i % cites]
+            order_s[total] = place
+            total = total + jnp.where(place >= 0, 1, 0)
+
+    def copies(place, slot, key_ref, value_ref):
+        return (
+            pltpu.make_async_copy(key_ref.at[place], key_s.at[slot], sems.at[0, slot]),
+            pltpu.make_async_copy(value_ref.at[place], value_s.at[slot], sems.at[1, slot]),
+        )
+
+    def fetch(i):
+        place, slot = order_s[i], i % 2
+
+        @pl.when(place < local)
+        def _():
+            for copy in copies(place, slot, own_key, own_value):
+                copy.start()
+
+        @pl.when(place >= local)
+        def _():
+            for copy in copies(place - local, slot, other_key, other_value):
+                copy.start()
+
+    @pl.when(total > 0)
+    def _():
+        fetch(0)
+
+    order_s[limit] = 0
+
+    def add_slot(slot, bias):
+        parts = [pl.ds(start, chunk) for start in range(0, rows, chunk)]
+        ahead = contract_last(query_s[parts[0], :], key_s[slot])
+        for i, part in enumerate(parts):
+            scores = ahead * log2_scale + bias
+            if i + 1 < len(parts):
+                ahead = contract_last(query_s[parts[i + 1], :], key_s[slot])
             old_max = max_s[part, :]
             new_max = jnp.maximum(old_max, jnp.max(scores, axis=1, keepdims=True))
-            weights = jnp.exp2(scores - new_max[:, 0:1]).astype(jnp.bfloat16)
+            level = jnp.concatenate([new_max] * (scores.shape[1] // LANES), axis=1)
+            weights = jnp.exp2(scores - level).astype(jnp.bfloat16)
             factor = jnp.exp2(old_max - new_max)
-            value = value_ref[place]
+            value = value_s[slot]
             value = jnp.concatenate([value, jnp.ones_like(value)], axis=1)
             added = jnp.dot(weights, value, preferred_element_type=jnp.float32)
             acc_s[part, :] = acc_s[part, :] * jnp.concatenate([factor, factor], axis=1) + added
@@ -85,7 +130,7 @@
 
     for table_ref, packed_ref, out_ref in zip(tables, blocks, outs):
 
-        def one_request(j, carry):
+        def one_request(j, carry, table_ref=table_ref, packed_ref=packed_ref, out_ref=out_ref):
             found = table_ref[j, 0]
             for c in range(1, cites):
                 found = jnp.maximum(found, table_ref[j, c])
@@ -99,15 +144,18 @@
                 acc_s[...] = jnp.zeros_like(acc_s)
 
                 def one_cite(c, inner):
-                    place = table_ref[j, c]
-
-                    @pl.when((place >= 0) & (place < local))
+                    @pl.when(table_ref[j, c] >= 0)
                     def _():
-                        add_slot(own_key, own_value, place, mask_s[pl.ds(c, 1), :])
-
-                    @pl.when(place >= local)
-                    def _():
-                        add_slot(other_key, other_value, place - local, mask_s[pl.ds(c, 1), :])
+                        i = order_s[limit]
+                        order_s[limit] = i + 1
+                        for copy in copies(0, i % 2, own_key, own_value):
+                            copy.wait()
+
+                        @pl.when(i + 1 < total)
+                        def _():
+                            fetch(i + 1)
+
+                        add_slot(i % 2, mask_s[pl.ds(c, 1), :])
 
                     return inner
 
@@ -116,9 +164,9 @@
                 stats = jnp.zeros((suffix_len, LANES), jnp.float32)
                 for g in range(heads):
                     part = slice(g * suffix_len, (g + 1) * suffix_len)
-                    total = acc_s[part, HD : 2 * HD]
-                    out_ref[j, :, g * HD : (g + 1) * HD] = (acc_s[part, 0:HD] / total).astype(jnp.bfloat16)
-                    stats = jnp.where(lane % heads == g, max_s[part, :] + jnp.log2(total), stats)
+                    total_weight = acc_s[part, HD : 2 * HD]
+                    out_ref[j, :, g * HD : (g + 1) * HD] = (acc_s[part, 0:HD] / total_weight).astype(jnp.bfloat16)
+                    stats = jnp.where(lane % heads == g, max_s[part, :] + jnp.log2(total_weight), stats)
                 out_ref[j, :, heads * HD :] = split_level(stats, lane, heads).astype(jnp.bfloat16)
 
             @pl.when(found < 0)
@@ -181,12 +229,22 @@
     return [share / total for share in shares], top + jnp.log2(total)
 
 
+def spread_parts(level, lane, heads):
+    wide = level
+    for i in range(1, PARTS):
+        wide = jnp.where(lane // heads == i, pltpu.roll(level, i * heads, 1), wide)
+    return split_level(wide, lane, heads).astype(jnp.bfloat16)
+
+
 def merge_kernel(*refs, packed, wide, wide_out):
     heads = refs[0].shape[-1] // HD - (1 if packed else 0)
     width = heads * HD
     outs = refs[packed + 2 * wide :]
     requests, suffix_len = outs[0].shape[:2]
     lane = lax.broadcasted_iota(jnp.int32, (suffix_len, LANES), 1)
+    part = lax.broadcasted_iota(jnp.int32, (LANES, width), 0)
+    head = lax.broadcasted_iota(jnp.int32, (LANES, width), 1) // HD
+    widen = jnp.where((part % heads == head) & (part < PARTS * heads), 1.0, 0.0).astype(jnp.bfloat16)
     for j in range(requests):
         bodies = [refs[i] for i in range(packed)] + [refs[packed + 2 * i] for i in range(wide)]
         levels = [get_level(refs[i][j, :, width:], heads) for i in range(packed)]
@@ -195,18 +253,16 @@
         shares = [jnp.exp2(level - top) for level in levels]
         total = functools.reduce(jnp.add, shares)
         shares = [share / total for share in shares]
-        for g in range(heads):
-            part = slice(g * HD, (g + 1) * HD)
-            terms = [b[j, :, part].astype(jnp.float32) * w[:, g : g + 1] for b, w in zip(bodies, shares)]
-            outs[0][j, :, part] = functools.reduce(jnp.add, terms).astype(outs[0].dtype)
+        terms = [
+            b[j, :, 0:width].astype(jnp.float32) * jnp.dot(spread_parts(w, lane, heads), widen, preferred_element_type=jnp.float32)
+            for b, w in zip(bodies, shares)
+        ]
+        outs[0][j, :, 0:width] = functools.reduce(jnp.add, terms).astype(outs[0].dtype)
         level = top + jnp.log2(total)
         if wide_out:
             outs[1][j] = level
         elif outs[0].shape[-1] > width:
-            spread = level
-            for i in range(1, PARTS):
-                spread = jnp.where(lane // heads == i, pltpu.roll(level, i * heads, 1), spread)
-            outs[0][j, :, width:] = split_level(spread, lane, heads).astype(jnp.bfloat16)
+            outs[0][j, :, width:] = spread_parts(level, lane, heads)
 
 
 def merge_call(packed, wide, out_shape, name):
@@ -251,6 +307,7 @@
 def attend_call(tables, blocks, caches):
     requests, packed_len, width = blocks[0].shape
     cites = tables[0].shape[1]
+    length = caches[0].shape[1]
     suffix_len, heads = packed_len - cites, width // HD
     rows = suffix_len * heads
     count = len(blocks)
@@ -258,16 +315,22 @@
     return in_vmem(
         functools.partial(attend_kernel, count=count, suffix_len=suffix_len, heads=heads, cites=cites),
         (out,) * count,
-        (*tables, *blocks, *caches),
+        (*tables, *blocks, *(pltpu.with_memory_space_constraint(v, pltpu.HBM) for v in caches)),
         scratch=(
-            pltpu.VMEM((cites, caches[0].shape[1]), jnp.float32),
+            pltpu.VMEM((cites, length), jnp.float32),
             pltpu.VMEM((rows, HD), jnp.bfloat16),
             pltpu.VMEM((rows, LANES), jnp.float32),
             pltpu.VMEM((rows, 2 * HD), jnp.float32),
-        ),
-        smem=count,
+            pltpu.VMEM((2, length, HD), jnp.bfloat16),
+            pltpu.VMEM((2, length, HD), jnp.bfloat16),
+            pltpu.SMEM((count * requests * cites + 1,), jnp.int32),
+            pltpu.SemaphoreType.DMA((2, 2)),
+        ),
+        spaces=(pltpu.SMEM,) * count + (pltpu.VMEM,) * count + (pltpu.HBM,) * len(caches),
         cost=pl.CostEstimate(
-            flops=count * requests * cites * rows * HD * 1024, transcendentals=0, bytes_accessed=count * 16 * 1024 * 1024
+            flops=count * requests * cites * rows * HD * length,
+            transcendentals=0,
+            bytes_accessed=count * 16 * 1024 * 1024,
         ),
         name="attend_class",
     )
@@ -294,9 +357,13 @@
     packed = in_vmem(
         pack_kernel,
         jax.ShapeDtypeStruct((suffix_len + cites, width), jnp.bfloat16),
-        (citations, queries[0], selected[0]),
-        scratch=(pltpu.SemaphoreType.DMA,),
-        spaces=(pltpu.SMEM, pl.ANY, pltpu.VMEM),
+        tuple(pltpu.with_memory_space_constraint(v, pltpu.HBM) for v in (citations, queries[0], selected[0])),
+        scratch=(
+            pltpu.SMEM(citations.shape, jnp.int32),
+            pltpu.VMEM(selected.shape[1:], jnp.int32),
+            pltpu.SemaphoreType.DMA((3,)),
+        ),
+        spaces=(pltpu.HBM,) * 3,
         name="pack",
     )
     packed, passage_keys, passage_values = lax.optimization_barrier((packed, passage_keys, passage_values))
@@ -339,12 +406,10 @@
     def attend(blocks):
         return attend_call([places(b) for b in blocks], blocks, (passage_keys, passage_values, other_keys, other_values))
 
-    own = attend(classes[0:1])
-    near_blocks, own = lax.optimization_barrier((classes[1:3], own))
-    near = attend(near_blocks)
-    far_block, near = lax.optimization_barrier((classes[3:4], near))
-    far = attend(far_block)
-    results = list(own) + list(near) + list(far)
+    results = [attend(classes[0:1])[0]]
+    for block in classes[1:]:
+        block, results[-1] = lax.optimization_barrier((block, results[-1]))
+        results.append(attend([block])[0])
     back = [shift(r, False, RING - hop) for r, hop in zip(results[1:], HOPS[1:])]
     partial = merge_call(
         (results[0], *back[:2]),

time: 93.7 us -> 87.6 us (0.935)
  the two profiles are of different devices: /device:TPU:24 before, /device:TPU:16 now
where the time goes in v3:
time: 87.6 us; the launch traced here: 88.2 us
  waiting for transfers between devices  25.7 us (29%)
  starting transfers between devices  21.9 us (25%)
  Pallas kernels  18.8 us (21%)
  blocking collectives  17.3 us (20%)
  local copies, waits for them, and re-layouts  3.56 us (4%)
    ppermute x12, waiting for transfers between devices, shift(): return lax.ppermute(value, ('x', 'y', 'c'), pairs)  25.7 us
    ppermute x12, starting transfers between devices, shift(): return lax.ppermute(value, ('x', 'y', 'c'), pairs)  21.3 us
    pallas_call x10, Pallas kernels, in_vmem(): pl.pallas_call(kernel, out_shape=out_shape, in_specs=[pl.BlockSpec(memory...  18.8 us
    all_to_all x1, blocking collectives, body(): lax.all_to_all(pieces, 'kv', split_axis=0, concat_axis=0, tiled=True)  17.3 us
    unnamed x13, local copies, waits for them, and re-layouts  3.51 us
  transfers between devices with their start and end apart: 14, of which 6 were waited for; matrix products, arithmetic and copies ran while one was open for 1% of the time, Pallas kernels for 19%

profile of v3, /device:TPU:16, one launch (start us, length us, event | category | flops | bytes accessed | tf_op | source)
XLA Modules:
  0.0 88.2 jit_solution(853630682361750478)
XLA Ops:
  0.0 1.0 %pack.1.refs_0_ = bf16[72,1024]{1,0:T(8,128)(2,1)S(1)} custom-call(s32[1,8]{1,0:T(1,128)} %cite_ref.1, bf16[64,1024]{1,0:T(8,128)(2,1)} %bitcast.12, s32[8,128]{1,0:T(8,128)} %bitcast.22), custom_call_target="tpu_custom_call" | custom-call | tf_op jit(solution)/shard_map/pack/pallas_call | solution.py:281
  1.6 3.0 %collective-permute-start.2 = (bf16[72,1024]{1,0:T(8,128)(2,1)S(1)}, bf16[72,1024]{1,0:T(8,128)(2,1)S(1)}, u32[]{:S(2)}, u32[]{:S(2)}) collective-permute-start(bf16[72,1024]{1,0:T(8,128)(2,1)S(1)} %pack.1.refs_0_), channel_id=1, source_target_pairs={{0,128},{8,40},{16,144},{24,56},{32,160},{40,8},{48,176},{56,24},{... | collective-permute-start | bytes 442376 | tf_op jit(solution)/shard_map/ppermute | solution.py:304
  4.7 1.1 %collective-permute-start.1 = (bf16[72,1024]{1,0:T(8,128)(2,1)S(1)}, bf16[72,1024]{1,0:T(8,128)(2,1)S(1)}, u32[]{:S(2)}, u32[]{:S(2)}) collective-permute-start(bf16[72,1024]{1,0:T(8,128)(2,1)S(1)} %pack.1.refs_0_), channel_id=1, source_target_pairs={{0,192},{8,56},{16,208},{24,8},{32,224},{40,24},{48,240},{56,40},{... | collective-permute-start | bytes 442376 | tf_op jit(solution)/shard_map/ppermute | solution.py:304
  6.7 0.9 %copy-done.1 = bf16[1,8,128,128]{3,2,1,0:T(8,128)(2,1)S(1)} copy-done((bf16[1,8,128,128]{3,2,1,0:T(8,128)(2,1)S(1)}, bf16[1,8,128,128]{3,2,1,0:T(8,128)(2,1)}, u32[]{:S(2)}) %copy-start.1) | copy-done | bytes 262168
  7.6 0.9 %copy-done.2 = bf16[1,8,128,128]{3,2,1,0:T(8,128)(2,1)S(1)} copy-done((bf16[1,8,128,128]{3,2,1,0:T(8,128)(2,1)S(1)}, bf16[1,8,128,128]{3,2,1,0:T(8,128)(2,1)}, u32[]{:S(2)}) %copy-start.2) | copy-done | bytes 262168
  8.6 1.4 %host_part.1 = (f32[64,1024]{1,0:T(8,128)S(1)}, f32[64,128]{1,0:T(8,128)S(1)}) custom-call(bf16[64,1024]{1,0:T(8,128)(2,1)S(1)} %bitcast.13, bf16[1024,128]{1,0:T(8,128)(2,1)S(1)} %bitcast.15, bf16[1024,128]{1,0:T(8,128)(2,1)S(1)} %bitcast.16, bf16[64,128]{1,0:T(8,128)(2,1)S(1)} %bitcast.19, bf16[64,128]{1,0:T(8,128)(2,1)S(1)} %bitcast.20), custom_call_target="tpu_custom_call" | custom-call | tf_op jit(solution)/shard_map/host_part/pallas_call | solution.py:281
  10.1 2.1 %collective-permute-done.refs_1_ = bf16[72,1024]{1,0:T(8,128)(2,1)S(1)} collective-permute-done((bf16[72,1024]{1,0:T(8,128)(2,1)S(1)}, bf16[72,1024]{1,0:T(8,128)(2,1)S(1)}, u32[]{:S(2)}, u32[]{:S(2)}) %collective-permute-start) | collective-permute-done | bytes 147488 | tf_op jit(solution)/shard_map/ppermute | solution.py:304
  12.2 1.4 %collective-permute-start.5 = (bf16[4,72,1024]{2,1,0:T(8,128)(2,1)S(1)}, bf16[4,72,1024]{2,1,0:T(8,128)(2,1)S(1)}, u32[]{:S(2)}, u32[]{:S(2)}) collective-permute-start(bf16[4,72,1024]{2,1,0:T(8,128)(2,1)S(1)} %row.1.refs_1_), channel_id=1, source_target_pairs={{0,16},{8,72},{16,32},{24,88},{32,48},{40,104},{48,0},{56,120},{64... | collective-permute-start | bytes 1769480 | tf_op jit(solution)/shard_map/ppermute | solution.py:304
  14.3 1.5 %collective-permute-start.3 = (bf16[4,72,1024]{2,1,0:T(8,128)(2,1)S(1)}, bf16[4,72,1024]{2,1,0:T(8,128)(2,1)S(1)}, u32[]{:S(2)}, u32[]{:S(2)}) collective-permute-start(bf16[4,72,1024]{2,1,0:T(8,128)(2,1)S(1)} %row.1.refs_1_), channel_id=1, source_target_pairs={{0,32},{8,136},{16,48},{24,152},{32,0},{40,168},{48,16},{56,184},{... | collective-permute-start | bytes 1769480 | tf_op jit(solution)/shard_map/ppermute | solution.py:304
  16.0 1.0 %copy-done.5 = bf16[4,1024,128]{2,1,0:T(8,128)(2,1)} copy-done((bf16[4,1024,128]{2,1,0:T(8,128)(2,1)}, bf16[4,1024,128]{2,1,0:T(8,128)(2,1)S(1)}, u32[]{:S(2)}) %copy-start.5) | copy-done | bytes 1048600
  17.0 2.9 %attend_class.4.refs_0_ = bf16[4,64,1152]{2,1,0:T(8,128)(2,1)S(1)} custom-call(s32[4,8]{1,0:T(4,128)S(1)} %fusion.1.refs_0_, bf16[4,72,1024]{2,1,0:T(8,128)(2,1)S(1)} %row.1.refs_1_, bf16[4,1024,128]{2,1,0:T(8,128)(2,1)} %refs_2_.3, bf16[4,1024,128]{2,1,0:T(8,128)(2,1)} %refs_3_.3, bf16[4,1024,128]{2,1,0:T(8,128)(2,1)} %copy-done.5, ...), custom_call_target="tpu_custom_call" | custom-call | flops 2147483648 | bytes 16777216 | tf_op jit(solution)/shard_map/attend_class/pallas_call | solution.py:281
  19.9 8.6 %collective-permute-done.5.refs_1_ = bf16[4,72,1024]{2,1,0:T(8,128)(2,1)S(1)} collective-permute-done((bf16[4,72,1024]{2,1,0:T(8,128)(2,1)S(1)}, bf16[4,72,1024]{2,1,0:T(8,128)(2,1)S(1)}, u32[]{:S(2)}, u32[]{:S(2)}) %collective-permute-start.5) | collective-permute-done | bytes 589856 | tf_op jit(solution)/shard_map/ppermute | solution.py:304
  28.6 2.8 %attend_class.5 = bf16[4,64,1152]{2,1,0:T(8,128)(2,1)S(1)} custom-call(s32[4,8]{1,0:T(4,128)S(1)} %fusion.3.refs_0_, bf16[4,72,1024]{2,1,0:T(8,128)(2,1)S(1)} %collective-permute-done.5.refs_1_, bf16[4,1024,128]{2,1,0:T(8,128)(2,1)} %refs_2_.3, bf16[4,1024,128]{2,1,0:T(8,128)(2,1)} %refs_3_.3, bf16[4,1024,128]{2,1,0:T(8,128)(2,1)} %copy-done.5, ...), custom_call_target="tpu_custom_call" | custom-call | flops 2147483648 | bytes 16777216 | tf_op jit(solution)/shard_map/attend_class/pallas_call | solution.py:281
  31.7 2.9 %attend_class.6 = bf16[4,64,1152]{2,1,0:T(8,128)(2,1)S(1)} custom-call(s32[4,8]{1,0:T(4,128)S(1)} %fusion.5.refs_0_, bf16[4,72,1024]{2,1,0:T(8,128)(2,1)S(1)} %collective-permute-done.4.refs_1_, bf16[4,1024,128]{2,1,0:T(8,128)(2,1)} %refs_2_.3, bf16[4,1024,128]{2,1,0:T(8,128)(2,1)} %refs_3_.3, bf16[4,1024,128]{2,1,0:T(8,128)(2,1)} %copy-done.5, ...), custom_call_target="tpu_custom_call" | custom-call | flops 2147483648 | bytes 16777216 | tf_op jit(solution)/shard_map/attend_class/pallas_call | solution.py:281
  34.9 2.0 %collective-permute-start.9 = (bf16[4,64,1152]{2,1,0:T(8,128)(2,1)S(1)}, bf16[4,64,1152]{2,1,0:T(8,128)(2,1)S(1)}, u32[]{:S(2)}, u32[]{:S(2)}) collective-permute-start(bf16[4,64,1152]{2,1,0:T(8,128)(2,1)S(1)} %attend_class.5), channel_id=1, source_target_pairs={{0,48},{8,200},{16,0},{24,216},{32,16},{40,232},{48,32},{56,248},{... | collective-permute-start | bytes 1769480 | tf_op jit(solution)/shard_map/ppermute | solution.py:304
  36.9 5.3 %attend_class.7 = bf16[4,64,1152]{2,1,0:T(8,128)(2,1)S(1)} custom-call(s32[4,8]{1,0:T(4,128)S(1)} %fusion.7.refs_0_, bf16[4,72,1024]{2,1,0:T(8,128)(2,1)S(1)} %collective-permute-done.3.refs_1_, bf16[4,1024,128]{2,1,0:T(8,128)(2,1)} %refs_2_.3, bf16[4,1024,128]{2,1,0:T(8,128)(2,1)} %refs_3_.3, bf16[4,1024,128]{2,1,0:T(8,128)(2,1)} %copy-done.5, ...), custom_call_target="tpu_custom_call" | custom-call | flops 2147483648 | bytes 16777216 | tf_op jit(solution)/shard_map/attend_class/pallas_call | solution.py:281
  42.3 2.4 %collective-permute-done.10.refs_2_ = bf16[4,64,1152]{2,1,0:T(8,128)(2,1)S(1)} collective-permute-done((bf16[4,64,1152]{2,1,0:T(8,128)(2,1)S(1)}, bf16[4,64,1152]{2,1,0:T(8,128)(2,1)S(1)}, u32[]{:S(2)}, u32[]{:S(2)}) %collective-permute-start.10) | collective-permute-done | bytes 589856 | tf_op jit(solution)/shard_map/ppermute | solution.py:304
  44.7 5.9 %collective-permute-done.9.refs_1_ = bf16[4,64,1152]{2,1,0:T(8,128)(2,1)S(1)} collective-permute-done((bf16[4,64,1152]{2,1,0:T(8,128)(2,1)S(1)}, bf16[4,64,1152]{2,1,0:T(8,128)(2,1)S(1)}, u32[]{:S(2)}, u32[]{:S(2)}) %collective-permute-start.9) | collective-permute-done | bytes 589856 | tf_op jit(solution)/shard_map/ppermute | solution.py:304
  50.6 1.0 %merge_near.1 = (f32[4,64,1024]{2,1,0:T(8,128)S(1)}, f32[4,64,128]{2,1,0:T(8,128)S(1)}) custom-call(bf16[4,64,1152]{2,1,0:T(8,128)(2,1)S(1)} %attend_class.4.refs_0_, bf16[4,64,1152]{2,1,0:T(8,128)(2,1)S(1)} %collective-permute-done.9.refs_1_, bf16[4,64,1152]{2,1,0:T(8,128)(2,1)S(1)} %collective-permute-done.10.refs_2_), custom_call_target="tpu_custom_call" | custom-call | tf_op jit(solution)/shard_map/merge_near/pallas_call | solution.py:281
  51.6 3.6 %collective-permute-done.8.refs_0_ = bf16[4,64,1152]{2,1,0:T(8,128)(2,1)S(1)} collective-permute-done((bf16[4,64,1152]{2,1,0:T(8,128)(2,1)S(1)}, bf16[4,64,1152]{2,1,0:T(8,128)(2,1)S(1)}, u32[]{:S(2)}, u32[]{:S(2)}) %collective-permute-start.8) | collective-permute-done | bytes 589856 | tf_op jit(solution)/shard_map/ppermute | solution.py:304
  56.1 7.2 %collective-permute-start.13 = (bf16[1,64,1152]{2,1,0:T(8,128)(2,1)S(1)}, bf16[1,64,1152]{2,1,0:T(8,128)(2,1)S(1)}, u32[]{:S(2)}, u32[]{:S(2)}) collective-permute-start(bf16[1,64,1152]{2,1,0:T(8,128)(2,1)S(1)} %get-tuple-element.37), channel_id=1, source_target_pairs={{0,128},{8,40},{16,144},{24,56},{32,160},{40,8},{48,176},{56,24},{... | collective-permute-start | bytes 442376 | tf_op jit(solution)/shard_map/ppermute | solution.py:304
  63.3 3.2 %collective-permute-start.11 = (bf16[1,64,1152]{2,1,0:T(8,128)(2,1)S(1)}, bf16[1,64,1152]{2,1,0:T(8,128)(2,1)S(1)}, u32[]{:S(2)}, u32[]{:S(2)}) collective-permute-start(bf16[1,64,1152]{2,1,0:T(8,128)(2,1)S(1)} %get-tuple-element.39), channel_id=1, source_target_pairs={{0,192},{8,56},{16,208},{24,8},{32,224},{40,24},{48,240},{56,40},{... | collective-permute-start | bytes 442376 | tf_op jit(solution)/shard_map/ppermute | solution.py:304
  66.6 3.1 %collective-permute-done.12.refs_2_ = bf16[1,64,1152]{2,1,0:T(8,128)(2,1)S(1)} collective-permute-done((bf16[1,64,1152]{2,1,0:T(8,128)(2,1)S(1)}, bf16[1,64,1152]{2,1,0:T(8,128)(2,1)S(1)}, u32[]{:S(2)}, u32[]{:S(2)}) %collective-permute-start.12) | collective-permute-done | bytes 147488 | tf_op jit(solution)/shard_map/ppermute | solution.py:304
  70.2 17.3 %all_to_all.5 = bf16[8,8,1024]{2,1,0:T(8,128)(2,1)S(1)} all-to-all(bf16[8,8,1024]{2,1,0:T(8,128)(2,1)S(1)} %bitcast.14), channel_id=1, replica_groups=mesh['x'=4,'y'=4,'c'=2,'kv'=8] {'kv'}, dimensions={0} | all-to-all | bytes 262144 | tf_op jit(solution)/shard_map/all_to_all | solution.py:436
  (37 shorter events, 5.1 us)
Async XLA Ops:
  0.0 6.7 %copy-start = (bf16[1,64,1024]{2,1,0:T(8,128)(2,1)S(1)}, bf16[1,64,1024]{2,1,0:T(8,128)(2,1)}, u32[]{:S(2)}) copy-start(bf16[1,64,1024]{2,1,0:T(8,128)(2,1)} %param.9) | copy-start | bytes 393220
  0.0 6.7 %copy-start.3 = (bf16[1,64,128]{2,1,0:T(8,128)(2,1)S(1)}, bf16[1,64,128]{2,1,0:T(8,128)(2,1)}, u32[]{:S(2)}) copy-start(bf16[1,64,128]{2,1,0:T(8,128)(2,1)} %param.10) | copy-start | bytes 49156
  0.0 6.7 %copy-start.4 = (bf16[1,64,128]{2,1,0:T(8,128)(2,1)S(1)}, bf16[1,64,128]{2,1,0:T(8,128)(2,1)}, u32[]{:S(2)}) copy-start(bf16[1,64,128]{2,1,0:T(8,128)(2,1)} %param.11) | copy-start | bytes 49156
  1.0 15.0 %collective-permute-start.6 = (bf16[4,1024,128]{2,1,0:T(8,128)(2,1)}, bf16[4,1024,128]{2,1,0:T(8,128)(2,1)S(1)}, u32[]{:S(2)}, u32[]{:S(2)}) collective-permute-start(bf16[4,1024,128]{2,1,0:T(8,128)(2,1)} %refs_2_.3), channel_id=1, source_target_pairs={{0,8},{8,0},{1,9},{9,1},{2,10},{10,2},{3,11},{11,3},{4,12},{12,4},... | collective-permute-start | bytes 3145736 | tf_op jit(solution)/shard_map/ppermute | solution.py:371
  1.1 14.9 %collective-permute-start.7 = (bf16[4,1024,128]{2,1,0:T(8,128)(2,1)}, bf16[4,1024,128]{2,1,0:T(8,128)(2,1)}, u32[]{:S(2)}, u32[]{:S(2)}) collective-permute-start(bf16[4,1024,128]{2,1,0:T(8,128)(2,1)} %refs_3_.3), channel_id=1, source_target_pairs={{0,8},{8,0},{1,9},{9,1},{2,10},{10,2},{3,11},{11,3},{4,12},{12,4},... | collective-permute-start | bytes 3145736 | tf_op jit(solution)/shard_map/ppermute | solution.py:372
  1.6 8.4 %collective-permute-start.2 = (bf16[72,1024]{1,0:T(8,128)(2,1)S(1)}, bf16[72,1024]{1,0:T(8,128)(2,1)S(1)}, u32[]{:S(2)}, u32[]{:S(2)}) collective-permute-start(bf16[72,1024]{1,0:T(8,128)(2,1)S(1)} %pack.1.refs_0_), channel_id=1, source_target_pairs={{0,128},{8,40},{16,144},{24,56},{32,160},{40,8},{48,176},{56,24},{... | collective-permute-start | bytes 442376 | tf_op jit(solution)/shard_map/ppermute | solution.py:304
  4.7 5.4 %collective-permute-start.1 = (bf16[72,1024]{1,0:T(8,128)(2,1)S(1)}, bf16[72,1024]{1,0:T(8,128)(2,1)S(1)}, u32[]{:S(2)}, u32[]{:S(2)}) collective-permute-start(bf16[72,1024]{1,0:T(8,128)(2,1)S(1)} %pack.1.refs_0_), channel_id=1, source_target_pairs={{0,192},{8,56},{16,208},{24,8},{32,224},{40,24},{48,240},{56,40},{... | collective-permute-start | bytes 442376 | tf_op jit(solution)/shard_map/ppermute | solution.py:304
  5.8 6.4 %collective-permute-start = (bf16[72,1024]{1,0:T(8,128)(2,1)S(1)}, bf16[72,1024]{1,0:T(8,128)(2,1)S(1)}, u32[]{:S(2)}, u32[]{:S(2)}) collective-permute-start(bf16[72,1024]{1,0:T(8,128)(2,1)S(1)} %pack.1.refs_0_), channel_id=1, source_target_pairs={{0,64},{8,24},{16,80},{24,40},{32,96},{40,56},{48,112},{56,8},{64,... | collective-permute-start | bytes 442376 | tf_op jit(solution)/shard_map/ppermute | solution.py:304
  6.7 1.0 %copy-start.1 = (bf16[1,8,128,128]{3,2,1,0:T(8,128)(2,1)S(1)}, bf16[1,8,128,128]{3,2,1,0:T(8,128)(2,1)}, u32[]{:S(2)}) copy-start(bf16[1,8,128,128]{3,2,1,0:T(8,128)(2,1)} %param.14) | copy-start | bytes 786436
  7.6 0.9 %copy-start.2 = (bf16[1,8,128,128]{3,2,1,0:T(8,128)(2,1)S(1)}, bf16[1,8,128,128]{3,2,1,0:T(8,128)(2,1)}, u32[]{:S(2)}) copy-start(bf16[1,8,128,128]{3,2,1,0:T(8,128)(2,1)} %param.15) | copy-start | bytes 786436
  12.2 16.3 %collective-permute-start.5 = (bf16[4,72,1024]{2,1,0:T(8,128)(2,1)S(1)}, bf16[4,72,1024]{2,1,0:T(8,128)(2,1)S(1)}, u32[]{:S(2)}, u32[]{:S(2)}) collective-permute-start(bf16[4,72,1024]{2,1,0:T(8,128)(2,1)S(1)} %row.1.refs_1_), channel_id=1, source_target_pairs={{0,16},{8,72},{16,32},{24,88},{32,48},{40,104},{48,0},{56,120},{64... | collective-permute-start | bytes 1769480 | tf_op jit(solution)/shard_map/ppermute | solution.py:304
  13.6 17.9 %collective-permute-start.4 = (bf16[4,72,1024]{2,1,0:T(8,128)(2,1)S(1)}, bf16[4,72,1024]{2,1,0:T(8,128)(2,1)S(1)}, u32[]{:S(2)}, u32[]{:S(2)}) collective-permute-start(bf16[4,72,1024]{2,1,0:T(8,128)(2,1)S(1)} %row.1.refs_1_), channel_id=1, source_target_pairs={{0,48},{8,200},{16,0},{24,216},{32,16},{40,232},{48,32},{56,248},{... | collective-permute-start | bytes 1769480 | tf_op jit(solution)/shard_map/ppermute | solution.py:304
  14.3 20.3 %collective-permute-start.3 = (bf16[4,72,1024]{2,1,0:T(8,128)(2,1)S(1)}, bf16[4,72,1024]{2,1,0:T(8,128)(2,1)S(1)}, u32[]{:S(2)}, u32[]{:S(2)}) collective-permute-start(bf16[4,72,1024]{2,1,0:T(8,128)(2,1)S(1)} %row.1.refs_1_), channel_id=1, source_target_pairs={{0,32},{8,136},{16,48},{24,152},{32,0},{40,168},{48,16},{56,184},{... | collective-permute-start | bytes 1769480 | tf_op jit(solution)/shard_map/ppermute | solution.py:304
  16.0 1.0 %copy-start.5 = (bf16[4,1024,128]{2,1,0:T(8,128)(2,1)}, bf16[4,1024,128]{2,1,0:T(8,128)(2,1)S(1)}, u32[]{:S(2)}) copy-start(bf16[4,1024,128]{2,1,0:T(8,128)(2,1)S(1)} %collective-permute-done.6.refs_4_) | copy-start | bytes 3145732
  34.8 10.0 %collective-permute-start.10 = (bf16[4,64,1152]{2,1,0:T(8,128)(2,1)S(1)}, bf16[4,64,1152]{2,1,0:T(8,128)(2,1)S(1)}, u32[]{:S(2)}, u32[]{:S(2)}) collective-permute-start(bf16[4,64,1152]{2,1,0:T(8,128)(2,1)S(1)} %attend_class.6), channel_id=1, source_target_pairs={{0,16},{8,72},{16,32},{24,88},{32,48},{40,104},{48,0},{56,120},{64... | collective-permute-start | bytes 1769480 | tf_op jit(solution)/shard_map/ppermute | solution.py:304
  34.9 15.8 %collective-permute-start.9 = (bf16[4,64,1152]{2,1,0:T(8,128)(2,1)S(1)}, bf16[4,64,1152]{2,1,0:T(8,128)(2,1)S(1)}, u32[]{:S(2)}, u32[]{:S(2)}) collective-permute-start(bf16[4,64,1152]{2,1,0:T(8,128)(2,1)S(1)} %attend_class.5), channel_id=1, source_target_pairs={{0,48},{8,200},{16,0},{24,216},{32,16},{40,232},{48,32},{56,248},{... | collective-permute-start | bytes 1769480 | tf_op jit(solution)/shard_map/ppermute | solution.py:304
  42.2 13.1 %collective-permute-start.8 = (bf16[4,64,1152]{2,1,0:T(8,128)(2,1)S(1)}, bf16[4,64,1152]{2,1,0:T(8,128)(2,1)S(1)}, u32[]{:S(2)}, u32[]{:S(2)}) collective-permute-start(bf16[4,64,1152]{2,1,0:T(8,128)(2,1)S(1)} %attend_class.7), channel_id=1, source_target_pairs={{0,32},{8,136},{16,48},{24,152},{32,0},{40,168},{48,16},{56,184},{... | collective-permute-start | bytes 1769480 | tf_op jit(solution)/shard_map/ppermute | solution.py:304
  56.1 10.4 %collective-permute-start.13 = (bf16[1,64,1152]{2,1,0:T(8,128)(2,1)S(1)}, bf16[1,64,1152]{2,1,0:T(8,128)(2,1)S(1)}, u32[]{:S(2)}, u32[]{:S(2)}) collective-permute-start(bf16[1,64,1152]{2,1,0:T(8,128)(2,1)S(1)} %get-tuple-element.37), channel_id=1, source_target_pairs={{0,128},{8,40},{16,144},{24,56},{32,160},{40,8},{48,176},{56,24},{... | collective-permute-start | bytes 442376 | tf_op jit(solution)/shard_map/ppermute | solution.py:304
  63.3 6.4 %collective-permute-start.12 = (bf16[1,64,1152]{2,1,0:T(8,128)(2,1)S(1)}, bf16[1,64,1152]{2,1,0:T(8,128)(2,1)S(1)}, u32[]{:S(2)}, u32[]{:S(2)}) collective-permute-start(bf16[1,64,1152]{2,1,0:T(8,128)(2,1)S(1)} %get-tuple-element.38), channel_id=1, source_target_pairs={{0,64},{8,24},{16,80},{24,40},{32,96},{40,56},{48,112},{56,8},{64,... | collective-permute-start | bytes 442376 | tf_op jit(solution)/shard_map/ppermute | solution.py:304
  63.3 6.4 %collective-permute-start.11 = (bf16[1,64,1152]{2,1,0:T(8,128)(2,1)S(1)}, bf16[1,64,1152]{2,1,0:T(8,128)(2,1)S(1)}, u32[]{:S(2)}, u32[]{:S(2)}) collective-permute-start(bf16[1,64,1152]{2,1,0:T(8,128)(2,1)S(1)} %get-tuple-element.39), channel_id=1, source_target_pairs={{0,192},{8,56},{16,208},{24,8},{32,224},{40,24},{48,240},{56,40},{... | collective-permute-start | bytes 442376 | tf_op jit(solution)/shard_map/ppermute | solution.py:304

commit v4 on v3

--- a/solution.py
+++ b/solution.py
@@ -67,117 +67,84 @@
         refs[-1][j, :, :] = source[...]
 
 
-def attend_kernel(*refs, count, suffix_len, heads, cites):
-    tables, blocks = refs[0:count], refs[count : 2 * count]
-    own_key, own_value, other_key, other_value = refs[2 * count : 2 * count + 4]
-    outs = refs[2 * count + 4 : 3 * count + 4]
-    mask_s, query_s, max_s, acc_s, key_s, value_s, order_s, sems = refs[3 * count + 4 :]
+def stage_kernel(own_key, own_value, other_key, other_value, key_ref, value_ref, sems):
+    local = own_key.shape[0]
+    copies = []
+    for i, (source, target, start) in enumerate(
+        ((own_key, key_ref, 0), (own_value, value_ref, 0), (other_key, key_ref, local), (other_value, value_ref, local))
+    ):
+        copies.append(pltpu.make_async_copy(source, target.at[pl.ds(start, local)], sems.at[i]))
+        copies[-1].start()
+    for copy in copies:
+        copy.wait()
+
+
+def attend_kernel(table_ref, packed_ref, key_ref, value_ref, out_ref, mask_s, query_s, max_s, acc_s):
+    requests, suffix_len, wide = out_ref.shape
+    heads = wide // HD - 1
+    cites = packed_ref.shape[1] - suffix_len
     rows = suffix_len * heads
     chunk = rows // CHUNKS
-    requests = blocks[0].shape[0]
-    local = own_key.shape[0]
-
-    limit = count * requests * cites
-    total = jnp.int32(0)
-    for table_ref in tables:
-        for i in range(requests * cites):
-            place = table_ref[i // cites, i % cites]
-            order_s[total] = place
-            total = total + jnp.where(place >= 0, 1, 0)
-
-    def copies(place, slot, key_ref, value_ref):
-        return (
-            pltpu.make_async_copy(key_ref.at[place], key_s.at[slot], sems.at[0, slot]),
-            pltpu.make_async_copy(value_ref.at[place], value_s.at[slot], sems.at[1, slot]),
-        )
-
-    def fetch(i):
-        place, slot = order_s[i], i % 2
-
-        @pl.when(place < local)
-        def _():
-            for copy in copies(place, slot, own_key, own_value):
-                copy.start()
-
-        @pl.when(place >= local)
-        def _():
-            for copy in copies(place - local, slot, other_key, other_value):
-                copy.start()
-
-    @pl.when(total > 0)
-    def _():
-        fetch(0)
-
-    order_s[limit] = 0
-
-    def add_slot(slot, bias):
-        parts = [pl.ds(start, chunk) for start in range(0, rows, chunk)]
-        ahead = contract_last(query_s[parts[0], :], key_s[slot])
+    parts = [pl.ds(start, chunk) for start in range(0, rows, chunk)]
+
+    def add_slot(place, bias):
+        ahead = contract_last(query_s[parts[0], :], key_ref[place])
         for i, part in enumerate(parts):
             scores = ahead * log2_scale + bias
             if i + 1 < len(parts):
-                ahead = contract_last(query_s[parts[i + 1], :], key_s[slot])
+                ahead = contract_last(query_s[parts[i + 1], :], key_ref[place])
             old_max = max_s[part, :]
             new_max = jnp.maximum(old_max, jnp.max(scores, axis=1, keepdims=True))
             level = jnp.concatenate([new_max] * (scores.shape[1] // LANES), axis=1)
             weights = jnp.exp2(scores - level).astype(jnp.bfloat16)
             factor = jnp.exp2(old_max - new_max)
-            value = value_s[slot]
+            value = value_ref[place]
             value = jnp.concatenate([value, jnp.ones_like(value)], axis=1)
             added = jnp.dot(weights, value, preferred_element_type=jnp.float32)
             acc_s[part, :] = acc_s[part, :] * jnp.concatenate([factor, factor], axis=1) + added
             max_s[part, :] = new_max
 
-    for table_ref, packed_ref, out_ref in zip(tables, blocks, outs):
-
-        def one_request(j, carry, table_ref=table_ref, packed_ref=packed_ref, out_ref=out_ref):
-            found = table_ref[j, 0]
-            for c in range(1, cites):
-                found = jnp.maximum(found, table_ref[j, c])
-
-            @pl.when(found >= 0)
-            def _():
-                query_s[...] = stack_heads(packed_ref[j, 0:suffix_len, :], heads)
-                marks = packed_ref[j, suffix_len : suffix_len + cites, :].astype(jnp.float32)
-                mask_s[...] = jnp.where(marks < 0.0, very_low, 0.0)
-                max_s[...] = jnp.full_like(max_s, very_low)
-                acc_s[...] = jnp.zeros_like(acc_s)
-
-                def one_cite(c, inner):
-                    @pl.when(table_ref[j, c] >= 0)
-                    def _():
-                        i = order_s[limit]
-                        order_s[limit] = i + 1
-                        for copy in copies(0, i % 2, own_key, own_value):
-                            copy.wait()
-
-                        @pl.when(i + 1 < total)
-                        def _():
-                            fetch(i + 1)
-
-                        add_slot(i % 2, mask_s[pl.ds(c, 1), :])
-
-                    return inner
-
-                lax.fori_loop(0, cites, one_cite, 0)
-                lane = lax.broadcasted_iota(jnp.int32, (suffix_len, LANES), 1)
-                stats = jnp.zeros((suffix_len, LANES), jnp.float32)
-                for g in range(heads):
-                    part = slice(g * suffix_len, (g + 1) * suffix_len)
-                    total_weight = acc_s[part, HD : 2 * HD]
-                    out_ref[j, :, g * HD : (g + 1) * HD] = (acc_s[part, 0:HD] / total_weight).astype(jnp.bfloat16)
-                    stats = jnp.where(lane % heads == g, max_s[part, :] + jnp.log2(total_weight), stats)
-                out_ref[j, :, heads * HD :] = split_level(stats, lane, heads).astype(jnp.bfloat16)
-
-            @pl.when(found < 0)
-            def _():
-                out_ref[j, :, 0 : heads * HD] = jnp.zeros((suffix_len, heads * HD), jnp.bfloat16)
-                lane = lax.broadcasted_iota(jnp.int32, (suffix_len, LANES), 1)
-                out_ref[j, :, heads * HD :] = jnp.where(lane < heads, very_low, 0.0).astype(jnp.bfloat16)
-
-            return carry
-
-        lax.fori_loop(0, requests, one_request, 0)
+    lane = lax.broadcasted_iota(jnp.int32, (suffix_len, LANES), 1)
+
+    def one_request(j, carry):
+        found = table_ref[j, 0]
+        for c in range(1, cites):
+            found = jnp.maximum(found, table_ref[j, c])
+
+        @pl.when(found >= 0)
+        def _():
+            query_s[...] = stack_heads(packed_ref[j, 0:suffix_len, :], heads)
+            marks = packed_ref[j, suffix_len : suffix_len + cites, :].astype(jnp.float32)
+            mask_s[...] = jnp.where(marks < 0.0, very_low, 0.0)
+            max_s[...] = jnp.full_like(max_s, very_low)
+            acc_s[...] = jnp.zeros_like(acc_s)
+
+            def one_cite(c, inner):
+                place = table_ref[j, c]
+
+                @pl.when(place >= 0)
+                def _():
+                    add_slot(place, mask_s[pl.ds(c, 1), :])
+
+                return inner
+
+            lax.fori_loop(0, cites, one_cite, 0)
+            stats = jnp.zeros((suffix_len, LANES), jnp.float32)
+            for g in range(heads):
+                part = slice(g * suffix_len, (g + 1) * suffix_len)
+                total = acc_s[part, HD : 2 * HD]
+                out_ref[j, :, g * HD : (g + 1) * HD] = (acc_s[part, 0:HD] / total).astype(jnp.bfloat16)
+                stats = jnp.where(lane % heads == g, max_s[part, :] + jnp.log2(total), stats)
+            out_ref[j, :, heads * HD :] = split_level(stats, lane, heads).astype(jnp.bfloat16)
+
+        @pl.when(found < 0)
+        def _():
+            out_ref[j, :, 0 : heads * HD] = jnp.zeros((suffix_len, heads * HD), jnp.bfloat16)
+            out_ref[j, :, heads * HD :] = jnp.where(lane < heads, very_low, 0.0).astype(jnp.bfloat16)
+
+        return carry
+
+    lax.fori_loop(0, requests, one_request, 0)
 
 
 def split_level(level, lane, heads):
@@ -304,33 +271,25 @@
     return lax.ppermute(value, ("x", "y", "c"), pairs)
 
 
-def attend_call(tables, blocks, caches):
-    requests, packed_len, width = blocks[0].shape
-    cites = tables[0].shape[1]
-    length = caches[0].shape[1]
+def attend_call(table, block, keys, values):
+    requests, packed_len, width = block.shape
+    cites = table.shape[1]
+    length = keys.shape[1]
     suffix_len, heads = packed_len - cites, width // HD
     rows = suffix_len * heads
-    count = len(blocks)
-    out = jax.ShapeDtypeStruct((requests, suffix_len, width + LANES), jnp.bfloat16)
     return in_vmem(
-        functools.partial(attend_kernel, count=count, suffix_len=suffix_len, heads=heads, cites=cites),
-        (out,) * count,
-        (*tables, *blocks, *(pltpu.with_memory_space_constraint(v, pltpu.HBM) for v in caches)),
+        attend_kernel,
+        jax.ShapeDtypeStruct((requests, suffix_len, width + LANES), jnp.bfloat16),
+        (table, block, keys, values),
         scratch=(
             pltpu.VMEM((cites, length), jnp.float32),
             pltpu.VMEM((rows, HD), jnp.bfloat16),
             pltpu.VMEM((rows, LANES), jnp.float32),
             pltpu.VMEM((rows, 2 * HD), jnp.float32),
-            pltpu.VMEM((2, length, HD), jnp.bfloat16),
-            pltpu.VMEM((2, length, HD), jnp.bfloat16),
-            pltpu.SMEM((count * requests * cites + 1,), jnp.int32),
-            pltpu.SemaphoreType.DMA((2, 2)),
-        ),
-        spaces=(pltpu.SMEM,) * count + (pltpu.VMEM,) * count + (pltpu.HBM,) * len(caches),
+        ),
+        smem=1,
         cost=pl.CostEstimate(
-            flops=count * requests * cites * rows * HD * length,
-            transcendentals=0,
-            bytes_accessed=count * 16 * 1024 * 1024,
+            flops=requests * cites * rows * HD * length, transcendentals=0, bytes_accessed=16 * 1024 * 1024
         ),
         name="attend_class",
     )
@@ -403,13 +362,20 @@
         here = (local >= 0) & (local < 2 * local_passages)
         return jnp.where(here, (local + core * local_passages) % (2 * local_passages), -1)
 
-    def attend(blocks):
-        return attend_call([places(b) for b in blocks], blocks, (passage_keys, passage_values, other_keys, other_values))
-
-    results = [attend(classes[0:1])[0]]
+    caches = (passage_keys, passage_values, other_keys, other_values)
+    both = jax.ShapeDtypeStruct((2 * local_passages, *passage_keys.shape[1:]), passage_keys.dtype)
+    keys, values = in_vmem(
+        stage_kernel,
+        (both, both),
+        tuple(pltpu.with_memory_space_constraint(v, pltpu.HBM) for v in caches),
+        scratch=(pltpu.SemaphoreType.DMA((4,)),),
+        spaces=(pltpu.HBM,) * 4,
+        name="stage",
+    )
+    results = [attend_call(places(row), row, keys, values)]
     for block in classes[1:]:
         block, results[-1] = lax.optimization_barrier((block, results[-1]))
-        results.append(attend([block])[0])
+        results.append(attend_call(places(block), block, keys, values))
     back = [shift(r, False, RING - hop) for r, hop in zip(results[1:], HOPS[1:])]
     partial = merge_call(
         (results[0], *back[:2]),

time: 87.6 us -> 83 us (0.947)
  the two profiles are of different devices: /device:TPU:16 before, /device:TPU:24 now
where the time goes in v4:
time: 83 us; the launch traced here: 83.5 us
  starting transfers between devices  29.6 us (36%)
  waiting for transfers between devices  18.8 us (23%)
  Pallas kernels  16.9 us (20%)
  blocking collectives  11.5 us (14%)
  local copies, waits for them, and re-layouts  5.9 us (7%)
    ppermute x12, starting transfers between devices, shift(): return lax.ppermute(value, ('x', 'y', 'c'), pairs)  29 us
    ppermute x12, waiting for transfers between devices, shift(): return lax.ppermute(value, ('x', 'y', 'c'), pairs)  18.8 us
    pallas_call x11, Pallas kernels, in_vmem(): pl.pallas_call(kernel, out_shape=out_shape, in_specs=[pl.BlockSpec(memory...  16.9 us
    all_to_all x1, blocking collectives, body(): lax.all_to_all(pieces, 'kv', split_axis=0, concat_axis=0, tiled=True)  11.5 us
    unnamed x13, local copies, waits for them, and re-layouts  5.85 us
  transfers between devices with their start and end apart: 14, of which 5 were waited for; matrix products, arithmetic and copies ran while one was open for 1% of the time, Pallas kernels for 18%

profile of v4, /device:TPU:24, one launch (start us, length us, event | category | flops | bytes accessed | tf_op | source)
XLA Modules:
  0.0 83.5 jit_solution(12924563566752804474)
XLA Ops:
  0.0 1.0 %pack.1.refs_0_ = bf16[72,1024]{1,0:T(8,128)(2,1)S(1)} custom-call(s32[1,8]{1,0:T(1,128)} %cite_ref.1, bf16[64,1024]{1,0:T(8,128)(2,1)} %bitcast.12, s32[8,128]{1,0:T(8,128)} %bitcast.22), custom_call_target="tpu_custom_call" | custom-call | tf_op jit(solution)/shard_map/pack/pallas_call | solution.py:248
  1.6 1.5 %collective-permute-start = (bf16[72,1024]{1,0:T(8,128)(2,1)S(1)}, bf16[72,1024]{1,0:T(8,128)(2,1)S(1)}, u32[]{:S(2)}, u32[]{:S(2)}) collective-permute-start(bf16[72,1024]{1,0:T(8,128)(2,1)S(1)} %pack.1.refs_0_), channel_id=1, source_target_pairs={{0,64},{8,24},{16,80},{24,40},{32,96},{40,56},{48,112},{56,8},{64,... | collective-permute-start | bytes 442376 | tf_op jit(solution)/shard_map/ppermute | solution.py:271
  3.1 1.7 %collective-permute-start.1 = (bf16[72,1024]{1,0:T(8,128)(2,1)S(1)}, bf16[72,1024]{1,0:T(8,128)(2,1)S(1)}, u32[]{:S(2)}, u32[]{:S(2)}) collective-permute-start(bf16[72,1024]{1,0:T(8,128)(2,1)S(1)} %pack.1.refs_0_), channel_id=1, source_target_pairs={{0,192},{8,56},{16,208},{24,8},{32,224},{40,24},{48,240},{56,40},{... | collective-permute-start | bytes 442376 | tf_op jit(solution)/shard_map/ppermute | solution.py:271
  4.8 1.8 %collective-permute-start.2 = (bf16[72,1024]{1,0:T(8,128)(2,1)S(1)}, bf16[72,1024]{1,0:T(8,128)(2,1)S(1)}, u32[]{:S(2)}, u32[]{:S(2)}) collective-permute-start(bf16[72,1024]{1,0:T(8,128)(2,1)S(1)} %pack.1.refs_0_), channel_id=1, source_target_pairs={{0,128},{8,40},{16,144},{24,56},{32,160},{40,8},{48,176},{56,24},{... | collective-permute-start | bytes 442376 | tf_op jit(solution)/shard_map/ppermute | solution.py:271
  10.9 1.4 %host_part.1 = (f32[64,1024]{1,0:T(8,128)S(1)}, f32[64,128]{1,0:T(8,128)S(1)}) custom-call(bf16[64,1024]{1,0:T(8,128)(2,1)S(1)} %bitcast.13, bf16[1024,128]{1,0:T(8,128)(2,1)S(1)} %bitcast.15, bf16[1024,128]{1,0:T(8,128)(2,1)S(1)} %bitcast.16, bf16[64,128]{1,0:T(8,128)(2,1)S(1)} %bitcast.19, bf16[64,128]{1,0:T(8,128)(2,1)S(1)} %bitcast.20), custom_call_target="tpu_custom_call" | custom-call | tf_op jit(solution)/shard_map/host_part/pallas_call | solution.py:248
  12.4 1.1 %collective-permute-start.5 = (bf16[4,72,1024]{2,1,0:T(8,128)(2,1)S(1)}, bf16[4,72,1024]{2,1,0:T(8,128)(2,1)S(1)}, u32[]{:S(2)}, u32[]{:S(2)}) collective-permute-start(bf16[4,72,1024]{2,1,0:T(8,128)(2,1)S(1)} %row.1.packed_ref), channel_id=1, source_target_pairs={{0,16},{8,72},{16,32},{24,88},{32,48},{40,104},{48,0},{56,120},{64... | collective-permute-start | bytes 1769480 | tf_op jit(solution)/shard_map/ppermute | solution.py:271
  13.6 1.0 %collective-permute-start.4 = (bf16[4,72,1024]{2,1,0:T(8,128)(2,1)S(1)}, bf16[4,72,1024]{2,1,0:T(8,128)(2,1)S(1)}, u32[]{:S(2)}, u32[]{:S(2)}) collective-permute-start(bf16[4,72,1024]{2,1,0:T(8,128)(2,1)S(1)} %row.1.packed_ref), channel_id=1, source_target_pairs={{0,48},{8,200},{16,0},{24,216},{32,16},{40,232},{48,32},{56,248},{... | collective-permute-start | bytes 1769480 | tf_op jit(solution)/shard_map/ppermute | solution.py:271
  14.5 1.2 %collective-permute-start.3 = (bf16[4,72,1024]{2,1,0:T(8,128)(2,1)S(1)}, bf16[4,72,1024]{2,1,0:T(8,128)(2,1)S(1)}, u32[]{:S(2)}, u32[]{:S(2)}) collective-permute-start(bf16[4,72,1024]{2,1,0:T(8,128)(2,1)S(1)} %row.1.packed_ref), channel_id=1, source_target_pairs={{0,32},{8,136},{16,48},{24,152},{32,0},{40,168},{48,16},{56,184},{... | collective-permute-start | bytes 1769480 | tf_op jit(solution)/shard_map/ppermute | solution.py:271
  16.9 2.2 %stage.1 = (bf16[8,1024,128]{2,1,0:T(8,128)(2,1)S(1)}, bf16[8,1024,128]{2,1,0:T(8,128)(2,1)S(1)}) custom-call(bf16[4,1024,128]{2,1,0:T(8,128)(2,1)} %own_key, bf16[4,1024,128]{2,1,0:T(8,128)(2,1)} %own_value, bf16[4,1024,128]{2,1,0:T(8,128)(2,1)} %copy-done.5, bf16[4,1024,128]{2,1,0:T(8,128)(2,1)} %collective-permute-done.7.other_value), custom_call_target="tpu_custom_call" | custom-call | tf_op jit(solution)/shard_map/stage/pallas_call | solution.py:248
  19.1 4.2 %attend_class.4.refs_0_ = bf16[4,64,1152]{2,1,0:T(8,128)(2,1)S(1)} custom-call(s32[4,8]{1,0:T(4,128)S(1)} %fusion.1.table_ref, bf16[4,72,1024]{2,1,0:T(8,128)(2,1)S(1)} %row.1.packed_ref, bf16[8,1024,128]{2,1,0:T(8,128)(2,1)S(1)} %get-tuple-element.29.key_ref, bf16[8,1024,128]{2,1,0:T(8,128)(2,1)S(1)} %get-tuple-element.30.value_ref), custom_call_target="tpu_custom_call" | custom-call | flops 2147483648 | bytes 16777216 | tf_op jit(solution)/shard_map/attend_class/pallas_call | solution.py:248
  23.6 3.1 %attend_class.5 = bf16[4,64,1152]{2,1,0:T(8,128)(2,1)S(1)} custom-call(s32[4,8]{1,0:T(4,128)S(1)} %fusion.3.table_ref, bf16[4,72,1024]{2,1,0:T(8,128)(2,1)S(1)} %collective-permute-done.5.packed_ref, bf16[8,1024,128]{2,1,0:T(8,128)(2,1)S(1)} %get-tuple-element.29.key_ref, bf16[8,1024,128]{2,1,0:T(8,128)(2,1)S(1)} %get-tuple-element.30.value_ref), custom_call_target="tpu_custom_call" | custom-call | flops 2147483648 | bytes 16777216 | tf_op jit(solution)/shard_map/attend_class/pallas_call | solution.py:248
  26.6 4.3 %collective-permute-done.4.packed_ref = bf16[4,72,1024]{2,1,0:T(8,128)(2,1)S(1)} collective-permute-done((bf16[4,72,1024]{2,1,0:T(8,128)(2,1)S(1)}, bf16[4,72,1024]{2,1,0:T(8,128)(2,1)S(1)}, u32[]{:S(2)}, u32[]{:S(2)}) %collective-permute-start.4) | collective-permute-done | bytes 589856 | tf_op jit(solution)/shard_map/ppermute | solution.py:271
  31.1 1.9 %attend_class.6 = bf16[4,64,1152]{2,1,0:T(8,128)(2,1)S(1)} custom-call(s32[4,8]{1,0:T(4,128)S(1)} %fusion.5.table_ref, bf16[4,72,1024]{2,1,0:T(8,128)(2,1)S(1)} %collective-permute-done.4.packed_ref, bf16[8,1024,128]{2,1,0:T(8,128)(2,1)S(1)} %get-tuple-element.29.key_ref, bf16[8,1024,128]{2,1,0:T(8,128)(2,1)S(1)} %get-tuple-element.30.value_ref), custom_call_target="tpu_custom_call" | custom-call | flops 2147483648 | bytes 16777216 | tf_op jit(solution)/shard_map/attend_class/pallas_call | solution.py:248
  33.1 3.2 %collective-permute-start.10 = (bf16[4,64,1152]{2,1,0:T(8,128)(2,1)S(1)}, bf16[4,64,1152]{2,1,0:T(8,128)(2,1)S(1)}, u32[]{:S(2)}, u32[]{:S(2)}) collective-permute-start(bf16[4,64,1152]{2,1,0:T(8,128)(2,1)S(1)} %attend_class.6), channel_id=1, source_target_pairs={{0,16},{8,72},{16,32},{24,88},{32,48},{40,104},{48,0},{56,120},{64... | collective-permute-start | bytes 1769480 | tf_op jit(solution)/shard_map/ppermute | solution.py:271
  36.2 1.2 %collective-permute-start.9 = (bf16[4,64,1152]{2,1,0:T(8,128)(2,1)S(1)}, bf16[4,64,1152]{2,1,0:T(8,128)(2,1)S(1)}, u32[]{:S(2)}, u32[]{:S(2)}) collective-permute-start(bf16[4,64,1152]{2,1,0:T(8,128)(2,1)S(1)} %attend_class.5), channel_id=1, source_target_pairs={{0,48},{8,200},{16,0},{24,216},{32,16},{40,232},{48,32},{56,248},{... | collective-permute-start | bytes 1769480 | tf_op jit(solution)/shard_map/ppermute | solution.py:271
  38.4 5.4 %collective-permute-start.8 = (bf16[4,64,1152]{2,1,0:T(8,128)(2,1)S(1)}, bf16[4,64,1152]{2,1,0:T(8,128)(2,1)S(1)}, u32[]{:S(2)}, u32[]{:S(2)}) collective-permute-start(bf16[4,64,1152]{2,1,0:T(8,128)(2,1)S(1)} %attend_class.7), channel_id=1, source_target_pairs={{0,32},{8,136},{16,48},{24,152},{32,0},{40,168},{48,16},{56,184},{... | collective-permute-start | bytes 1769480 | tf_op jit(solution)/shard_map/ppermute | solution.py:271
  43.8 1.3 %collective-permute-done.10.refs_2_ = bf16[4,64,1152]{2,1,0:T(8,128)(2,1)S(1)} collective-permute-done((bf16[4,64,1152]{2,1,0:T(8,128)(2,1)S(1)}, bf16[4,64,1152]{2,1,0:T(8,128)(2,1)S(1)}, u32[]{:S(2)}, u32[]{:S(2)}) %collective-permute-start.10) | collective-permute-done | bytes 589856 | tf_op jit(solution)/shard_map/ppermute | solution.py:271
  45.1 8.4 %collective-permute-done.9.refs_1_ = bf16[4,64,1152]{2,1,0:T(8,128)(2,1)S(1)} collective-permute-done((bf16[4,64,1152]{2,1,0:T(8,128)(2,1)S(1)}, bf16[4,64,1152]{2,1,0:T(8,128)(2,1)S(1)}, u32[]{:S(2)}, u32[]{:S(2)}) %collective-permute-start.9) | collective-permute-done | bytes 589856 | tf_op jit(solution)/shard_map/ppermute | solution.py:271
  53.5 1.0 %merge_near.1 = (f32[4,64,1024]{2,1,0:T(8,128)S(1)}, f32[4,64,128]{2,1,0:T(8,128)S(1)}) custom-call(bf16[4,64,1152]{2,1,0:T(8,128)(2,1)S(1)} %attend_class.4.refs_0_, bf16[4,64,1152]{2,1,0:T(8,128)(2,1)S(1)} %collective-permute-done.9.refs_1_, bf16[4,64,1152]{2,1,0:T(8,128)(2,1)S(1)} %collective-permute-done.10.refs_2_), custom_call_target="tpu_custom_call" | custom-call | tf_op jit(solution)/shard_map/merge_near/pallas_call | solution.py:248
  55.7 1.8 %collective-permute-start.12 = (bf16[1,64,1152]{2,1,0:T(8,128)(2,1)S(1)}, bf16[1,64,1152]{2,1,0:T(8,128)(2,1)S(1)}, u32[]{:S(2)}, u32[]{:S(2)}) collective-permute-start(bf16[1,64,1152]{2,1,0:T(8,128)(2,1)S(1)} %get-tuple-element.42), channel_id=1, source_target_pairs={{0,64},{8,24},{16,80},{24,40},{32,96},{40,56},{48,112},{56,8},{64,... | collective-permute-start | bytes 442376 | tf_op jit(solution)/shard_map/ppermute | solution.py:271
  57.5 8.7 %collective-permute-start.13 = (bf16[1,64,1152]{2,1,0:T(8,128)(2,1)S(1)}, bf16[1,64,1152]{2,1,0:T(8,128)(2,1)S(1)}, u32[]{:S(2)}, u32[]{:S(2)}) collective-permute-start(bf16[1,64,1152]{2,1,0:T(8,128)(2,1)S(1)} %get-tuple-element.41), channel_id=1, source_target_pairs={{0,128},{8,40},{16,144},{24,56},{32,160},{40,8},{48,176},{56,24},{... | collective-permute-start | bytes 442376 | tf_op jit(solution)/shard_map/ppermute | solution.py:271
  66.2 1.7 %collective-permute-done.12.refs_2_ = bf16[1,64,1152]{2,1,0:T(8,128)(2,1)S(1)} collective-permute-done((bf16[1,64,1152]{2,1,0:T(8,128)(2,1)S(1)}, bf16[1,64,1152]{2,1,0:T(8,128)(2,1)S(1)}, u32[]{:S(2)}, u32[]{:S(2)}) %collective-permute-start.12) | collective-permute-done | bytes 147488 | tf_op jit(solution)/shard_map/ppermute | solution.py:271
  67.9 3.0 %collective-permute-done.13.refs_3_ = bf16[1,64,1152]{2,1,0:T(8,128)(2,1)S(1)} collective-permute-done((bf16[1,64,1152]{2,1,0:T(8,128)(2,1)S(1)}, bf16[1,64,1152]{2,1,0:T(8,128)(2,1)S(1)}, u32[]{:S(2)}, u32[]{:S(2)}) %collective-permute-start.13) | collective-permute-done | bytes 147488 | tf_op jit(solution)/shard_map/ppermute | solution.py:271
  71.4 11.5 %all_to_all.5 = bf16[8,8,1024]{2,1,0:T(8,128)(2,1)S(1)} all-to-all(bf16[8,8,1024]{2,1,0:T(8,128)(2,1)S(1)} %bitcast.14), channel_id=1, replica_groups=mesh['x'=4,'y'=4,'c'=2,'kv'=8] {'kv'}, dimensions={0} | all-to-all | bytes 262144 | tf_op jit(solution)/shard_map/all_to_all | solution.py:402
  (38 shorter events, 9.6 us)
Async XLA Ops:
  1.0 14.9 %collective-permute-start.6 = (bf16[4,1024,128]{2,1,0:T(8,128)(2,1)}, bf16[4,1024,128]{2,1,0:T(8,128)(2,1)S(1)}, u32[]{:S(2)}, u32[]{:S(2)}) collective-permute-start(bf16[4,1024,128]{2,1,0:T(8,128)(2,1)} %own_key), channel_id=1, source_target_pairs={{0,8},{8,0},{1,9},{9,1},{2,10},{10,2},{3,11},{11,3},{4,12},{12,4},... | collective-permute-start | bytes 3145736 | tf_op jit(solution)/shard_map/ppermute | solution.py:330
  1.1 14.8 %collective-permute-start.7 = (bf16[4,1024,128]{2,1,0:T(8,128)(2,1)}, bf16[4,1024,128]{2,1,0:T(8,128)(2,1)}, u32[]{:S(2)}, u32[]{:S(2)}) collective-permute-start(bf16[4,1024,128]{2,1,0:T(8,128)(2,1)} %own_value), channel_id=1, source_target_pairs={{0,8},{8,0},{1,9},{9,1},{2,10},{10,2},{3,11},{11,3},{4,12},{12,4},... | collective-permute-start | bytes 3145736 | tf_op jit(solution)/shard_map/ppermute | solution.py:331
  1.6 10.7 %collective-permute-start = (bf16[72,1024]{1,0:T(8,128)(2,1)S(1)}, bf16[72,1024]{1,0:T(8,128)(2,1)S(1)}, u32[]{:S(2)}, u32[]{:S(2)}) collective-permute-start(bf16[72,1024]{1,0:T(8,128)(2,1)S(1)} %pack.1.refs_0_), channel_id=1, source_target_pairs={{0,64},{8,24},{16,80},{24,40},{32,96},{40,56},{48,112},{56,8},{64,... | collective-permute-start | bytes 442376 | tf_op jit(solution)/shard_map/ppermute | solution.py:271
  3.1 9.3 %collective-permute-start.1 = (bf16[72,1024]{1,0:T(8,128)(2,1)S(1)}, bf16[72,1024]{1,0:T(8,128)(2,1)S(1)}, u32[]{:S(2)}, u32[]{:S(2)}) collective-permute-start(bf16[72,1024]{1,0:T(8,128)(2,1)S(1)} %pack.1.refs_0_), channel_id=1, source_target_pairs={{0,192},{8,56},{16,208},{24,8},{32,224},{40,24},{48,240},{56,40},{... | collective-permute-start | bytes 442376 | tf_op jit(solution)/shard_map/ppermute | solution.py:271
  4.8 7.5 %collective-permute-start.2 = (bf16[72,1024]{1,0:T(8,128)(2,1)S(1)}, bf16[72,1024]{1,0:T(8,128)(2,1)S(1)}, u32[]{:S(2)}, u32[]{:S(2)}) collective-permute-start(bf16[72,1024]{1,0:T(8,128)(2,1)S(1)} %pack.1.refs_0_), channel_id=1, source_target_pairs={{0,128},{8,40},{16,144},{24,56},{32,160},{40,8},{48,176},{56,24},{... | collective-permute-start | bytes 442376 | tf_op jit(solution)/shard_map/ppermute | solution.py:271
  6.6 0.9 %copy-start = (bf16[1,64,1024]{2,1,0:T(8,128)(2,1)S(1)}, bf16[1,64,1024]{2,1,0:T(8,128)(2,1)}, u32[]{:S(2)}) copy-start(bf16[1,64,1024]{2,1,0:T(8,128)(2,1)} %param.9) | copy-start | bytes 393220
  7.5 0.9 %copy-start.1 = (bf16[1,8,128,128]{3,2,1,0:T(8,128)(2,1)S(1)}, bf16[1,8,128,128]{3,2,1,0:T(8,128)(2,1)}, u32[]{:S(2)}) copy-start(bf16[1,8,128,128]{3,2,1,0:T(8,128)(2,1)} %param.14) | copy-start | bytes 786436
  8.5 0.9 %copy-start.2 = (bf16[1,8,128,128]{3,2,1,0:T(8,128)(2,1)S(1)}, bf16[1,8,128,128]{3,2,1,0:T(8,128)(2,1)}, u32[]{:S(2)}) copy-start(bf16[1,8,128,128]{3,2,1,0:T(8,128)(2,1)} %param.15) | copy-start | bytes 786436
  9.4 0.7 copy-start.3
  10.2 0.7 copy-start.4
  12.4 11.0 %collective-permute-start.5 = (bf16[4,72,1024]{2,1,0:T(8,128)(2,1)S(1)}, bf16[4,72,1024]{2,1,0:T(8,128)(2,1)S(1)}, u32[]{:S(2)}, u32[]{:S(2)}) collective-permute-start(bf16[4,72,1024]{2,1,0:T(8,128)(2,1)S(1)} %row.1.packed_ref), channel_id=1, source_target_pairs={{0,16},{8,72},{16,32},{24,88},{32,48},{40,104},{48,0},{56,120},{64... | collective-permute-start | bytes 1769480 | tf_op jit(solution)/shard_map/ppermute | solution.py:271
  13.6 17.4 %collective-permute-start.4 = (bf16[4,72,1024]{2,1,0:T(8,128)(2,1)S(1)}, bf16[4,72,1024]{2,1,0:T(8,128)(2,1)S(1)}, u32[]{:S(2)}, u32[]{:S(2)}) collective-permute-start(bf16[4,72,1024]{2,1,0:T(8,128)(2,1)S(1)} %row.1.packed_ref), channel_id=1, source_target_pairs={{0,48},{8,200},{16,0},{24,216},{32,16},{40,232},{48,32},{56,248},{... | collective-permute-start | bytes 1769480 | tf_op jit(solution)/shard_map/ppermute | solution.py:271
  14.5 18.5 %collective-permute-start.3 = (bf16[4,72,1024]{2,1,0:T(8,128)(2,1)S(1)}, bf16[4,72,1024]{2,1,0:T(8,128)(2,1)S(1)}, u32[]{:S(2)}, u32[]{:S(2)}) collective-permute-start(bf16[4,72,1024]{2,1,0:T(8,128)(2,1)S(1)} %row.1.packed_ref), channel_id=1, source_target_pairs={{0,32},{8,136},{16,48},{24,152},{32,0},{40,168},{48,16},{56,184},{... | collective-permute-start | bytes 1769480 | tf_op jit(solution)/shard_map/ppermute | solution.py:271
  15.9 1.0 %copy-start.5 = (bf16[4,1024,128]{2,1,0:T(8,128)(2,1)}, bf16[4,1024,128]{2,1,0:T(8,128)(2,1)S(1)}, u32[]{:S(2)}) copy-start(bf16[4,1024,128]{2,1,0:T(8,128)(2,1)S(1)} %collective-permute-done.6.other_key) | copy-start | bytes 3145732
  33.1 12.0 %collective-permute-start.10 = (bf16[4,64,1152]{2,1,0:T(8,128)(2,1)S(1)}, bf16[4,64,1152]{2,1,0:T(8,128)(2,1)S(1)}, u32[]{:S(2)}, u32[]{:S(2)}) collective-permute-start(bf16[4,64,1152]{2,1,0:T(8,128)(2,1)S(1)} %attend_class.6), channel_id=1, source_target_pairs={{0,16},{8,72},{16,32},{24,88},{32,48},{40,104},{48,0},{56,120},{64... | collective-permute-start | bytes 1769480 | tf_op jit(solution)/shard_map/ppermute | solution.py:271
  36.2 17.3 %collective-permute-start.9 = (bf16[4,64,1152]{2,1,0:T(8,128)(2,1)S(1)}, bf16[4,64,1152]{2,1,0:T(8,128)(2,1)S(1)}, u32[]{:S(2)}, u32[]{:S(2)}) collective-permute-start(bf16[4,64,1152]{2,1,0:T(8,128)(2,1)S(1)} %attend_class.5), channel_id=1, source_target_pairs={{0,48},{8,200},{16,0},{24,216},{32,16},{40,232},{48,32},{56,248},{... | collective-permute-start | bytes 1769480 | tf_op jit(solution)/shard_map/ppermute | solution.py:271
  38.4 16.2 %collective-permute-start.8 = (bf16[4,64,1152]{2,1,0:T(8,128)(2,1)S(1)}, bf16[4,64,1152]{2,1,0:T(8,128)(2,1)S(1)}, u32[]{:S(2)}, u32[]{:S(2)}) collective-permute-start(bf16[4,64,1152]{2,1,0:T(8,128)(2,1)S(1)} %attend_class.7), channel_id=1, source_target_pairs={{0,32},{8,136},{16,48},{24,152},{32,0},{40,168},{48,16},{56,184},{... | collective-permute-start | bytes 1769480 | tf_op jit(solution)/shard_map/ppermute | solution.py:271
  55.4 10.8 %collective-permute-start.11 = (bf16[1,64,1152]{2,1,0:T(8,128)(2,1)S(1)}, bf16[1,64,1152]{2,1,0:T(8,128)(2,1)S(1)}, u32[]{:S(2)}, u32[]{:S(2)}) collective-permute-start(bf16[1,64,1152]{2,1,0:T(8,128)(2,1)S(1)} %get-tuple-element.43), channel_id=1, source_target_pairs={{0,192},{8,56},{16,208},{24,8},{32,224},{40,24},{48,240},{56,40},{... | collective-permute-start | bytes 442376 | tf_op jit(solution)/shard_map/ppermute | solution.py:271
  55.7 12.1 %collective-permute-start.12 = (bf16[1,64,1152]{2,1,0:T(8,128)(2,1)S(1)}, bf16[1,64,1152]{2,1,0:T(8,128)(2,1)S(1)}, u32[]{:S(2)}, u32[]{:S(2)}) collective-permute-start(bf16[1,64,1152]{2,1,0:T(8,128)(2,1)S(1)} %get-tuple-element.42), channel_id=1, source_target_pairs={{0,64},{8,24},{16,80},{24,40},{32,96},{40,56},{48,112},{56,8},{64,... | collective-permute-start | bytes 442376 | tf_op jit(solution)/shard_map/ppermute | solution.py:271
  57.5 13.4 %collective-permute-start.13 = (bf16[1,64,1152]{2,1,0:T(8,128)(2,1)S(1)}, bf16[1,64,1152]{2,1,0:T(8,128)(2,1)S(1)}, u32[]{:S(2)}, u32[]{:S(2)}) collective-permute-start(bf16[1,64,1152]{2,1,0:T(8,128)(2,1)S(1)} %get-tuple-element.41), channel_id=1, source_target_pairs={{0,128},{8,40},{16,144},{24,56},{32,160},{40,8},{48,176},{56,24},{... | collective-permute-start | bytes 442376 | tf_op jit(solution)/shard_map/ppermute | solution.py:271

commit v5 on v4

--- a/solution.py
+++ b/solution.py
@@ -164,7 +164,14 @@
     return total
 
 
-def host_kernel(query_ref, fresh_key_ref, fresh_value_ref, suffix_key_ref, suffix_value_ref, out_ref, level_ref):
+def host_kernel(*refs):
+    inputs, (out_ref, level_ref), held, sems = refs[0:5], refs[5:7], refs[7:12], refs[12]
+    copies = [pltpu.make_async_copy(source, target, sems.at[i]) for i, (source, target) in enumerate(zip(inputs, held))]
+    for copy in copies:
+        copy.start()
+    for copy in copies:
+        copy.wait()
+    query_ref, fresh_key_ref, fresh_value_ref, suffix_key_ref, suffix_value_ref = held
     suffix_len, width = query_ref.shape
     heads = width // HD
     query = stack_heads(query_ref[...], heads)
@@ -330,19 +337,22 @@
     other_keys = lax.ppermute(passage_keys, "c", swap)
     other_values = lax.ppermute(passage_values, "c", swap)
 
+    host_inputs = (
+        queries[0],
+        fresh_keys.reshape(-1, HD),
+        fresh_values.reshape(-1, HD),
+        suffix_keys[0],
+        suffix_values[0],
+    )
     host_out, host_level = in_vmem(
         host_kernel,
         (
             jax.ShapeDtypeStruct((suffix_len, width), jnp.float32),
             jax.ShapeDtypeStruct((suffix_len, LANES), jnp.float32),
         ),
-        (
-            queries[0],
-            fresh_keys.reshape(-1, HD),
-            fresh_values.reshape(-1, HD),
-            suffix_keys[0],
-            suffix_values[0],
-        ),
+        tuple(pltpu.with_memory_space_constraint(v, pltpu.HBM) for v in host_inputs),
+        scratch=tuple(pltpu.VMEM(v.shape, v.dtype) for v in host_inputs) + (pltpu.SemaphoreType.DMA((5,)),),
+        spaces=(pltpu.HBM,) * 5,
         name="host_part",
     )
 

time: 83 us -> 83.8 us (level)
  starting transfers between devices: 29.6 us -> 20.1 us
  waiting for transfers between devices: 18.8 us -> 25.5 us
  Pallas kernels: 16.9 us -> 21.6 us
  local copies, waits for them, and re-layouts: 5.9 us -> 1.65 us
  blocking collectives: 11.5 us -> 14.1 us
    ppermute x12, starting transfers between devices: 29 us -> 19.5 us  [shift(): return lax.ppermute(value, ('x', 'y', 'c'), pairs)]
    ppermute x12, waiting for transfers between devices: 18.8 us -> 25.5 us  [shift(): return lax.ppermute(value, ('x', 'y', 'c'), pairs)]
    pallas_call x11, Pallas kernels: 16.9 us -> 21.6 us  [in_vmem(): pl.pallas_call(kernel, out_shape=out_shape, in_specs=[pl.BlockSpec(memory...]
    unnamed x13 -> x3, local copies, waits for them, and re-layouts: 5.85 us -> 1.6 us
    all_to_all x1, blocking collectives: 11.5 us -> 14.1 us  [body(): lax.all_to_all(pieces, 'kv', split_axis=0, concat_axis=0, tiled=True)]
  transfers between devices with their start and end apart: 14 -> 14, of which waited for: 5 -> 6; matrix products, arithmetic and copies ran while one was open for 1% -> 1% of each run, Pallas kernels for 18% -> 23%
where the time goes in v5:
time: 83.8 us
  waiting for transfers between devices  25.5 us (30%)
  Pallas kernels  21.6 us (26%)
  starting transfers between devices  20.1 us (24%)
  blocking collectives  14.1 us (17%)
  local copies, waits for them, and re-layouts  1.65 us (2%)
    ppermute x12, waiting for transfers between devices, shift(): return lax.ppermute(value, ('x', 'y', 'c'), pairs)  25.5 us
    pallas_call x11, Pallas kernels, in_vmem(): pl.pallas_call(kernel, out_shape=out_shape, in_specs=[pl.BlockSpec(memory...  21.6 us
    ppermute x12, starting transfers between devices, shift(): return lax.ppermute(value, ('x', 'y', 'c'), pairs)  19.5 us
    all_to_all x1, blocking collectives, body(): lax.all_to_all(pieces, 'kv', split_axis=0, concat_axis=0, tiled=True)  14.1 us
  transfers between devices with their start and end apart: 14, of which 6 were waited for; matrix products, arithmetic and copies ran while one was open for 1% of the time, Pallas kernels for 23%

profile of v5, /device:TPU:24, one launch (start us, length us, event | category | flops | bytes accessed | tf_op | source)
XLA Modules:
  0.0 83.8 jit_solution(6646995733718082283)
XLA Ops:
  0.0 1.0 %pack.1.refs_0_ = bf16[72,1024]{1,0:T(8,128)(2,1)S(1)} custom-call(s32[1,8]{1,0:T(1,128)} %cite_ref.1, bf16[64,1024]{1,0:T(8,128)(2,1)} %bitcast.16, s32[8,128]{1,0:T(8,128)} %bitcast.22), custom_call_target="tpu_custom_call" | custom-call | tf_op jit(solution)/shard_map/pack/pallas_call | solution.py:255
  1.6 1.5 %collective-permute-start = (bf16[72,1024]{1,0:T(8,128)(2,1)S(1)}, bf16[72,1024]{1,0:T(8,128)(2,1)S(1)}, u32[]{:S(2)}, u32[]{:S(2)}) collective-permute-start(bf16[72,1024]{1,0:T(8,128)(2,1)S(1)} %pack.1.refs_0_), channel_id=1, source_target_pairs={{0,64},{8,24},{16,80},{24,40},{32,96},{40,56},{48,112},{56,8},{64,... | collective-permute-start | bytes 442376 | tf_op jit(solution)/shard_map/ppermute | solution.py:278
  3.1 1.7 %collective-permute-start.1 = (bf16[72,1024]{1,0:T(8,128)(2,1)S(1)}, bf16[72,1024]{1,0:T(8,128)(2,1)S(1)}, u32[]{:S(2)}, u32[]{:S(2)}) collective-permute-start(bf16[72,1024]{1,0:T(8,128)(2,1)S(1)} %pack.1.refs_0_), channel_id=1, source_target_pairs={{0,192},{8,56},{16,208},{24,8},{32,224},{40,24},{48,240},{56,40},{... | collective-permute-start | bytes 442376 | tf_op jit(solution)/shard_map/ppermute | solution.py:278
  4.8 1.8 %collective-permute-start.2 = (bf16[72,1024]{1,0:T(8,128)(2,1)S(1)}, bf16[72,1024]{1,0:T(8,128)(2,1)S(1)}, u32[]{:S(2)}, u32[]{:S(2)}) collective-permute-start(bf16[72,1024]{1,0:T(8,128)(2,1)S(1)} %pack.1.refs_0_), channel_id=1, source_target_pairs={{0,128},{8,40},{16,144},{24,56},{32,160},{40,8},{48,176},{56,24},{... | collective-permute-start | bytes 442376 | tf_op jit(solution)/shard_map/ppermute | solution.py:278
  6.6 2.6 %host_part.1 = (f32[64,1024]{1,0:T(8,128)S(1)}, f32[64,128]{1,0:T(8,128)S(1)}) custom-call(bf16[64,1024]{1,0:T(8,128)(2,1)} %bitcast.17, bf16[1024,128]{1,0:T(8,128)(2,1)} %bitcast.18, bf16[1024,128]{1,0:T(8,128)(2,1)} %bitcast.19, bf16[64,128]{1,0:T(8,128)(2,1)} %bitcast.20, bf16[64,128]{1,0:T(8,128)(2,1)} %bitcast.21), custom_call_target="tpu_custom_call" | custom-call | tf_op jit(solution)/shard_map/host_part/pallas_call | solution.py:255
  9.3 2.2 %collective-permute-done.2.refs_3_ = bf16[72,1024]{1,0:T(8,128)(2,1)S(1)} collective-permute-done((bf16[72,1024]{1,0:T(8,128)(2,1)S(1)}, bf16[72,1024]{1,0:T(8,128)(2,1)S(1)}, u32[]{:S(2)}, u32[]{:S(2)}) %collective-permute-start.2) | collective-permute-done | bytes 147488 | tf_op jit(solution)/shard_map/ppermute | solution.py:278
  11.5 2.0 %collective-permute-start.5 = (bf16[4,72,1024]{2,1,0:T(8,128)(2,1)S(1)}, bf16[4,72,1024]{2,1,0:T(8,128)(2,1)S(1)}, u32[]{:S(2)}, u32[]{:S(2)}) collective-permute-start(bf16[4,72,1024]{2,1,0:T(8,128)(2,1)S(1)} %row.1.packed_ref), channel_id=1, source_target_pairs={{0,16},{8,72},{16,32},{24,88},{32,48},{40,104},{48,0},{56,120},{64... | collective-permute-start | bytes 1769480 | tf_op jit(solution)/shard_map/ppermute | solution.py:278
  13.6 1.5 %collective-permute-start.3 = (bf16[4,72,1024]{2,1,0:T(8,128)(2,1)S(1)}, bf16[4,72,1024]{2,1,0:T(8,128)(2,1)S(1)}, u32[]{:S(2)}, u32[]{:S(2)}) collective-permute-start(bf16[4,72,1024]{2,1,0:T(8,128)(2,1)S(1)} %row.1.packed_ref), channel_id=1, source_target_pairs={{0,32},{8,136},{16,48},{24,152},{32,0},{40,168},{48,16},{56,184},{... | collective-permute-start | bytes 1769480 | tf_op jit(solution)/shard_map/ppermute | solution.py:278
  16.3 2.2 %stage.1 = (bf16[8,1024,128]{2,1,0:T(8,128)(2,1)S(1)}, bf16[8,1024,128]{2,1,0:T(8,128)(2,1)S(1)}) custom-call(bf16[4,1024,128]{2,1,0:T(8,128)(2,1)} %own_key, bf16[4,1024,128]{2,1,0:T(8,128)(2,1)} %own_value, bf16[4,1024,128]{2,1,0:T(8,128)(2,1)} %copy-done, bf16[4,1024,128]{2,1,0:T(8,128)(2,1)} %collective-permute-done.7.other_value), custom_call_target="tpu_custom_call" | custom-call | tf_op jit(solution)/shard_map/stage/pallas_call | solution.py:255
  18.5 4.2 %attend_class.4.refs_0_ = bf16[4,64,1152]{2,1,0:T(8,128)(2,1)S(1)} custom-call(s32[4,8]{1,0:T(4,128)S(1)} %fusion.1.table_ref, bf16[4,72,1024]{2,1,0:T(8,128)(2,1)S(1)} %row.1.packed_ref, bf16[8,1024,128]{2,1,0:T(8,128)(2,1)S(1)} %get-tuple-element.29.key_ref, bf16[8,1024,128]{2,1,0:T(8,128)(2,1)S(1)} %get-tuple-element.30.value_ref), custom_call_target="tpu_custom_call" | custom-call | flops 2147483648 | bytes 16777216 | tf_op jit(solution)/shard_map/attend_class/pallas_call | solution.py:255
  22.7 4.6 %collective-permute-done.5.packed_ref = bf16[4,72,1024]{2,1,0:T(8,128)(2,1)S(1)} collective-permute-done((bf16[4,72,1024]{2,1,0:T(8,128)(2,1)S(1)}, bf16[4,72,1024]{2,1,0:T(8,128)(2,1)S(1)}, u32[]{:S(2)}, u32[]{:S(2)}) %collective-permute-start.5) | collective-permute-done | bytes 589856 | tf_op jit(solution)/shard_map/ppermute | solution.py:278
  27.5 4.2 %attend_class.5 = bf16[4,64,1152]{2,1,0:T(8,128)(2,1)S(1)} custom-call(s32[4,8]{1,0:T(4,128)S(1)} %fusion.3.table_ref, bf16[4,72,1024]{2,1,0:T(8,128)(2,1)S(1)} %collective-permute-done.5.packed_ref, bf16[8,1024,128]{2,1,0:T(8,128)(2,1)S(1)} %get-tuple-element.29.key_ref, bf16[8,1024,128]{2,1,0:T(8,128)(2,1)S(1)} %get-tuple-element.30.value_ref), custom_call_target="tpu_custom_call" | custom-call | flops 2147483648 | bytes 16777216 | tf_op jit(solution)/shard_map/attend_class/pallas_call | solution.py:255
  31.9 1.9 %attend_class.6 = bf16[4,64,1152]{2,1,0:T(8,128)(2,1)S(1)} custom-call(s32[4,8]{1,0:T(4,128)S(1)} %fusion.5.table_ref, bf16[4,72,1024]{2,1,0:T(8,128)(2,1)S(1)} %collective-permute-done.4.packed_ref, bf16[8,1024,128]{2,1,0:T(8,128)(2,1)S(1)} %get-tuple-element.29.key_ref, bf16[8,1024,128]{2,1,0:T(8,128)(2,1)S(1)} %get-tuple-element.30.value_ref), custom_call_target="tpu_custom_call" | custom-call | flops 2147483648 | bytes 16777216 | tf_op jit(solution)/shard_map/attend_class/pallas_call | solution.py:255
  33.8 3.7 %collective-permute-start.10 = (bf16[4,64,1152]{2,1,0:T(8,128)(2,1)S(1)}, bf16[4,64,1152]{2,1,0:T(8,128)(2,1)S(1)}, u32[]{:S(2)}, u32[]{:S(2)}) collective-permute-start(bf16[4,64,1152]{2,1,0:T(8,128)(2,1)S(1)} %attend_class.6), channel_id=1, source_target_pairs={{0,16},{8,72},{16,32},{24,88},{32,48},{40,104},{48,0},{56,120},{64... | collective-permute-start | bytes 1769480 | tf_op jit(solution)/shard_map/ppermute | solution.py:278
  37.7 3.1 %attend_class.7 = bf16[4,64,1152]{2,1,0:T(8,128)(2,1)S(1)} custom-call(s32[4,8]{1,0:T(4,128)S(1)} %fusion.7.table_ref, bf16[4,72,1024]{2,1,0:T(8,128)(2,1)S(1)} %collective-permute-done.3.packed_ref, bf16[8,1024,128]{2,1,0:T(8,128)(2,1)S(1)} %get-tuple-element.29.key_ref, bf16[8,1024,128]{2,1,0:T(8,128)(2,1)S(1)} %get-tuple-element.30.value_ref), custom_call_target="tpu_custom_call" | custom-call | flops 2147483648 | bytes 16777216 | tf_op jit(solution)/shard_map/attend_class/pallas_call | solution.py:255
  40.8 1.8 %collective-permute-start.8 = (bf16[4,64,1152]{2,1,0:T(8,128)(2,1)S(1)}, bf16[4,64,1152]{2,1,0:T(8,128)(2,1)S(1)}, u32[]{:S(2)}, u32[]{:S(2)}) collective-permute-start(bf16[4,64,1152]{2,1,0:T(8,128)(2,1)S(1)} %attend_class.7), channel_id=1, source_target_pairs={{0,32},{8,136},{16,48},{24,152},{32,0},{40,168},{48,16},{56,184},{... | collective-permute-start | bytes 1769480 | tf_op jit(solution)/shard_map/ppermute | solution.py:278
  42.6 8.7 %collective-permute-done.10.refs_2_ = bf16[4,64,1152]{2,1,0:T(8,128)(2,1)S(1)} collective-permute-done((bf16[4,64,1152]{2,1,0:T(8,128)(2,1)S(1)}, bf16[4,64,1152]{2,1,0:T(8,128)(2,1)S(1)}, u32[]{:S(2)}, u32[]{:S(2)}) %collective-permute-start.10) | collective-permute-done | bytes 589856 | tf_op jit(solution)/shard_map/ppermute | solution.py:278
  51.3 3.7 %collective-permute-done.9.refs_1_ = bf16[4,64,1152]{2,1,0:T(8,128)(2,1)S(1)} collective-permute-done((bf16[4,64,1152]{2,1,0:T(8,128)(2,1)S(1)}, bf16[4,64,1152]{2,1,0:T(8,128)(2,1)S(1)}, u32[]{:S(2)}, u32[]{:S(2)}) %collective-permute-start.9) | collective-permute-done | bytes 589856 | tf_op jit(solution)/shard_map/ppermute | solution.py:278
  55.0 1.0 %merge_near.1 = (f32[4,64,1024]{2,1,0:T(8,128)S(1)}, f32[4,64,128]{2,1,0:T(8,128)S(1)}) custom-call(bf16[4,64,1152]{2,1,0:T(8,128)(2,1)S(1)} %attend_class.4.refs_0_, bf16[4,64,1152]{2,1,0:T(8,128)(2,1)S(1)} %collective-permute-done.9.refs_1_, bf16[4,64,1152]{2,1,0:T(8,128)(2,1)S(1)} %collective-permute-done.10.refs_2_), custom_call_target="tpu_custom_call" | custom-call | tf_op jit(solution)/shard_map/merge_near/pallas_call | solution.py:255
  56.9 3.7 %collective-permute-start.11 = (bf16[1,64,1152]{2,1,0:T(8,128)(2,1)S(1)}, bf16[1,64,1152]{2,1,0:T(8,128)(2,1)S(1)}, u32[]{:S(2)}, u32[]{:S(2)}) collective-permute-start(bf16[1,64,1152]{2,1,0:T(8,128)(2,1)S(1)} %get-tuple-element.43), channel_id=1, source_target_pairs={{0,192},{8,56},{16,208},{24,8},{32,224},{40,24},{48,240},{56,40},{... | collective-permute-start | bytes 442376 | tf_op jit(solution)/shard_map/ppermute | solution.py:278
  60.6 1.6 %collective-permute-start.13 = (bf16[1,64,1152]{2,1,0:T(8,128)(2,1)S(1)}, bf16[1,64,1152]{2,1,0:T(8,128)(2,1)S(1)}, u32[]{:S(2)}, u32[]{:S(2)}) collective-permute-start(bf16[1,64,1152]{2,1,0:T(8,128)(2,1)S(1)} %get-tuple-element.41), channel_id=1, source_target_pairs={{0,128},{8,40},{16,144},{24,56},{32,160},{40,8},{48,176},{56,24},{... | collective-permute-start | bytes 442376 | tf_op jit(solution)/shard_map/ppermute | solution.py:278
  62.2 1.1 %collective-permute-done.11.refs_1_ = bf16[1,64,1152]{2,1,0:T(8,128)(2,1)S(1)} collective-permute-done((bf16[1,64,1152]{2,1,0:T(8,128)(2,1)S(1)}, bf16[1,64,1152]{2,1,0:T(8,128)(2,1)S(1)}, u32[]{:S(2)}, u32[]{:S(2)}) %collective-permute-start.11) | collective-permute-done | bytes 147488 | tf_op jit(solution)/shard_map/ppermute | solution.py:278
  63.3 5.3 %collective-permute-done.12.refs_2_ = bf16[1,64,1152]{2,1,0:T(8,128)(2,1)S(1)} collective-permute-done((bf16[1,64,1152]{2,1,0:T(8,128)(2,1)S(1)}, bf16[1,64,1152]{2,1,0:T(8,128)(2,1)S(1)}, u32[]{:S(2)}, u32[]{:S(2)}) %collective-permute-start.12) | collective-permute-done | bytes 147488 | tf_op jit(solution)/shard_map/ppermute | solution.py:278
  69.0 14.1 %all_to_all.5 = bf16[8,8,1024]{2,1,0:T(8,128)(2,1)S(1)} all-to-all(bf16[8,8,1024]{2,1,0:T(8,128)(2,1)S(1)} %bitcast.12), channel_id=1, replica_groups=mesh['x'=4,'y'=4,'c'=2,'kv'=8] {'kv'}, dimensions={0} | all-to-all | bytes 262144 | tf_op jit(solution)/shard_map/all_to_all | solution.py:412
  (28 shorter events, 4.3 us)
Async XLA Ops:
  1.0 14.3 %collective-permute-start.6 = (bf16[4,1024,128]{2,1,0:T(8,128)(2,1)}, bf16[4,1024,128]{2,1,0:T(8,128)(2,1)S(1)}, u32[]{:S(2)}, u32[]{:S(2)}) collective-permute-start(bf16[4,1024,128]{2,1,0:T(8,128)(2,1)} %own_key), channel_id=1, source_target_pairs={{0,8},{8,0},{1,9},{9,1},{2,10},{10,2},{3,11},{11,3},{4,12},{12,4},... | collective-permute-start | bytes 3145736 | tf_op jit(solution)/shard_map/ppermute | solution.py:337
  1.1 14.2 %collective-permute-start.7 = (bf16[4,1024,128]{2,1,0:T(8,128)(2,1)}, bf16[4,1024,128]{2,1,0:T(8,128)(2,1)}, u32[]{:S(2)}, u32[]{:S(2)}) collective-permute-start(bf16[4,1024,128]{2,1,0:T(8,128)(2,1)} %own_value), channel_id=1, source_target_pairs={{0,8},{8,0},{1,9},{9,1},{2,10},{10,2},{3,11},{11,3},{4,12},{12,4},... | collective-permute-start | bytes 3145736 | tf_op jit(solution)/shard_map/ppermute | solution.py:338
  1.6 7.7 %collective-permute-start = (bf16[72,1024]{1,0:T(8,128)(2,1)S(1)}, bf16[72,1024]{1,0:T(8,128)(2,1)S(1)}, u32[]{:S(2)}, u32[]{:S(2)}) collective-permute-start(bf16[72,1024]{1,0:T(8,128)(2,1)S(1)} %pack.1.refs_0_), channel_id=1, source_target_pairs={{0,64},{8,24},{16,80},{24,40},{32,96},{40,56},{48,112},{56,8},{64,... | collective-permute-start | bytes 442376 | tf_op jit(solution)/shard_map/ppermute | solution.py:278
  3.1 6.2 %collective-permute-start.1 = (bf16[72,1024]{1,0:T(8,128)(2,1)S(1)}, bf16[72,1024]{1,0:T(8,128)(2,1)S(1)}, u32[]{:S(2)}, u32[]{:S(2)}) collective-permute-start(bf16[72,1024]{1,0:T(8,128)(2,1)S(1)} %pack.1.refs_0_), channel_id=1, source_target_pairs={{0,192},{8,56},{16,208},{24,8},{32,224},{40,24},{48,240},{56,40},{... | collective-permute-start | bytes 442376 | tf_op jit(solution)/shard_map/ppermute | solution.py:278
  4.8 6.6 %collective-permute-start.2 = (bf16[72,1024]{1,0:T(8,128)(2,1)S(1)}, bf16[72,1024]{1,0:T(8,128)(2,1)S(1)}, u32[]{:S(2)}, u32[]{:S(2)}) collective-permute-start(bf16[72,1024]{1,0:T(8,128)(2,1)S(1)} %pack.1.refs_0_), channel_id=1, source_target_pairs={{0,128},{8,40},{16,144},{24,56},{32,160},{40,8},{48,176},{56,24},{... | collective-permute-start | bytes 442376 | tf_op jit(solution)/shard_map/ppermute | solution.py:278
  11.5 15.8 %collective-permute-start.5 = (bf16[4,72,1024]{2,1,0:T(8,128)(2,1)S(1)}, bf16[4,72,1024]{2,1,0:T(8,128)(2,1)S(1)}, u32[]{:S(2)}, u32[]{:S(2)}) collective-permute-start(bf16[4,72,1024]{2,1,0:T(8,128)(2,1)S(1)} %row.1.packed_ref), channel_id=1, source_target_pairs={{0,16},{8,72},{16,32},{24,88},{32,48},{40,104},{48,0},{56,120},{64... | collective-permute-start | bytes 1769480 | tf_op jit(solution)/shard_map/ppermute | solution.py:278
  13.6 18.2 %collective-permute-start.4 = (bf16[4,72,1024]{2,1,0:T(8,128)(2,1)S(1)}, bf16[4,72,1024]{2,1,0:T(8,128)(2,1)S(1)}, u32[]{:S(2)}, u32[]{:S(2)}) collective-permute-start(bf16[4,72,1024]{2,1,0:T(8,128)(2,1)S(1)} %row.1.packed_ref), channel_id=1, source_target_pairs={{0,48},{8,200},{16,0},{24,216},{32,16},{40,232},{48,32},{56,248},{... | collective-permute-start | bytes 1769480 | tf_op jit(solution)/shard_map/ppermute | solution.py:278
  13.6 20.2 %collective-permute-start.3 = (bf16[4,72,1024]{2,1,0:T(8,128)(2,1)S(1)}, bf16[4,72,1024]{2,1,0:T(8,128)(2,1)S(1)}, u32[]{:S(2)}, u32[]{:S(2)}) collective-permute-start(bf16[4,72,1024]{2,1,0:T(8,128)(2,1)S(1)} %row.1.packed_ref), channel_id=1, source_target_pairs={{0,32},{8,136},{16,48},{24,152},{32,0},{40,168},{48,16},{56,184},{... | collective-permute-start | bytes 1769480 | tf_op jit(solution)/shard_map/ppermute | solution.py:278
  15.3 1.0 %copy-start = (bf16[4,1024,128]{2,1,0:T(8,128)(2,1)}, bf16[4,1024,128]{2,1,0:T(8,128)(2,1)S(1)}, u32[]{:S(2)}) copy-start(bf16[4,1024,128]{2,1,0:T(8,128)(2,1)S(1)} %collective-permute-done.6.other_key) | copy-start | bytes 3145732
  33.8 17.5 %collective-permute-start.10 = (bf16[4,64,1152]{2,1,0:T(8,128)(2,1)S(1)}, bf16[4,64,1152]{2,1,0:T(8,128)(2,1)S(1)}, u32[]{:S(2)}, u32[]{:S(2)}) collective-permute-start(bf16[4,64,1152]{2,1,0:T(8,128)(2,1)S(1)} %attend_class.6), channel_id=1, source_target_pairs={{0,16},{8,72},{16,32},{24,88},{32,48},{40,104},{48,0},{56,120},{64... | collective-permute-start | bytes 1769480 | tf_op jit(solution)/shard_map/ppermute | solution.py:278
  37.6 17.4 %collective-permute-start.9 = (bf16[4,64,1152]{2,1,0:T(8,128)(2,1)S(1)}, bf16[4,64,1152]{2,1,0:T(8,128)(2,1)S(1)}, u32[]{:S(2)}, u32[]{:S(2)}) collective-permute-start(bf16[4,64,1152]{2,1,0:T(8,128)(2,1)S(1)} %attend_class.5), channel_id=1, source_target_pairs={{0,48},{8,200},{16,0},{24,216},{32,16},{40,232},{48,32},{56,248},{... | collective-permute-start | bytes 1769480 | tf_op jit(solution)/shard_map/ppermute | solution.py:278
  40.8 15.2 %collective-permute-start.8 = (bf16[4,64,1152]{2,1,0:T(8,128)(2,1)S(1)}, bf16[4,64,1152]{2,1,0:T(8,128)(2,1)S(1)}, u32[]{:S(2)}, u32[]{:S(2)}) collective-permute-start(bf16[4,64,1152]{2,1,0:T(8,128)(2,1)S(1)} %attend_class.7), channel_id=1, source_target_pairs={{0,32},{8,136},{16,48},{24,152},{32,0},{40,168},{48,16},{56,184},{... | collective-permute-start | bytes 1769480 | tf_op jit(solution)/shard_map/ppermute | solution.py:278
  56.9 6.4 %collective-permute-start.11 = (bf16[1,64,1152]{2,1,0:T(8,128)(2,1)S(1)}, bf16[1,64,1152]{2,1,0:T(8,128)(2,1)S(1)}, u32[]{:S(2)}, u32[]{:S(2)}) collective-permute-start(bf16[1,64,1152]{2,1,0:T(8,128)(2,1)S(1)} %get-tuple-element.43), channel_id=1, source_target_pairs={{0,192},{8,56},{16,208},{24,8},{32,224},{40,24},{48,240},{56,40},{... | collective-permute-start | bytes 442376 | tf_op jit(solution)/shard_map/ppermute | solution.py:278
  60.6 7.9 %collective-permute-start.12 = (bf16[1,64,1152]{2,1,0:T(8,128)(2,1)S(1)}, bf16[1,64,1152]{2,1,0:T(8,128)(2,1)S(1)}, u32[]{:S(2)}, u32[]{:S(2)}) collective-permute-start(bf16[1,64,1152]{2,1,0:T(8,128)(2,1)S(1)} %get-tuple-element.42), channel_id=1, source_target_pairs={{0,64},{8,24},{16,80},{24,40},{32,96},{40,56},{48,112},{56,8},{64,... | collective-permute-start | bytes 442376 | tf_op jit(solution)/shard_map/ppermute | solution.py:278
  60.6 7.9 %collective-permute-start.13 = (bf16[1,64,1152]{2,1,0:T(8,128)(2,1)S(1)}, bf16[1,64,1152]{2,1,0:T(8,128)(2,1)S(1)}, u32[]{:S(2)}, u32[]{:S(2)}) collective-permute-start(bf16[1,64,1152]{2,1,0:T(8,128)(2,1)S(1)} %get-tuple-element.41), channel_id=1, source_target_pairs={{0,128},{8,40},{16,144},{24,56},{32,160},{40,8},{48,176},{56,24},{... | collective-permute-start | bytes 442376 | tf_op jit(solution)/shard_map/ppermute | solution.py:278

commit v6 on v5

--- a/solution.py
+++ b/solution.py
@@ -332,7 +332,6 @@
         spaces=(pltpu.HBM,) * 3,
         name="pack",
     )
-    packed, passage_keys, passage_values = lax.optimization_barrier((packed, passage_keys, passage_values))
     swap = [(0, 1), (1, 0)]
     other_keys = lax.ppermute(passage_keys, "c", swap)
     other_values = lax.ppermute(passage_values, "c", swap)
@@ -377,9 +376,9 @@
     keys, values = in_vmem(
         stage_kernel,
         (both, both),
-        tuple(pltpu.with_memory_space_constraint(v, pltpu.HBM) for v in caches),
+        tuple(v if v is other_keys else pltpu.with_memory_space_constraint(v, pltpu.HBM) for v in caches),
         scratch=(pltpu.SemaphoreType.DMA((4,)),),
-        spaces=(pltpu.HBM,) * 4,
+        spaces=(pltpu.HBM, pltpu.HBM, pl.ANY, pltpu.HBM),
         name="stage",
     )
     results = [attend_call(places(row), row, keys, values)]

time: 83.8 us -> 82.3 us (0.982)
  waiting for transfers between devices: 25.5 us -> 29.5 us
  Pallas kernels: 21.6 us -> 17.8 us
  blocking collectives: 14.1 us -> 15.8 us
  starting transfers between devices: 20.1 us -> 18.5 us
  local copies, waits for them, and re-layouts: 1.65 us -> 0.7 us
    ppermute x12, waiting for transfers between devices: 25.5 us -> 29.5 us  [shift(): return lax.ppermute(value, ('x', 'y', 'c'), pairs)]
    pallas_call x11, Pallas kernels: 21.6 us -> 17.8 us  [in_vmem(): pl.pallas_call(kernel, out_shape=out_shape, in_specs=[pl.BlockSpec(memory...]
    all_to_all x1, blocking collectives: 14.1 us -> 15.8 us  [body(): lax.all_to_all(pieces, 'kv', split_axis=0, concat_axis=0, tiled=True)]
    ppermute x12, starting transfers between devices: 19.5 us -> 18 us  [shift(): return lax.ppermute(value, ('x', 'y', 'c'), pairs)]
    unnamed x3 -> x1, local copies, waits for them, and re-layouts: 1.6 us -> 0.66 us
  transfers between devices with their start and end apart: 14 -> 14, of which waited for: 6 -> 7; matrix products, arithmetic and copies ran while one was open for 1% -> 1% of each run, Pallas kernels for 23% -> 20%
where the time goes in v6:
time: 82.3 us; the launch traced here: 83.1 us
  waiting for transfers between devices  29.5 us (36%)
  starting transfers between devices  18.5 us (22%)
  Pallas kernels  17.8 us (22%)
  blocking collectives  15.8 us (19%)
    ppermute x12, waiting for transfers between devices, shift(): return lax.ppermute(value, ('x', 'y', 'c'), pairs)  29.5 us
    ppermute x12, starting transfers between devices, shift(): return lax.ppermute(value, ('x', 'y', 'c'), pairs)  18 us
    pallas_call x11, Pallas kernels, in_vmem(): pl.pallas_call(kernel, out_shape=out_shape, in_specs=[pl.BlockSpec(memory...  17.8 us
    all_to_all x1, blocking collectives, body(): lax.all_to_all(pieces, 'kv', split_axis=0, concat_axis=0, tiled=True)  15.8 us
  transfers between devices with their start and end apart: 14, of which 7 were waited for; matrix products, arithmetic and copies ran while one was open for 1% of the time, Pallas kernels for 20%

profile of v6, /device:TPU:24, one launch (start us, length us, event | category | flops | bytes accessed | tf_op | source)
XLA Modules:
  0.0 83.1 jit_solution(13599720176814764994)
XLA Ops:
  0.5 1.0 %pack.1.refs_0_ = bf16[72,1024]{1,0:T(8,128)(2,1)S(1)} custom-call(s32[1,8]{1,0:T(1,128)} %cite_ref.1, bf16[64,1024]{1,0:T(8,128)(2,1)} %bitcast.16, s32[8,128]{1,0:T(8,128)} %bitcast.22), custom_call_target="tpu_custom_call" | custom-call | tf_op jit(solution)/shard_map/pack/pallas_call | solution.py:255
  1.5 1.6 %collective-permute-start = (bf16[72,1024]{1,0:T(8,128)(2,1)S(1)}, bf16[72,1024]{1,0:T(8,128)(2,1)S(1)}, u32[]{:S(2)}, u32[]{:S(2)}) collective-permute-start(bf16[72,1024]{1,0:T(8,128)(2,1)S(1)} %pack.1.refs_0_), channel_id=1, source_target_pairs={{0,64},{8,24},{16,80},{24,40},{32,96},{40,56},{48,112},{56,8},{64,... | collective-permute-start | bytes 442376 | tf_op jit(solution)/shard_map/ppermute | solution.py:278
  3.1 1.7 %collective-permute-start.1 = (bf16[72,1024]{1,0:T(8,128)(2,1)S(1)}, bf16[72,1024]{1,0:T(8,128)(2,1)S(1)}, u32[]{:S(2)}, u32[]{:S(2)}) collective-permute-start(bf16[72,1024]{1,0:T(8,128)(2,1)S(1)} %pack.1.refs_0_), channel_id=1, source_target_pairs={{0,192},{8,56},{16,208},{24,8},{32,224},{40,24},{48,240},{56,40},{... | collective-permute-start | bytes 442376 | tf_op jit(solution)/shard_map/ppermute | solution.py:278
  4.8 1.8 %collective-permute-start.2 = (bf16[72,1024]{1,0:T(8,128)(2,1)S(1)}, bf16[72,1024]{1,0:T(8,128)(2,1)S(1)}, u32[]{:S(2)}, u32[]{:S(2)}) collective-permute-start(bf16[72,1024]{1,0:T(8,128)(2,1)S(1)} %pack.1.refs_0_), channel_id=1, source_target_pairs={{0,128},{8,40},{16,144},{24,56},{32,160},{40,8},{48,176},{56,24},{... | collective-permute-start | bytes 442376 | tf_op jit(solution)/shard_map/ppermute | solution.py:278
  6.6 2.6 %host_part.1 = (f32[64,1024]{1,0:T(8,128)S(1)}, f32[64,128]{1,0:T(8,128)S(1)}) custom-call(bf16[64,1024]{1,0:T(8,128)(2,1)} %bitcast.17, bf16[1024,128]{1,0:T(8,128)(2,1)} %bitcast.18, bf16[1024,128]{1,0:T(8,128)(2,1)} %bitcast.19, bf16[64,128]{1,0:T(8,128)(2,1)} %bitcast.20, bf16[64,128]{1,0:T(8,128)(2,1)} %bitcast.21), custom_call_target="tpu_custom_call" | custom-call | tf_op jit(solution)/shard_map/host_part/pallas_call | solution.py:255
  9.2 2.2 %collective-permute-done.2.refs_3_ = bf16[72,1024]{1,0:T(8,128)(2,1)S(1)} collective-permute-done((bf16[72,1024]{1,0:T(8,128)(2,1)S(1)}, bf16[72,1024]{1,0:T(8,128)(2,1)S(1)}, u32[]{:S(2)}, u32[]{:S(2)}) %collective-permute-start.2) | collective-permute-done | bytes 147488 | tf_op jit(solution)/shard_map/ppermute | solution.py:278
  11.5 2.0 %collective-permute-start.5 = (bf16[4,72,1024]{2,1,0:T(8,128)(2,1)S(1)}, bf16[4,72,1024]{2,1,0:T(8,128)(2,1)S(1)}, u32[]{:S(2)}, u32[]{:S(2)}) collective-permute-start(bf16[4,72,1024]{2,1,0:T(8,128)(2,1)S(1)} %row.1.packed_ref), channel_id=1, source_target_pairs={{0,16},{8,72},{16,32},{24,88},{32,48},{40,104},{48,0},{56,120},{64... | collective-permute-start | bytes 1769480 | tf_op jit(solution)/shard_map/ppermute | solution.py:278
  13.6 1.5 %collective-permute-start.3 = (bf16[4,72,1024]{2,1,0:T(8,128)(2,1)S(1)}, bf16[4,72,1024]{2,1,0:T(8,128)(2,1)S(1)}, u32[]{:S(2)}, u32[]{:S(2)}) collective-permute-start(bf16[4,72,1024]{2,1,0:T(8,128)(2,1)S(1)} %row.1.packed_ref), channel_id=1, source_target_pairs={{0,32},{8,136},{16,48},{24,152},{32,0},{40,168},{48,16},{56,184},{... | collective-permute-start | bytes 1769480 | tf_op jit(solution)/shard_map/ppermute | solution.py:278
  15.3 1.9 %stage.1 = (bf16[8,1024,128]{2,1,0:T(8,128)(2,1)S(1)}, bf16[8,1024,128]{2,1,0:T(8,128)(2,1)S(1)}) custom-call(bf16[4,1024,128]{2,1,0:T(8,128)(2,1)} %own_key.1, bf16[4,1024,128]{2,1,0:T(8,128)(2,1)} %own_value.1, bf16[4,1024,128]{2,1,0:T(8,128)(2,1)S(1)} %collective-permute-done.6.other_key, bf16[4,1024,128]{2,1,0:T(8,128)(2,1)} %collective-permute-done.7.other_value), custom_call_target="tpu_custom_call" | custom-call | tf_op jit(solution)/shard_map/stage/pallas_call | solution.py:255
  17.2 3.1 %attend_class.4.refs_0_ = bf16[4,64,1152]{2,1,0:T(8,128)(2,1)S(1)} custom-call(s32[4,8]{1,0:T(4,128)S(1)} %fusion.1.table_ref, bf16[4,72,1024]{2,1,0:T(8,128)(2,1)S(1)} %row.1.packed_ref, bf16[8,1024,128]{2,1,0:T(8,128)(2,1)S(1)} %get-tuple-element.23.key_ref, bf16[8,1024,128]{2,1,0:T(8,128)(2,1)S(1)} %get-tuple-element.24.value_ref), custom_call_target="tpu_custom_call" | custom-call | flops 2147483648 | bytes 16777216 | tf_op jit(solution)/shard_map/attend_class/pallas_call | solution.py:255
  20.3 7.0 %collective-permute-done.5.packed_ref = bf16[4,72,1024]{2,1,0:T(8,128)(2,1)S(1)} collective-permute-done((bf16[4,72,1024]{2,1,0:T(8,128)(2,1)S(1)}, bf16[4,72,1024]{2,1,0:T(8,128)(2,1)S(1)}, u32[]{:S(2)}, u32[]{:S(2)}) %collective-permute-start.5) | collective-permute-done | bytes 589856 | tf_op jit(solution)/shard_map/ppermute | solution.py:278
  27.5 1.9 %attend_class.5 = bf16[4,64,1152]{2,1,0:T(8,128)(2,1)S(1)} custom-call(s32[4,8]{1,0:T(4,128)S(1)} %fusion.3.table_ref, bf16[4,72,1024]{2,1,0:T(8,128)(2,1)S(1)} %collective-permute-done.5.packed_ref, bf16[8,1024,128]{2,1,0:T(8,128)(2,1)S(1)} %get-tuple-element.23.key_ref, bf16[8,1024,128]{2,1,0:T(8,128)(2,1)S(1)} %get-tuple-element.24.value_ref), custom_call_target="tpu_custom_call" | custom-call | flops 2147483648 | bytes 16777216 | tf_op jit(solution)/shard_map/attend_class/pallas_call | solution.py:255
  29.4 1.6 %collective-permute-done.4.packed_ref = bf16[4,72,1024]{2,1,0:T(8,128)(2,1)S(1)} collective-permute-done((bf16[4,72,1024]{2,1,0:T(8,128)(2,1)S(1)}, bf16[4,72,1024]{2,1,0:T(8,128)(2,1)S(1)}, u32[]{:S(2)}, u32[]{:S(2)}) %collective-permute-start.4) | collective-permute-done | bytes 589856 | tf_op jit(solution)/shard_map/ppermute | solution.py:278
  31.1 1.9 %attend_class.6 = bf16[4,64,1152]{2,1,0:T(8,128)(2,1)S(1)} custom-call(s32[4,8]{1,0:T(4,128)S(1)} %fusion.5.table_ref, bf16[4,72,1024]{2,1,0:T(8,128)(2,1)S(1)} %collective-permute-done.4.packed_ref, bf16[8,1024,128]{2,1,0:T(8,128)(2,1)S(1)} %get-tuple-element.23.key_ref, bf16[8,1024,128]{2,1,0:T(8,128)(2,1)S(1)} %get-tuple-element.24.value_ref), custom_call_target="tpu_custom_call" | custom-call | flops 2147483648 | bytes 16777216 | tf_op jit(solution)/shard_map/attend_class/pallas_call | solution.py:255
  33.0 4.5 %collective-permute-start.10 = (bf16[4,64,1152]{2,1,0:T(8,128)(2,1)S(1)}, bf16[4,64,1152]{2,1,0:T(8,128)(2,1)S(1)}, u32[]{:S(2)}, u32[]{:S(2)}) collective-permute-start(bf16[4,64,1152]{2,1,0:T(8,128)(2,1)S(1)} %attend_class.6), channel_id=1, source_target_pairs={{0,16},{8,72},{16,32},{24,88},{32,48},{40,104},{48,0},{56,120},{64... | collective-permute-start | bytes 1769480 | tf_op jit(solution)/shard_map/ppermute | solution.py:278
  37.7 3.1 %attend_class.7 = bf16[4,64,1152]{2,1,0:T(8,128)(2,1)S(1)} custom-call(s32[4,8]{1,0:T(4,128)S(1)} %fusion.7.table_ref, bf16[4,72,1024]{2,1,0:T(8,128)(2,1)S(1)} %collective-permute-done.3.packed_ref, bf16[8,1024,128]{2,1,0:T(8,128)(2,1)S(1)} %get-tuple-element.23.key_ref, bf16[8,1024,128]{2,1,0:T(8,128)(2,1)S(1)} %get-tuple-element.24.value_ref), custom_call_target="tpu_custom_call" | custom-call | flops 2147483648 | bytes 16777216 | tf_op jit(solution)/shard_map/attend_class/pallas_call | solution.py:255
  40.8 1.8 %collective-permute-start.8 = (bf16[4,64,1152]{2,1,0:T(8,128)(2,1)S(1)}, bf16[4,64,1152]{2,1,0:T(8,128)(2,1)S(1)}, u32[]{:S(2)}, u32[]{:S(2)}) collective-permute-start(bf16[4,64,1152]{2,1,0:T(8,128)(2,1)S(1)} %attend_class.7), channel_id=1, source_target_pairs={{0,32},{8,136},{16,48},{24,152},{32,0},{40,168},{48,16},{56,184},{... | collective-permute-start | bytes 1769480 | tf_op jit(solution)/shard_map/ppermute | solution.py:278
  42.6 2.3 %collective-permute-done.10.refs_2_ = bf16[4,64,1152]{2,1,0:T(8,128)(2,1)S(1)} collective-permute-done((bf16[4,64,1152]{2,1,0:T(8,128)(2,1)S(1)}, bf16[4,64,1152]{2,1,0:T(8,128)(2,1)S(1)}, u32[]{:S(2)}, u32[]{:S(2)}) %collective-permute-start.10) | collective-permute-done | bytes 589856 | tf_op jit(solution)/shard_map/ppermute | solution.py:278
  45.0 10.0 %collective-permute-done.9.refs_1_ = bf16[4,64,1152]{2,1,0:T(8,128)(2,1)S(1)} collective-permute-done((bf16[4,64,1152]{2,1,0:T(8,128)(2,1)S(1)}, bf16[4,64,1152]{2,1,0:T(8,128)(2,1)S(1)}, u32[]{:S(2)}, u32[]{:S(2)}) %collective-permute-start.9) | collective-permute-done | bytes 589856 | tf_op jit(solution)/shard_map/ppermute | solution.py:278
  55.0 1.0 %merge_near.1 = (f32[4,64,1024]{2,1,0:T(8,128)S(1)}, f32[4,64,128]{2,1,0:T(8,128)S(1)}) custom-call(bf16[4,64,1152]{2,1,0:T(8,128)(2,1)S(1)} %attend_class.4.refs_0_, bf16[4,64,1152]{2,1,0:T(8,128)(2,1)S(1)} %collective-permute-done.9.refs_1_, bf16[4,64,1152]{2,1,0:T(8,128)(2,1)S(1)} %collective-permute-done.10.refs_2_), custom_call_target="tpu_custom_call" | custom-call | tf_op jit(solution)/shard_map/merge_near/pallas_call | solution.py:255
  56.9 1.4 %collective-permute-start.11 = (bf16[1,64,1152]{2,1,0:T(8,128)(2,1)S(1)}, bf16[1,64,1152]{2,1,0:T(8,128)(2,1)S(1)}, u32[]{:S(2)}, u32[]{:S(2)}) collective-permute-start(bf16[1,64,1152]{2,1,0:T(8,128)(2,1)S(1)} %get-tuple-element.37), channel_id=1, source_target_pairs={{0,192},{8,56},{16,208},{24,8},{32,224},{40,24},{48,240},{56,40},{... | collective-permute-start | bytes 442376 | tf_op jit(solution)/shard_map/ppermute | solution.py:278
  59.8 2.3 %collective-permute-done.11.refs_1_ = bf16[1,64,1152]{2,1,0:T(8,128)(2,1)S(1)} collective-permute-done((bf16[1,64,1152]{2,1,0:T(8,128)(2,1)S(1)}, bf16[1,64,1152]{2,1,0:T(8,128)(2,1)S(1)}, u32[]{:S(2)}, u32[]{:S(2)}) %collective-permute-start.11) | collective-permute-done | bytes 147488 | tf_op jit(solution)/shard_map/ppermute | solution.py:278
  62.1 4.1 %collective-permute-done.12.refs_2_ = bf16[1,64,1152]{2,1,0:T(8,128)(2,1)S(1)} collective-permute-done((bf16[1,64,1152]{2,1,0:T(8,128)(2,1)S(1)}, bf16[1,64,1152]{2,1,0:T(8,128)(2,1)S(1)}, u32[]{:S(2)}, u32[]{:S(2)}) %collective-permute-start.12) | collective-permute-done | bytes 147488 | tf_op jit(solution)/shard_map/ppermute | solution.py:278
  66.7 15.8 %all_to_all.5 = bf16[8,8,1024]{2,1,0:T(8,128)(2,1)S(1)} all-to-all(bf16[8,8,1024]{2,1,0:T(8,128)(2,1)S(1)} %bitcast.12), channel_id=1, replica_groups=mesh['x'=4,'y'=4,'c'=2,'kv'=8] {'kv'}, dimensions={0} | all-to-all | bytes 262144 | tf_op jit(solution)/shard_map/all_to_all | solution.py:411
  (26 shorter events, 4.8 us)
Async XLA Ops:
  0.0 15.3 %collective-permute-start.6 = (bf16[4,1024,128]{2,1,0:T(8,128)(2,1)}, bf16[4,1024,128]{2,1,0:T(8,128)(2,1)S(1)}, u32[]{:S(2)}, u32[]{:S(2)}) collective-permute-start(bf16[4,1024,128]{2,1,0:T(8,128)(2,1)} %own_key.1), channel_id=1, source_target_pairs={{0,8},{8,0},{1,9},{9,1},{2,10},{10,2},{3,11},{11,3},{4,12},{12,4},... | collective-permute-start | bytes 3145736 | tf_op jit(solution)/shard_map/ppermute | solution.py:336
  0.0 15.3 %collective-permute-start.7 = (bf16[4,1024,128]{2,1,0:T(8,128)(2,1)}, bf16[4,1024,128]{2,1,0:T(8,128)(2,1)}, u32[]{:S(2)}, u32[]{:S(2)}) collective-permute-start(bf16[4,1024,128]{2,1,0:T(8,128)(2,1)} %own_value.1), channel_id=1, source_target_pairs={{0,8},{8,0},{1,9},{9,1},{2,10},{10,2},{3,11},{11,3},{4,12},{12,4},... | collective-permute-start | bytes 3145736 | tf_op jit(solution)/shard_map/ppermute | solution.py:337
  1.5 7.7 %collective-permute-start = (bf16[72,1024]{1,0:T(8,128)(2,1)S(1)}, bf16[72,1024]{1,0:T(8,128)(2,1)S(1)}, u32[]{:S(2)}, u32[]{:S(2)}) collective-permute-start(bf16[72,1024]{1,0:T(8,128)(2,1)S(1)} %pack.1.refs_0_), channel_id=1, source_target_pairs={{0,64},{8,24},{16,80},{24,40},{32,96},{40,56},{48,112},{56,8},{64,... | collective-permute-start | bytes 442376 | tf_op jit(solution)/shard_map/ppermute | solution.py:278
  3.1 6.2 %collective-permute-start.1 = (bf16[72,1024]{1,0:T(8,128)(2,1)S(1)}, bf16[72,1024]{1,0:T(8,128)(2,1)S(1)}, u32[]{:S(2)}, u32[]{:S(2)}) collective-permute-start(bf16[72,1024]{1,0:T(8,128)(2,1)S(1)} %pack.1.refs_0_), channel_id=1, source_target_pairs={{0,192},{8,56},{16,208},{24,8},{32,224},{40,24},{48,240},{56,40},{... | collective-permute-start | bytes 442376 | tf_op jit(solution)/shard_map/ppermute | solution.py:278
  4.8 6.6 %collective-permute-start.2 = (bf16[72,1024]{1,0:T(8,128)(2,1)S(1)}, bf16[72,1024]{1,0:T(8,128)(2,1)S(1)}, u32[]{:S(2)}, u32[]{:S(2)}) collective-permute-start(bf16[72,1024]{1,0:T(8,128)(2,1)S(1)} %pack.1.refs_0_), channel_id=1, source_target_pairs={{0,128},{8,40},{16,144},{24,56},{32,160},{40,8},{48,176},{56,24},{... | collective-permute-start | bytes 442376 | tf_op jit(solution)/shard_map/ppermute | solution.py:278
  11.5 15.8 %collective-permute-start.5 = (bf16[4,72,1024]{2,1,0:T(8,128)(2,1)S(1)}, bf16[4,72,1024]{2,1,0:T(8,128)(2,1)S(1)}, u32[]{:S(2)}, u32[]{:S(2)}) collective-permute-start(bf16[4,72,1024]{2,1,0:T(8,128)(2,1)S(1)} %row.1.packed_ref), channel_id=1, source_target_pairs={{0,16},{8,72},{16,32},{24,88},{32,48},{40,104},{48,0},{56,120},{64... | collective-permute-start | bytes 1769480 | tf_op jit(solution)/shard_map/ppermute | solution.py:278
  13.5 17.4 %collective-permute-start.4 = (bf16[4,72,1024]{2,1,0:T(8,128)(2,1)S(1)}, bf16[4,72,1024]{2,1,0:T(8,128)(2,1)S(1)}, u32[]{:S(2)}, u32[]{:S(2)}) collective-permute-start(bf16[4,72,1024]{2,1,0:T(8,128)(2,1)S(1)} %row.1.packed_ref), channel_id=1, source_target_pairs={{0,48},{8,200},{16,0},{24,216},{32,16},{40,232},{48,32},{56,248},{... | collective-permute-start | bytes 1769480 | tf_op jit(solution)/shard_map/ppermute | solution.py:278
  13.6 19.4 %collective-permute-start.3 = (bf16[4,72,1024]{2,1,0:T(8,128)(2,1)S(1)}, bf16[4,72,1024]{2,1,0:T(8,128)(2,1)S(1)}, u32[]{:S(2)}, u32[]{:S(2)}) collective-permute-start(bf16[4,72,1024]{2,1,0:T(8,128)(2,1)S(1)} %row.1.packed_ref), channel_id=1, source_target_pairs={{0,32},{8,136},{16,48},{24,152},{32,0},{40,168},{48,16},{56,184},{... | collective-permute-start | bytes 1769480 | tf_op jit(solution)/shard_map/ppermute | solution.py:278
  33.0 11.9 %collective-permute-start.10 = (bf16[4,64,1152]{2,1,0:T(8,128)(2,1)S(1)}, bf16[4,64,1152]{2,1,0:T(8,128)(2,1)S(1)}, u32[]{:S(2)}, u32[]{:S(2)}) collective-permute-start(bf16[4,64,1152]{2,1,0:T(8,128)(2,1)S(1)} %attend_class.6), channel_id=1, source_target_pairs={{0,16},{8,72},{16,32},{24,88},{32,48},{40,104},{48,0},{56,120},{64... | collective-permute-start | bytes 1769480 | tf_op jit(solution)/shard_map/ppermute | solution.py:278
  37.6 17.4 %collective-permute-start.9 = (bf16[4,64,1152]{2,1,0:T(8,128)(2,1)S(1)}, bf16[4,64,1152]{2,1,0:T(8,128)(2,1)S(1)}, u32[]{:S(2)}, u32[]{:S(2)}) collective-permute-start(bf16[4,64,1152]{2,1,0:T(8,128)(2,1)S(1)} %attend_class.5), channel_id=1, source_target_pairs={{0,48},{8,200},{16,0},{24,216},{32,16},{40,232},{48,32},{56,248},{... | collective-permute-start | bytes 1769480 | tf_op jit(solution)/shard_map/ppermute | solution.py:278
  40.8 15.2 %collective-permute-start.8 = (bf16[4,64,1152]{2,1,0:T(8,128)(2,1)S(1)}, bf16[4,64,1152]{2,1,0:T(8,128)(2,1)S(1)}, u32[]{:S(2)}, u32[]{:S(2)}) collective-permute-start(bf16[4,64,1152]{2,1,0:T(8,128)(2,1)S(1)} %attend_class.7), channel_id=1, source_target_pairs={{0,32},{8,136},{16,48},{24,152},{32,0},{40,168},{48,16},{56,184},{... | collective-permute-start | bytes 1769480 | tf_op jit(solution)/shard_map/ppermute | solution.py:278
  56.9 5.2 %collective-permute-start.11 = (bf16[1,64,1152]{2,1,0:T(8,128)(2,1)S(1)}, bf16[1,64,1152]{2,1,0:T(8,128)(2,1)S(1)}, u32[]{:S(2)}, u32[]{:S(2)}) collective-permute-start(bf16[1,64,1152]{2,1,0:T(8,128)(2,1)S(1)} %get-tuple-element.37), channel_id=1, source_target_pairs={{0,192},{8,56},{16,208},{24,8},{32,224},{40,24},{48,240},{56,40},{... | collective-permute-start | bytes 442376 | tf_op jit(solution)/shard_map/ppermute | solution.py:278
  58.3 7.9 %collective-permute-start.12 = (bf16[1,64,1152]{2,1,0:T(8,128)(2,1)S(1)}, bf16[1,64,1152]{2,1,0:T(8,128)(2,1)S(1)}, u32[]{:S(2)}, u32[]{:S(2)}) collective-permute-start(bf16[1,64,1152]{2,1,0:T(8,128)(2,1)S(1)} %get-tuple-element.36), channel_id=1, source_target_pairs={{0,64},{8,24},{16,80},{24,40},{32,96},{40,56},{48,112},{56,8},{64,... | collective-permute-start | bytes 442376 | tf_op jit(solution)/shard_map/ppermute | solution.py:278
  59.0 7.2 %collective-permute-start.13 = (bf16[1,64,1152]{2,1,0:T(8,128)(2,1)S(1)}, bf16[1,64,1152]{2,1,0:T(8,128)(2,1)S(1)}, u32[]{:S(2)}, u32[]{:S(2)}) collective-permute-start(bf16[1,64,1152]{2,1,0:T(8,128)(2,1)S(1)} %get-tuple-element.35), channel_id=1, source_target_pairs={{0,128},{8,40},{16,144},{24,56},{32,160},{40,8},{48,176},{56,24},{... | collective-permute-start | bytes 442376 | tf_op jit(solution)/shard_map/ppermute | solution.py:278
